TPU v7x, 32 devices: a whole 2x2x4 slice. The times are simulated.
32 devices in a mesh: dp: 4 (over z), fsdp: 8 (over y, x, core).
Axes of the slice: x: 2, y: 2, z: 4, core: 2. Of those that a mesh axis runs over, the one named last changes fastest.
Arguments:
- hidden_in: float32 [32768, 768], P(('dp', 'fsdp')), may hold values from -6 to 6
- time_embed: float32 [512, 768], P(('dp', 'fsdp')), may hold values from -6 to 6
- seg_ids: int32 [32768], P(('dp', 'fsdp')), may hold values from -1 to 15, as said below
- pre_gain: float32 [768], P(('dp', 'fsdp')), may hold values from 0.5 to 1.5
- pre_shift: float32 [768], P(('dp', 'fsdp')), may hold values from -3 to 3
- qkv_weight: float32 [768, 2304], P(('dp', 'fsdp')), may hold values from -0.21875 to 0.21875
- qv_bias: float32 [1536], P(('dp', 'fsdp')), may hold values from -3 to 3
- out_weight: float32 [768, 768], P(('dp', 'fsdp')), may hold values from -0.625 to 0.625
- out_bias: float32 [768], P(('dp', 'fsdp')), may hold values from -3 to 3
- mid_gain: float32 [768], P(('dp', 'fsdp')), may hold values from 0.5 to 1.5
- mid_shift: float32 [768], P(('dp', 'fsdp')), may hold values from -3 to 3
- in_weight: float32 [768, 3072], P(('dp', 'fsdp')), may hold values from -0.21875 to 0.21875
- in_bias: float32 [3072], P(('dp', 'fsdp')), may hold values from -3 to 3
- down_weight: float32 [3072, 768], P(('dp', 'fsdp')), may hold values from -0.109375 to 0.109375
- down_bias: float32 [768], P(('dp', 'fsdp')), may hold values from -3 to 3
- grad_out: float32 [32768, 768], P(('dp', 'fsdp')), may hold values from -6 to 6
Outputs:
- block_out: float32 [32768, 768], P(('dp', 'fsdp'))
- input_grad: float32 [32768, 768], P(('dp', 'fsdp'))
- time_grad: float32 [512, 768], P(('dp', 'fsdp'))
- grad_pre_gain: float32 [768], P(('dp', 'fsdp'))
- grad_pre_shift: float32 [768], P(('dp', 'fsdp'))
- grad_qkv_weight: float32 [768, 2304], P(('dp', 'fsdp'))
- grad_qv_bias: float32 [1536], P(('dp', 'fsdp'))
- grad_out_weight: float32 [768, 768], P(('dp', 'fsdp'))
- grad_out_bias: float32 [768], P(('dp', 'fsdp'))
- grad_mid_gain: float32 [768], P(('dp', 'fsdp'))
- grad_mid_shift: float32 [768], P(('dp', 'fsdp'))
- grad_in_weight: float32 [768, 3072], P(('dp', 'fsdp'))
- grad_in_bias: float32 [3072], P(('dp', 'fsdp'))
- grad_down_weight: float32 [3072, 768], P(('dp', 'fsdp'))
- grad_down_bias: float32 [768], P(('dp', 'fsdp'))
Inputs may be any that keep to these rules, and one draw needn't show every extreme that they name: Within each block of 1024 tokens, either every token has seg_ids 0 (one item of 1024 tokens), or items of 64 tokens numbered 0, 1, 2, ... follow one another from the block's start and the rest of the block is padding with -1. Some block of every draw is one whole item and some other block is filled with short items.
All inputs are finite; a program needn't handle non-finite values.
Results may differ from a plain program's by a relative error of at most 0.011.
Values may be sent and summed in bfloat16 or wider, within the bound.
A program may use at most 256 MiB of HBM per device.

v0:
```python
import jax
import jax.numpy as jnp
from jax import lax
from jax.sharding import PartitionSpec as P

D = 768
HEADS = 12
HEAD_DIM = 64


def layer_norm(v, gain_vec, shift_vec):
    center = v - jnp.mean(v, axis=-1, keepdims=True)
    spread = jnp.mean(center * center, axis=-1, keepdims=True)
    return center * lax.rsqrt(spread + 1e-05) * gain_vec + shift_vec


def gelu_exact(v):
    return jax.nn.gelu(v, approximate=False)


def masked_scores(q_part, k, seg_rows, seg_cols, score_scale):
    scores = jnp.einsum("qhd,khd->hqk", q_part, k, preferred_element_type=jnp.float32) * score_scale
    allowed = (seg_rows[:, None] == seg_cols[None, :]) & (seg_cols[None, :] >= 0)
    return jnp.where(allowed[None], scores, -1e30)


def left_product(a, b):
    return lax.dot_general(a, b, (((0,), (0,)), ((), ())), preferred_element_type=jnp.float32)


def right_product(a, b):
    return lax.dot_general(a, b, (((1,), (1,)), ((), ())), preferred_element_type=jnp.float32)


def local(
    hidden_in,
    time_embed,
    seg_ids,
    pre_gain,
    pre_shift,
    qkv_weight,
    qv_bias,
    out_weight,
    out_bias,
    mid_gain,
    mid_shift,
    in_weight,
    in_bias,
    down_weight,
    down_bias,
    grad_out,
):
    row_count = hidden_in.shape[0]
    items_here = time_embed.shape[0]
    live_mask = (seg_ids >= 0).astype(jnp.float32)[:, None]
    onehot = (seg_ids[:, None] == jnp.arange(items_here, dtype=jnp.int32)[None, :]).astype(
        jnp.float32
    )
    x = (hidden_in + jnp.dot(onehot, time_embed, precision=lax.Precision.HIGHEST)) * live_mask
    gathered = (
        lax.all_gather(pre_gain.astype(jnp.bfloat16), ("dp", "fsdp"), axis=0, tiled=True),
        lax.all_gather(pre_shift.astype(jnp.bfloat16), ("dp", "fsdp"), axis=0, tiled=True),
        lax.all_gather(qkv_weight.astype(jnp.bfloat16), ("dp", "fsdp"), axis=0, tiled=True),
        lax.all_gather(qv_bias.astype(jnp.bfloat16), ("dp", "fsdp"), axis=0, tiled=True),
        lax.all_gather(out_weight.astype(jnp.bfloat16), ("dp", "fsdp"), axis=0, tiled=True),
        lax.all_gather(out_bias.astype(jnp.bfloat16), ("dp", "fsdp"), axis=0, tiled=True),
        lax.all_gather(mid_gain.astype(jnp.bfloat16), ("dp", "fsdp"), axis=0, tiled=True),
        lax.all_gather(mid_shift.astype(jnp.bfloat16), ("dp", "fsdp"), axis=0, tiled=True),
        lax.all_gather(in_weight.astype(jnp.bfloat16), ("dp", "fsdp"), axis=0, tiled=True),
        lax.all_gather(in_bias.astype(jnp.bfloat16), ("dp", "fsdp"), axis=0, tiled=True),
        lax.all_gather(down_weight.astype(jnp.bfloat16), ("dp", "fsdp"), axis=0, tiled=True),
        lax.all_gather(down_bias.astype(jnp.bfloat16), ("dp", "fsdp"), axis=0, tiled=True),
    )
    (
        attn_gain,
        attn_shift,
        qkv_full,
        qvb_full,
        proj_full,
        projb_full,
        mlp_gain,
        mlp_shift,
        up_full,
        upb_full,
        down_full,
        downb_full,
    ) = gathered
    normed, attn_norm_back = jax.vjp(
        layer_norm, x, attn_gain.astype(jnp.float32), attn_shift.astype(jnp.float32)
    )
    normed_low = normed.astype(jnp.bfloat16)
    qv_float = qvb_full.astype(jnp.float32)
    bias_full = jnp.concatenate([qv_float[:D], jnp.zeros((D,), jnp.float32), qv_float[D:]])
    projected = jnp.dot(normed_low, qkv_full, preferred_element_type=jnp.float32) + bias_full
    projected_low = projected.astype(jnp.bfloat16)
    q = projected_low[:, :D].reshape(row_count, HEADS, HEAD_DIM)
    k = projected_low[:, D : 2 * D].reshape(row_count, HEADS, HEAD_DIM)
    v = projected_low[:, 2 * D :].reshape(row_count, HEADS, HEAD_DIM)
    block_rows = min(512, row_count)
    block_count = row_count // block_rows
    score_scale = HEAD_DIM ** (-0.5)
    q_blocks = q.reshape(block_count, block_rows, HEADS, HEAD_DIM)
    seg_blocks = seg_ids.reshape(block_count, block_rows)

    def forward_block(pieces):
        q_part, seg_part = pieces
        scores = masked_scores(q_part, k, seg_part, seg_ids, score_scale)
        row_max = jnp.max(scores, axis=-1, keepdims=True)
        exp_terms = jnp.exp(scores - row_max)
        row_total = jnp.sum(exp_terms, axis=-1, keepdims=True)
        p = (exp_terms / row_total).astype(jnp.bfloat16)
        attended = jnp.einsum("hqk,khd->qhd", p, v, preferred_element_type=jnp.float32)
        return (attended, (row_max + jnp.log(row_total))[..., 0])

    attended, log_sums = lax.map(forward_block, (q_blocks, seg_blocks))
    attended_low = attended.reshape(row_count, D).astype(jnp.bfloat16)
    residual = (
        x
        + jnp.dot(attended_low, proj_full, preferred_element_type=jnp.float32)
        + projb_full.astype(jnp.float32)
    )
    normed_mid, mlp_norm_back = jax.vjp(
        layer_norm, residual, mlp_gain.astype(jnp.float32), mlp_shift.astype(jnp.float32)
    )
    normed_mid_low = normed_mid.astype(jnp.bfloat16)
    before = jnp.dot(normed_mid_low, up_full, preferred_element_type=jnp.float32) + upb_full.astype(
        jnp.float32
    )
    active, gelu_back = jax.vjp(gelu_exact, before)
    active_low = active.astype(jnp.bfloat16)
    branch = jnp.dot(active_low, down_full, preferred_element_type=jnp.float32) + downb_full.astype(
        jnp.float32
    )
    block_out = (residual + branch) * live_mask
    qkv_back, proj_back, up_back, down_back = (
        lax.all_gather(qkv_weight.astype(jnp.bfloat16), ("dp", "fsdp"), axis=0, tiled=True),
        lax.all_gather(out_weight.astype(jnp.bfloat16), ("dp", "fsdp"), axis=0, tiled=True),
        lax.all_gather(in_weight.astype(jnp.bfloat16), ("dp", "fsdp"), axis=0, tiled=True),
        lax.all_gather(down_weight.astype(jnp.bfloat16), ("dp", "fsdp"), axis=0, tiled=True),
    )
    upstream = grad_out * live_mask
    upstream_low = upstream.astype(jnp.bfloat16)
    grad_down_bias = jnp.sum(upstream_low, axis=0, dtype=jnp.float32)
    grad_down = left_product(active_low, upstream_low)
    grad_active = right_product(upstream_low, down_back)
    (grad_before,) = gelu_back(grad_active)
    grad_before_low = grad_before.astype(jnp.bfloat16)
    grad_in_bias = jnp.sum(grad_before_low, axis=0, dtype=jnp.float32)
    grad_in = left_product(normed_mid_low, grad_before_low)
    grad_normed_mid = right_product(grad_before_low, up_back)
    grad_residual_part, grad_mlp_gain, grad_mlp_shift = mlp_norm_back(grad_normed_mid)
    grad_residual = upstream + grad_residual_part
    grad_branch_low = grad_residual.astype(jnp.bfloat16)
    grad_proj_bias = jnp.sum(grad_branch_low, axis=0, dtype=jnp.float32)
    grad_proj = left_product(attended_low, grad_branch_low)
    grad_attended = right_product(grad_branch_low, proj_back)
    grad_att_blocks = grad_attended.astype(jnp.bfloat16).reshape(
        block_count, block_rows, HEADS, HEAD_DIM
    )

    def backward_block(running, pieces):
        grad_keys, grad_values = running
        q_part, seg_part, grad_part, log_part = pieces
        scores = masked_scores(q_part, k, seg_part, seg_ids, score_scale)
        p = jnp.exp(scores - log_part[..., None])
        grad_p = jnp.einsum("qhd,khd->hqk", grad_part, v, preferred_element_type=jnp.float32)
        row_dot = jnp.sum(p * grad_p, axis=-1, keepdims=True)
        grad_scores = (p * (grad_p - row_dot)).astype(jnp.bfloat16)
        grad_queries = (
            jnp.einsum("hqk,khd->qhd", grad_scores, k, preferred_element_type=jnp.float32)
            * score_scale
        )
        grad_keys = (
            grad_keys
            + jnp.einsum("hqk,qhd->khd", grad_scores, q_part, preferred_element_type=jnp.float32)
            * score_scale
        )
        grad_values = grad_values + jnp.einsum(
            "hqk,qhd->khd", p.astype(jnp.bfloat16), grad_part, preferred_element_type=jnp.float32
        )
        return ((grad_keys, grad_values), grad_queries)

    zero_keys = jnp.zeros((row_count, HEADS, HEAD_DIM), jnp.float32)
    (grad_keys, grad_values), grad_queries = lax.scan(
        backward_block, (zero_keys, zero_keys), (q_blocks, seg_blocks, grad_att_blocks, log_sums)
    )
    grad_projected = jnp.concatenate(
        [
            grad_queries.reshape(row_count, D),
            grad_keys.reshape(row_count, D),
            grad_values.reshape(row_count, D),
        ],
        axis=1,
    )
    grad_projected_low = grad_projected.astype(jnp.bfloat16)
    grad_qv = jnp.concatenate(
        [
            jnp.sum(grad_projected_low[:, :D], axis=0, dtype=jnp.float32),
            jnp.sum(grad_projected_low[:, 2 * D :], axis=0, dtype=jnp.float32),
        ]
    )
    grad_qkv = left_product(normed_low, grad_projected_low)
    grad_normed = right_product(grad_projected_low, qkv_back)
    grad_x_part, grad_attn_gain, grad_attn_shift = attn_norm_back(grad_normed)
    input_grad = (grad_residual + grad_x_part) * live_mask
    time_grad = lax.dot_general(
        onehot, input_grad, (((0,), (0,)), ((), ())), precision=lax.Precision.HIGHEST
    )
    summed = tuple(
        (
            lax.psum_scatter(grad_attn_gain, ("dp", "fsdp"), scatter_dimension=0, tiled=True),
            lax.psum_scatter(grad_attn_shift, ("dp", "fsdp"), scatter_dimension=0, tiled=True),
            lax.psum_scatter(grad_qkv, ("dp", "fsdp"), scatter_dimension=0, tiled=True),
            lax.psum_scatter(grad_qv, ("dp", "fsdp"), scatter_dimension=0, tiled=True),
            lax.psum_scatter(grad_proj, ("dp", "fsdp"), scatter_dimension=0, tiled=True),
            lax.psum_scatter(grad_proj_bias, ("dp", "fsdp"), scatter_dimension=0, tiled=True),
            lax.psum_scatter(grad_mlp_gain, ("dp", "fsdp"), scatter_dimension=0, tiled=True),
            lax.psum_scatter(grad_mlp_shift, ("dp", "fsdp"), scatter_dimension=0, tiled=True),
            lax.psum_scatter(grad_in, ("dp", "fsdp"), scatter_dimension=0, tiled=True),
            lax.psum_scatter(grad_in_bias, ("dp", "fsdp"), scatter_dimension=0, tiled=True),
            lax.psum_scatter(grad_down, ("dp", "fsdp"), scatter_dimension=0, tiled=True),
            lax.psum_scatter(grad_down_bias, ("dp", "fsdp"), scatter_dimension=0, tiled=True),
        )
    )
    return (block_out, input_grad, time_grad) + summed


def solution(mesh):
    placed = (
        P(("dp", "fsdp"), None),
        P(("dp", "fsdp"), None),
        P(("dp", "fsdp")),
        P(("dp", "fsdp")),
        P(("dp", "fsdp")),
        P(("dp", "fsdp"), None),
        P(("dp", "fsdp")),
        P(("dp", "fsdp"), None),
        P(("dp", "fsdp")),
        P(("dp", "fsdp")),
        P(("dp", "fsdp")),
        P(("dp", "fsdp"), None),
        P(("dp", "fsdp")),
        P(("dp", "fsdp"), None),
        P(("dp", "fsdp")),
        P(("dp", "fsdp"), None),
    )
    return jax.shard_map(
        local,
        mesh=mesh,
        in_specs=placed,
        out_specs=(
            P(("dp", "fsdp"), None),
            P(("dp", "fsdp"), None),
            P(("dp", "fsdp"), None),
            P(("dp", "fsdp")),
            P(("dp", "fsdp")),
            P(("dp", "fsdp"), None),
            P(("dp", "fsdp")),
            P(("dp", "fsdp"), None),
            P(("dp", "fsdp")),
            P(("dp", "fsdp")),
            P(("dp", "fsdp")),
            P(("dp", "fsdp"), None),
            P(("dp", "fsdp")),
            P(("dp", "fsdp"), None),
            P(("dp", "fsdp")),
        ),
        check_vma=False,
    )
```

profile of v0, /device:TPU:0, one launch (start us, length us, event | category | flops | bytes accessed | tf_op | source)
XLA Modules:
  0.0 919.4 jit_solution(14314571595099834646)
XLA Ops:
  22.2 42.8 %all-reduce.17 = (bf16[1536]{0:T(1024)(128)(2,1)S(1)}, bf16[768]{0:T(1024)(128)(2,1)S(1)}, bf16[768]{0:T(1024)(128)(2,1)S(1)}, bf16[768]{0:T(1024)(128)(2,1)S(1)...) all-reduce(bf16[1536]{0:T(1024)(128)(2,1)S(1)} %dynamic-update-slic, ...), channel_id=1, replica_groups=mesh['dp'=4,'fsdp'=8] {'dp','fsdp'}, use_global_device_ids=true, to_apply=%add.2 | all-reduce | flops 9216 | bytes 36864
  101.7 70.6 %while.27 = (s32[]{:T(128)}, bf16[2,512,12,64]{1,3,2,0:T(8,128)(2,1)}, f32[2,12,512]{2,1,0:T(8,128)S(1)}, s32[2,512]{1,0:T(2,128)S(1)}, s32[1024]{0:T(1024)S(1)}...) while((s32[]{:T(128)}, ...), condition=%wide.region_5.6_spmd, body=%wide.region_2.5_spmd.sunk | while | flops 1687153664 | bytes 190292144 | solution.py:115
  102.3 10.6 %fusion.106 = (f32[12,512]{1,0:T(8,128)S(1)}, f32[12,512,1024]{2,1,0:T(8,128)}) fusion(pred[512,1024]{1,0:T(8,128)(4,1)S(1)} %compare_and_fusion.4, bf16[1024,12,64]{0,2,1:T(8,128)(2,1)S(1)} %get-tuple-element.496, bf16[2,512,12,64]{1,3,2,0:T(8,128)(2,1)S(1)} %get-tuple-element.495, s32[]{:T(128)S(6)} %copy.100), kind=kOutput, calls=%fused_computation.3.clone.1 | convolution fusion | flops 824174592 | bytes 28073988 | tf_op jit(solution)/shard_map/while/body/eval_jaxpr/qhd,khd->hqk/dot_general | solution.py:22
  112.9 12.5 %fusion.107 = f32[12,512]{1,0:T(8,128)S(1)} fusion(f32[12,512,1024]{2,1,0:T(8,128)} %get-tuple-element.457, f32[12,512]{1,0:T(8,128)S(1)} %get-tuple-element.458, pred[512,1024]{1,0:T(8,128)(4,1)S(1)} %compare_and_fusion.4), kind=kLoop, calls=%fused_computation.4.clone.1 | loop fusion | flops 25159680 | bytes 25739264 | tf_op jit(solution)/shard_map/while/body/eval_jaxpr/reduce_sum | solution.py:110
  137.6 10.7 %fusion.106 = (f32[12,512]{1,0:T(8,128)S(1)}, f32[12,512,1024]{2,1,0:T(8,128)}) fusion(pred[512,1024]{1,0:T(8,128)(4,1)S(1)} %compare_and_fusion.4, bf16[1024,12,64]{0,2,1:T(8,128)(2,1)S(1)} %get-tuple-element.496, bf16[2,512,12,64]{1,3,2,0:T(8,128)(2,1)S(1)} %get-tuple-element.495, s32[]{:T(128)S(6)} %copy.100), kind=kOutput, calls=%fused_computation.3.clone.1 | convolution fusion | flops 824174592 | bytes 28073988 | tf_op jit(solution)/shard_map/while/body/eval_jaxpr/qhd,khd->hqk/dot_general | solution.py:22
  148.2 12.4 %fusion.107 = f32[12,512]{1,0:T(8,128)S(1)} fusion(f32[12,512,1024]{2,1,0:T(8,128)} %get-tuple-element.457, f32[12,512]{1,0:T(8,128)S(1)} %get-tuple-element.458, pred[512,1024]{1,0:T(8,128)(4,1)S(1)} %compare_and_fusion.4), kind=kLoop, calls=%fused_computation.4.clone.1 | loop fusion | flops 25159680 | bytes 25739264 | tf_op jit(solution)/shard_map/while/body/eval_jaxpr/reduce_sum | solution.py:110
  183.5 13.6 %all-gather.9.cloned.1.call-done = bf16[768,3072]{1,0:T(8,128)(2,1)} async-done(((bf16[24,3072]{1,0:T(8,128)(2,1)}), bf16[768,3072]{1,0:T(8,128)(2,1)}) %all-gather.9.cloned.1.call-update) | async-done | bytes 4718608 | tf_op jit(solution)/shard_map/all_gather | solution.py:69
  197.0 38.1 %multiply_convert_fusion.1 = (bf16[1024,3072]{1,0:T(8,128)(2,1)}, f32[1024,3072]{1,0:T(8,128)}, f32[1024,3072]{1,0:T(8,128)}) fusion(f32[3072]{0:T(1024)S(1)} %copy-done.48, bf16[768,3072]{1,0:T(8,128)(2,1)} %all-gather.9.cloned.1.call-done, f32[1024,768]{0,1:T(8,128)} %copy-done.14, f32[768]{0:T(1024)S(1)} %copy-done.50, f32[768]{0:T(1024)S(1)} %copy-done.41, ...), kind=kOutput, calls=%fused_computation.50 | convolution fusion | flops 5043388416 | bytes 39348224 | tf_op jit(solution)/shard_map/dot_general | solution.py:126
  235.1 27.2 %all-gather.11.cloned.1.call-done = bf16[3072,768]{1,0:T(8,128)(2,1)} async-done(((bf16[96,768]{1,0:T(8,128)(2,1)}), bf16[3072,768]{1,0:T(8,128)(2,1)}) %all-gather.11.cloned.1.call-update) | async-done | bytes 4718608 | tf_op jit(solution)/shard_map/all_gather | solution.py:71
  262.3 19.2 %convert_reduce_fusion = (f32[3072]{0:T(1024)}, bf16[1024,3072]{1,0:T(8,128)(2,1)}) fusion(f32[1024,3072]{1,0:T(8,128)} %get-tuple-element.327, bf16[1024,768]{0,1:T(8,128)(2,1)} %get-tuple-element.319, bf16[3072,768]{1,0:T(8,128)(2,1)} %all-gather.11.cloned.1.call-done, f32[1024,3072]{1,0:T(8,128)} %get-tuple-element.341, f32[3072]{0:T(1024)S(1)} %copy-done.48), kind=kOutput, calls=%fused_computation.48 | convolution fusion | flops 4885312512 | bytes 37773312 | tf_op jit(solution)/shard_map/dot_general | solution.py:32
  322.6 171.8 %while.28 = (s32[]{:T(128)}, f32[1024,12,64]{0,2,1:T(8,128)}, f32[1024,12,64]{0,2,1:T(8,128)}, bf16[2,512,12,64]{1,3,2,0:T(8,128)(2,1)}, bf16[2,512,12,64]{1,3,2...) while((s32[]{:T(128)}, f32[1024,12,64]{0,2,1:T(8,128)}, ...), condition=%wide.region_12.13_spmd.clone, body=%wide.region_10.12_spmd.clone.sunk | while | flops 4126272512 | bytes 231932144 | solution.py:184
  324.6 11.7 %fusion.117 = f32[12,512,1024]{2,1,0:T(8,128)} fusion(bf16[1024,12,64]{0,2,1:T(8,128)(2,1)S(1)} %get-tuple-element.532, bf16[2,512,12,64]{1,3,2,0:T(8,128)(2,1)} %copy-done.4, s32[]{:T(128)S(6)} %copy.110), kind=kOutput, calls=%fused_computation.31.clone.1 | convolution fusion | flops 805306368 | bytes 27525124 | tf_op jit(solution)/shard_map/while/body/eval_jaxpr/qhd,khd->hqk/dot_general | solution.py:22
  336.3 13.7 %bitcast_add_fusion.5 = f32[1024,12,64]{0,2,1:T(8,128)} fusion(f32[1024,12,64]{0,2,1:T(8,128)} %get-tuple-element.514, f32[12,512,1024]{2,1,0:T(8,128)} %fusion.117, f32[12,512]{1,0:T(8,128)S(1)} %dynamic-slice_bitcast_fusion.2, pred[512,1024]{1,0:T(8,128)(4,1)S(1)} %compare_and_fusion.5, pred[]{:T(512)S(6)} %compare.3, ...), kind=kOutput, calls=%fused_computation.23.clone.1 | convolution fusion | flops 832045056 | bytes 32800772 | tf_op jit(solution)/shard_map/while/body/eval_jaxpr/hqk,qhd->khd/dot_general | solution.py:178
  350.0 18.3 %multiply_reduce_fusion.8 = (f32[12,512]{1,0:T(8,128)S(1)}, f32[12,512,1024]{2,1,0:T(8,128)}) fusion(f32[12,512,1024]{2,1,0:T(8,128)} %fusion.117, f32[12,512]{1,0:T(8,128)S(1)} %dynamic-slice_bitcast_fusion.2, pred[512,1024]{1,0:T(8,128)(4,1)S(1)} %compare_and_fusion.5, bf16[1024,12,64]{0,2,1:T(8,128)(2,1)} %get-tuple-element.535, ...), kind=kOutput, calls=%fused_computation.18.clone.1 | convolution fusion | flops 836757504 | bytes 53264388 | tf_op jit(solution)/shard_map/while/body/eval_jaxpr/qhd,khd->hqk/dot_general | solution.py:166
  368.3 21.9 %multiply_convert_fusion.5 = bf16[12,512,1024]{2,1,0:T(8,128)(2,1)} fusion(f32[12,512,1024]{2,1,0:T(8,128)} %get-tuple-element.470, f32[12,512,1024]{2,1,0:T(8,128)} %fusion.117, f32[12,512]{1,0:T(8,128)S(1)} %get-tuple-element.471, f32[12,512]{1,0:T(8,128)S(1)} %dynamic-slice_bitcast_fusion.2, pred[512,1024]{1,0:T(8,128)(4,1)S(1)} %compare_and_fusion.5), kind=kLoop, calls=%fused_computation.17.clone.1 | loop fusion | flops 37748736 | bytes 63488000 | tf_op jit(solution)/shard_map/while/body/eval_jaxpr/convert_element_type | solution.py:168
  410.0 11.5 %fusion.117 = f32[12,512,1024]{2,1,0:T(8,128)} fusion(bf16[1024,12,64]{0,2,1:T(8,128)(2,1)S(1)} %get-tuple-element.532, bf16[2,512,12,64]{1,3,2,0:T(8,128)(2,1)} %copy-done.4, s32[]{:T(128)S(6)} %copy.110), kind=kOutput, calls=%fused_computation.31.clone.1 | convolution fusion | flops 805306368 | bytes 27525124 | tf_op jit(solution)/shard_map/while/body/eval_jaxpr/qhd,khd->hqk/dot_general | solution.py:22
  421.6 14.3 %bitcast_add_fusion.5 = f32[1024,12,64]{0,2,1:T(8,128)} fusion(f32[1024,12,64]{0,2,1:T(8,128)} %get-tuple-element.514, f32[12,512,1024]{2,1,0:T(8,128)} %fusion.117, f32[12,512]{1,0:T(8,128)S(1)} %dynamic-slice_bitcast_fusion.2, pred[512,1024]{1,0:T(8,128)(4,1)S(1)} %compare_and_fusion.5, pred[]{:T(512)S(6)} %compare.3, ...), kind=kOutput, calls=%fused_computation.23.clone.1 | convolution fusion | flops 832045056 | bytes 32800772 | tf_op jit(solution)/shard_map/while/body/eval_jaxpr/hqk,qhd->khd/dot_general | solution.py:178
  435.9 18.1 %multiply_reduce_fusion.8 = (f32[12,512]{1,0:T(8,128)S(1)}, f32[12,512,1024]{2,1,0:T(8,128)}) fusion(f32[12,512,1024]{2,1,0:T(8,128)} %fusion.117, f32[12,512]{1,0:T(8,128)S(1)} %dynamic-slice_bitcast_fusion.2, pred[512,1024]{1,0:T(8,128)(4,1)S(1)} %compare_and_fusion.5, bf16[1024,12,64]{0,2,1:T(8,128)(2,1)} %get-tuple-element.535, ...), kind=kOutput, calls=%fused_computation.18.clone.1 | convolution fusion | flops 836757504 | bytes 53264388 | tf_op jit(solution)/shard_map/while/body/eval_jaxpr/qhd,khd->hqk/dot_general | solution.py:166
  454.0 21.2 %multiply_convert_fusion.5 = bf16[12,512,1024]{2,1,0:T(8,128)(2,1)} fusion(f32[12,512,1024]{2,1,0:T(8,128)} %get-tuple-element.470, f32[12,512,1024]{2,1,0:T(8,128)} %fusion.117, f32[12,512]{1,0:T(8,128)S(1)} %get-tuple-element.471, f32[12,512]{1,0:T(8,128)S(1)} %dynamic-slice_bitcast_fusion.2, pred[512,1024]{1,0:T(8,128)(4,1)S(1)} %compare_and_fusion.5), kind=kLoop, calls=%fused_computation.17.clone.1 | loop fusion | flops 37748736 | bytes 63488000 | tf_op jit(solution)/shard_map/while/body/eval_jaxpr/convert_element_type | solution.py:168
  520.2 11.0 %fusion.50 = f32[768,3072]{1,0:T(8,128)} fusion(bf16[1024,3072]{1,0:T(8,128)(2,1)} %get-tuple-element.347, f32[1024,768]{0,1:T(8,128)} %copy-done.14, f32[768]{0:T(1024)S(1)} %copy-done.51, f32[768]{0:T(1024)S(1)} %copy-done.42, f32[1024]{0:T(1024)S(1)} %copy-done.44, f32[1024]{0:T(1024)S(1)} %copy-done.34), kind=kOutput, calls=%fused_computation.111 | convolution fusion | flops 4835770368 | bytes 18888704 | tf_op jit(solution)/shard_map/dot_general | solution.py:28
  531.9 10.6 %add_multiply_fusion.1 = f32[1024,768]{0,1:T(8,128)} fusion(f32[1024,768]{0,1:T(8,128)} %copy-done.14, bf16[1024,3072]{1,0:T(8,128)(2,1)} %get-tuple-element.326, bf16[3072,768]{1,0:T(8,128)(2,1)} %all-gather.11.cloned.1.call-done, f32[768]{0:T(1024)S(1)} %convert_element_type.149, f32[1024]{0:T(1024)S(1)} %copy-done.28), kind=kOutput, calls=%fused_computation.78 | convolution fusion | flops 4834197504 | bytes 17308672 | tf_op jit(solution)/shard_map/dot_general | solution.py:131
  565.1 41.5 %all-reduce.16 = (f32[768]{0:T(1024)S(1)}, f32[768]{0:T(1024)S(1)}, f32[1536]{0:T(1024)S(1)}, f32[768]{0:T(1024)S(1)}, f32[768]{0:T(1024)S(1)}, /*index=5*/f32[7...) all-reduce(f32[768]{0:T(1024)S(1)} %get-tuple-element.260, ...), channel_id=2, replica_groups=mesh['dp'=4,'fsdp'=8] {'dp','fsdp'}, use_global_device_ids=true, to_apply=%region_16.17.clone | all-reduce | flops 9216 | bytes 73728
  628.7 141.7 %reduce-scatter.11.cloned.1.call-done = f32[96,768]{1,0:T(8,128)} async-done(((f32[3072,768]{1,0:T(8,128)}), f32[96,768]{1,0:T(8,128)}) %reduce-scatter.11.cloned.1.call-update) | async-done | bytes 294928 | tf_op jit(solution)/shard_map/reduce_scatter | solution.py:221
  770.5 141.6 %reduce-scatter.9.cloned.1.call-done = f32[24,3072]{1,0:T(8,128)} async-done(((f32[768,3072]{1,0:T(8,128)}), f32[24,3072]{1,0:T(8,128)}) %reduce-scatter.9.cloned.1.call-update) | async-done | bytes 294928 | tf_op jit(solution)/shard_map/reduce_scatter | solution.py:219
  (269 shorter events, 238.9 us)
Async XLA Ops:
  7.2 69.4 %copy-start = (f32[16,768]{1,0:T(8,128)S(1)}, f32[16,768]{1,0:T(8,128)}, u32[]{:S(2)}) copy-start(f32[16,768]{1,0:T(8,128)} %param.21) | copy-start | bytes 147460
  7.2 72.2 %all-gather.5.cloned.1.call-start = ((), (), s32[]{:S(2)}) async-start(), calls=%async_computation.4 | async-start | bytes 3649536 | tf_op jit(solution)/shard_map/all_gather | solution.py:63
  8.9 168.1 %all-gather.7.cloned.1.call-start = ((), (), s32[]{:S(2)}) async-start(), calls=%async_computation.5 | async-start | bytes 1216512 | tf_op jit(solution)/shard_map/all_gather | solution.py:65
  10.4 186.6 %all-gather.9.cloned.1.call-start = ((), (), s32[]{:S(2)}) async-start(), calls=%async_computation.6 | async-start | bytes 4866048 | tf_op jit(solution)/shard_map/all_gather | solution.py:69
  12.2 250.2 %all-gather.11.cloned.1.call-start = ((), (), s32[]{:S(2)}) async-start(), calls=%async_computation.7 | async-start | bytes 4866048 | tf_op jit(solution)/shard_map/all_gather | solution.py:71
  13.9 610.7 %reduce-scatter.7.cloned.1.call-start = ((), (), s32[]{:S(2)}) async-start(), calls=%async_computation.9 | async-start | bytes 2433024 | tf_op jit(solution)/shard_map/reduce_scatter | solution.py:215
  14.6 62.0 %copy-start.26 = (f32[1024]{0:T(1024)}, f32[1024]{0:T(1024)S(1)}, u32[]{:S(2)}) copy-start(f32[1024]{0:T(1024)S(1)} %compare_convert_fusion) | copy-start | bytes 12292
  65.1 14.3 %copy-start.31 = (f32[768]{0:T(1024)}, f32[768]{0:T(1024)S(1)}, u32[]{:S(2)}) copy-start(f32[768]{0:T(1024)S(1)} %convert_element_type.125) | copy-start | bytes 9220
  65.7 13.7 %copy-start.52 = (f32[768]{0:T(1024)}, f32[768]{0:T(1024)S(1)}, u32[]{:S(2)}) copy-start(f32[768]{0:T(1024)S(1)} %convert_element_type.127) | copy-start | bytes 9220
  102.3 23.1 %copy-start.8 = (bf16[1024,12,64]{0,2,1:T(8,128)(2,1)S(1)}, bf16[1024,12,64]{0,2,1:T(8,128)(2,1)}, u32[]{:S(2)}) copy-start(bf16[1024,12,64]{0,2,1:T(8,128)(2,1)} %get-tuple-element.497) | copy-start | bytes 4718596 | tf_op jit(solution)/shard_map/while
  112.9 15.6 %copy-start.2 = (f32[12,512,1024]{2,1,0:T(8,128)S(1)}, f32[12,512,1024]{2,1,0:T(8,128)}, u32[]{:S(2)}) copy-start(f32[12,512,1024]{2,1,0:T(8,128)} %get-tuple-element.457) | copy-start | bytes 75497472 | tf_op jit(solution)/shard_map/while
  137.5 23.1 %copy-start.8 = (bf16[1024,12,64]{0,2,1:T(8,128)(2,1)S(1)}, bf16[1024,12,64]{0,2,1:T(8,128)(2,1)}, u32[]{:S(2)}) copy-start(bf16[1024,12,64]{0,2,1:T(8,128)(2,1)} %get-tuple-element.497) | copy-start | bytes 4718596 | tf_op jit(solution)/shard_map/while
  148.2 15.5 %copy-start.2 = (f32[12,512,1024]{2,1,0:T(8,128)S(1)}, f32[12,512,1024]{2,1,0:T(8,128)}, u32[]{:S(2)}) copy-start(f32[12,512,1024]{2,1,0:T(8,128)} %get-tuple-element.457) | copy-start | bytes 75497472 | tf_op jit(solution)/shard_map/while
  181.4 15.6 %copy-start.41 = (f32[768]{0:T(1024)S(1)}, f32[768]{0:T(1024)}, u32[]{:S(2)}) copy-start(f32[768]{0:T(1024)} %convert_element_type.139) | copy-start | bytes 9220
  181.4 15.6 %copy-start.48 = (f32[3072]{0:T(1024)S(1)}, f32[3072]{0:T(1024)}, u32[]{:S(2)}) copy-start(f32[3072]{0:T(1024)} %convert_element_type.145) | copy-start | bytes 36868
  181.4 15.6 %copy-start.50 = (f32[768]{0:T(1024)S(1)}, f32[768]{0:T(1024)}, u32[]{:S(2)}) copy-start(f32[768]{0:T(1024)} %convert_element_type.141) | copy-start | bytes 9220
  181.4 118.4 %copy-start.33 = (f32[1024]{0:T(1024)}, f32[1024]{0:T(1024)S(1)}, u32[]{:S(2)}) copy-start(f32[1024]{0:T(1024)S(1)} %broadcast_multiply_fusion) | copy-start | bytes 12292
  183.5 116.4 %copy-start.43 = (f32[1024]{0:T(1024)}, f32[1024]{0:T(1024)S(1)}, u32[]{:S(2)}) copy-start(f32[1024]{0:T(1024)S(1)} %fusion.46) | copy-start | bytes 12292
  321.2 307.5 %reduce-scatter.5.cloned.1.call-start = ((), (), s32[]{:S(2)}) async-start(), calls=%async_computation.8 | async-start | bytes 7299072 | tf_op jit(solution)/shard_map/reduce_scatter | solution.py:213
  324.5 11.7 %copy-start.17 = (bf16[2,512,12,64]{1,3,2,0:T(8,128)(2,1)S(1)}, bf16[2,512,12,64]{1,3,2,0:T(8,128)(2,1)}, u32[]{:S(2)}) copy-start(bf16[2,512,12,64]{1,3,2,0:T(8,128)(2,1)} %get-tuple-element.534) | copy-start | bytes 4718596 | tf_op jit(solution)/shard_map/while
  509.5 260.9 %reduce-scatter.11.cloned.1.call-start = ((), (), s32[]{:S(2)}) async-start(), calls=%async_computation.11 | async-start | bytes 9732096 | tf_op jit(solution)/shard_map/reduce_scatter | solution.py:221
  519.5 392.5 %reduce-scatter.9.cloned.1.call-start = ((), (), s32[]{:S(2)}) async-start(), calls=%async_computation.10 | async-start | bytes 9732096 | tf_op jit(solution)/shard_map/reduce_scatter | solution.py:219
  563.9 46.3 %copy-start.38 = (f32[1024]{0:T(1024)S(1)}, f32[1024]{0:T(1024)}, u32[]{:S(2)}) copy-start(f32[1024]{0:T(1024)} %copy-done.37) | copy-start | bytes 12292
  617.3 294.8 %copy-start.1 = (f32[16,768]{1,0:T(8,128)S(1)}, f32[16,768]{1,0:T(8,128)}, u32[]{:S(2)}) copy-start(f32[16,768]{1,0:T(8,128)} %param.21) | copy-start | bytes 147460
  (46 other events, 157.8 us)
Sparse Core Ops, SparseCore 0:
  11.5 63.2 all-gather.4
  78.3 52.6 all-gather.6
  134.5 62.4 all-gather.8
  200.4 61.9 all-gather.10
  321.3 98.0 reduce-scatter.6
  509.7 119.0 reduce-scatter.4
  635.2 135.2 reduce-scatter.10
  776.9 135.1 reduce-scatter.8
where the time goes:
time: 928 us; the launch traced here: 919 us
  waiting for transfers between devices  328 us (35%)
  matrix products  301 us (32%)
  other arithmetic  110 us (12%)
  blocking collectives  84.3 us (9%)
  local copies, waits for them, and re-layouts  78.8 us (8%)
  between operations  15.2 us (2%)
    reduce_scatter x1, waiting for transfers between devices, local(): lax.psum_scatter(grad_down, ('dp', 'fsdp'), scatter_dimension=0, tiled=True)  142 us
    reduce_scatter x1, waiting for transfers between devices, local(): lax.psum_scatter(grad_in, ('dp', 'fsdp'), scatter_dimension=0, tiled=True)  142 us
    unnamed x2, blocking collectives  84.3 us
    dot_general x4, matrix products, masked_scores(): jnp.einsum('qhd,khd->hqk', q_part, k, preferred_element_type=jnp.float32)  44.5 us
    convert_element_type x2, other arithmetic, backward_block(): grad_scores = (p * (grad_p - row_dot)).astype(jnp.bfloat16)  43.2 us
    dot_general x4, matrix products, right_product(): lax.dot_general(a, b, (((1,), (1,)), ((), ())), preferred_element_type=jn...  43.1 us
    dot_general x1, matrix products, local(): jnp.dot(normed_mid_low, up_full, preferred_element_type=jnp.float32)  38.1 us
    dot_general x2, matrix products, backward_block(): jnp.einsum('qhd,khd->hqk', grad_part, v, preferred_element_type=jnp.float32)  36.4 us
  transfers between devices with their start and end apart: 8, of which 5 were waited for; matrix products, arithmetic and copies ran while one was open for 45% of the time, Pallas kernels for 0%

commit v1 on v0

v1 whole, which is shorter than its diff:
```python
import functools

import jax
import jax.numpy as jnp
from jax import lax
from jax.experimental import pallas as pl
from jax.experimental.pallas import tpu as pltpu
from jax.sharding import PartitionSpec as P

D = 768
HEADS = 12
HEAD_DIM = 64
FF = 3072
BLOCK = 1024
SHORT = 64
GROUPS = BLOCK // SHORT
PAIRS = HEADS // 2
TB = 256
NEG = -1e30
F32 = jnp.float32
BF16 = jnp.bfloat16
VMEM_LIMIT = 62 * 1024 * 1024
ANY = pl.BlockSpec(memory_space=pl.ANY)
VMEM = pl.BlockSpec(memory_space=pltpu.VMEM)
SMEM = pl.BlockSpec(memory_space=pltpu.SMEM)
ERFC_SCALE = 0.44
ERFC_POLY = (
    0.24822097621403005,
    0.2488708795734658,
    0.21731516533725015,
    0.21580763970434977,
    -0.020173037922183695,
    0.2966799647080617,
    -0.2779439059726245,
    0.07122249905985603,
)


def rows_at(i, size):
    return pl.ds(pl.multiple_of(i * size, size), size)


def mm(a, b):
    return lax.dot_general(a, b, (((1,), (0,)), ((), ())), preferred_element_type=F32)


def mm_t(a, b):
    return lax.dot_general(a, b, (((1,), (1,)), ((), ())), preferred_element_type=F32)


def normalize(v):
    center = v - jnp.mean(v, axis=-1, keepdims=True)
    spread = jnp.mean(center * center, axis=-1, keepdims=True)
    scale = lax.rsqrt(spread + 1e-05)
    return center * scale, scale


def norm_back(grad, gain, n, scale):
    g = grad * gain
    return scale * (
        g - jnp.mean(g, axis=-1, keepdims=True) - n * jnp.mean(g * n, axis=-1, keepdims=True)
    )


def fold8(v):
    return jnp.sum(v.reshape(v.shape[0] // 8, 8, v.shape[1]), axis=0)


def gelu_parts(u):
    z = jnp.abs(u) * 0.7071067811865476
    t = 1.0 / (1.0 + ERFC_SCALE * z)
    poly = jnp.full_like(t, ERFC_POLY[-1])
    for c in ERFC_POLY[-2::-1]:
        poly = poly * t + c
    e = jnp.exp(-(z * z))
    tail = 0.5 * poly * t * e
    phi = jnp.where(u >= 0, 1.0 - tail, tail)
    return u * phi, phi + u * e * 0.3989422804014327


class Mover:
    def __init__(self, sems):
        self.sems, self.next = sems, 0

    def start(self, src, dst):
        copy = pltpu.make_async_copy(src, dst, self.sems.at[self.next])
        self.next += 1
        copy.start()
        return copy


def stage_norm1(sid, time, vecs, x, a1, a1t):
    gain, shift = vecs[0:1, :], vecs[1:2, :]

    @pl.loop(0, BLOCK // 128)
    def _(i):
        parts = []
        for half in range(2):
            s = sid[2 * i + half]
            live = (s >= 0).astype(F32)
            row = time[pl.ds(jnp.maximum(s, 0), 1), :]
            parts.append((x[rows_at(2 * i + half, SHORT), :] + row) * live)
        block = jnp.concatenate(parts, axis=0)
        at = rows_at(i, 128)
        x[at, :] = block
        n, _ = normalize(block)
        a = n * gain + shift
        a1[at, :] = a.astype(BF16)
        a1t[:, at] = a.T.astype(BF16)


def mask_rows(sid, i, groups):
    lane = lax.rem(lax.broadcasted_iota(jnp.int32, (SHORT, 128), 1), 64)
    mq, mk = [], []
    for g in range(groups):
        s = sid[groups * i + g]
        own = jnp.where(s >= 0, s, 16)
        mk.append((lane == own).astype(F32))
        bad = ((lane < 16) & (lane != s)) | (lane == 16)
        mq.append(jnp.where(bad, NEG, 0.0))
    return jnp.concatenate(mq, axis=0), jnp.concatenate(mk, axis=0)


def low_lanes(shape):
    return lax.broadcasted_iota(jnp.int32, shape, 1) < 64


def low_rows(shape):
    return lax.broadcasted_iota(jnp.int32, shape, 0) < 64


def stage_q(sid, vecs, a1, w, q0, q1):
    @pl.loop(0, BLOCK // TB)
    def _(i):
        at = rows_at(i, TB)
        mq, _ = mask_rows(sid, i, TB // SHORT)
        acc = mm(a1[at, :], w) + vecs[2:3, :]
        acc = acc.astype(BF16).astype(F32) * (HEAD_DIM**-0.5)
        low = low_lanes((TB, 128))
        for p in range(PAIRS):
            part = acc[:, 128 * p : 128 * p + 128]
            q0[at, 128 * p : 128 * p + 128] = jnp.where(low, part, mq).astype(BF16)
            q1[at, 128 * p : 128 * p + 128] = jnp.where(low, mq, part).astype(BF16)


def stage_k(sid, a1, w, k0, k1, kt):
    @pl.loop(0, BLOCK // TB)
    def _(i):
        at = rows_at(i, TB)
        _, mk = mask_rows(sid, i, TB // SHORT)
        acc = mm(a1[at, :], w)
        low = low_lanes((TB, 128))
        for p in range(PAIRS):
            part = acc[:, 128 * p : 128 * p + 128]
            k0[at, 128 * p : 128 * p + 128] = jnp.where(low, part, mk).astype(BF16)
            k1[at, 128 * p : 128 * p + 128] = jnp.where(low, mk, part).astype(BF16)
        kt[:, at] = acc.T.astype(BF16)


def stage_v(vecs, a1, w, v, vt0, vt1):
    @pl.loop(0, BLOCK // TB)
    def _(i):
        at = rows_at(i, TB)
        acc = mm(a1[at, :], w) + vecs[3:4, :]
        v[at, :] = acc.astype(BF16)
        accT = acc.T
        low = low_rows((128, TB))
        for p in range(PAIRS):
            part = accT[128 * p : 128 * p + 128, :]
            vt0[128 * p : 128 * p + 128, at] = jnp.where(low, part, 1.0).astype(BF16)
            vt1[128 * p : 128 * p + 128, at] = jnp.where(low, 1.0, part).astype(BF16)


QB = 256


def attention_step(step, q0, q1, k0, k1, vt0, vt1, o, ot, lse):
    pair, part = step // (BLOCK // QB), step % (BLOCK // QB)
    lanes, at = rows_at(pair, 128), rows_at(part, QB)
    outs, logs = [], []
    for q, k, vt, total_row in ((q0, k0, vt0, 64), (q1, k1, vt1, 0)):
        scores = mm_t(k[:, lanes], q[at, lanes])
        top = jnp.max(scores, axis=0, keepdims=True)
        e = jnp.exp(scores - top).astype(BF16)
        res = mm(vt[lanes, :], e)
        total = res[total_row : total_row + 1, :]
        outs.append(res * (1.0 / total))
        logs.append(top + jnp.log(total))
    both = jnp.where(low_rows((128, QB)), outs[0], outs[1])
    ot[lanes, at] = both.astype(BF16)
    o[at, lanes] = both.T.astype(BF16)
    lse[pl.ds(2 * pair, 1), at] = logs[0]
    lse[pl.ds(2 * pair + 1, 1), at] = logs[1]


def kernel_a(sid, hidden, time, vecs, wqkv, x_h, a1t_h, q0_h, q1_h, k0_h, k1_h, v_h, kt_h, o_h, ot_h, lse,
             x, a1, a1t, q0, q1, k0, k1, v, kt, vt0, vt1, o, ot, w, sems):
    mv = Mover(sems)
    cx = mv.start(hidden, x)
    cw = [mv.start(wqkv.at[:, pl.ds(D * j, D)], w.at[j]) for j in range(3)]
    cx.wait()
    stage_norm1(sid, time, vecs, x, a1, a1t)
    outs = [mv.start(x, x_h), mv.start(a1t, a1t_h)]
    cw[0].wait()
    stage_q(sid, vecs, a1, w[0], q0, q1)
    outs += [mv.start(q0, q0_h), mv.start(q1, q1_h)]
    cw[1].wait()
    stage_k(sid, a1, w[1], k0, k1, kt)
    outs += [mv.start(k0, k0_h), mv.start(k1, k1_h), mv.start(kt, kt_h)]
    cw[2].wait()
    stage_v(vecs, a1, w[2], v, vt0, vt1)
    outs += [mv.start(v, v_h)]

    @pl.loop(0, PAIRS * (BLOCK // QB))
    def _(step):
        attention_step(step, q0, q1, k0, k1, vt0, vt1, o, ot, lse)

    outs += [mv.start(o, o_h), mv.start(ot, ot_h)]
    for c in outs:
        c.wait()


def sds(shape, dtype):
    return jax.ShapeDtypeStruct(shape, dtype)


TOK = (BLOCK, D)
TOKT = (D, BLOCK)


def vm(shape, dtype):
    return pltpu.VMEM(shape, dtype)


def call_a(sid, hidden, time, vecs, wqkv):
    out = [sds(TOK, F32), sds(TOKT, BF16)] + [sds(TOK, BF16)] * 5 + [sds(TOKT, BF16), sds(TOK, BF16), sds(TOKT, BF16), sds((16, BLOCK), F32)]
    return pl.pallas_call(
        kernel_a,
        name="part_a",
        out_shape=out,
        in_specs=[SMEM, ANY, VMEM, VMEM, ANY],
        out_specs=[ANY] * 10 + [VMEM],
        scratch_shapes=[vm(TOK, F32), vm(TOK, BF16), vm(TOKT, BF16)] + [vm(TOK, BF16)] * 5 + [vm(TOKT, BF16)] * 3
        + [vm(TOK, BF16), vm(TOKT, BF16), vm((3, D, D), BF16), pltpu.SemaphoreType.DMA((16,))],
        compiler_params=pltpu.CompilerParams(vmem_limit_bytes=VMEM_LIMIT),
    )(sid, hidden, time, vecs, wqkv)


def kernel_b(sid, x_h, o_h, gout_h, vecs, wout_h, win_h, wdown_h,
             out_h, gx1_h, gb_h, go0_h, go1_h, dots, gdown_h, gin_h, sums,
             x, o, gy, wout, win, wdown, gm, a2t, ht, gu, gb, go0, go1, stage, sems):
    mv = Mover(sems)
    cx, co, cg = mv.start(x_h, x), mv.start(o_h, o), mv.start(gout_h, gy)
    cwo = mv.start(wout_h, wout)
    cwi = [mv.start(win_h.at[:, pl.ds(D * j, D)], win.at[j]) for j in range(4)]
    cwd = [mv.start(wdown_h.at[pl.ds(D * j, D), :], wdown.at[j]) for j in range(4)]
    sums[...] = jnp.zeros_like(sums)
    for c in [cx, co, cg, cwo] + cwi + cwd:
        c.wait()
    lane = lax.broadcasted_iota(jnp.int32, (16, D), 1) // HEAD_DIM
    heads = (lane == lax.broadcasted_iota(jnp.int32, (16, D), 0)).astype(BF16)
    blocks = BLOCK // TB
    outs = []
    so = mv.sems

    def out_copies(i):
        at = rows_at(i, TB)
        return [pltpu.make_async_copy(x.at[at, :], out_h.at[at, :], so.at[16]),
                pltpu.make_async_copy(gy.at[at, :], gx1_h.at[at, :], so.at[17])]

    @pl.loop(0, blocks)
    def _(i):
        at = rows_at(i, TB)
        live = jnp.concatenate(
            [jnp.full((SHORT, 1), (sid[(TB // SHORT) * i + g] >= 0).astype(F32), F32) for g in range(TB // SHORT)], axis=0)
        x1 = x[at, :] + mm(o[at, :], wout[...]) + vecs[4:5, :]
        n2, r2 = normalize(x1)
        a2f = n2 * vecs[5:6, :] + vecs[6:7, :]
        a2 = a2f.astype(BF16)
        a2t[:, at] = a2f.T.astype(BF16)
        gyb = gy[at, :] * live
        gmb = gyb.astype(BF16)
        gm[at, :] = gmb
        acc = x1 + vecs[11:12, :]
        ga2 = jnp.zeros((TB, D), F32)
        for j in range(4):
            u = mm(a2, win[j]) + vecs[7 + j : 8 + j, :]
            hf, slope = gelu_parts(u)
            ht[D * j : D * j + D, at] = hf.T.astype(BF16)
            acc = acc + mm(hf.astype(BF16), wdown[j])
            guf = mm_t(gmb, wdown[j]) * slope
            gub = guf.astype(BF16)
            gu[at, D * j : D * j + D] = gub
            sums[4 + j] += fold8(gub.astype(F32))
            ga2 = ga2 + mm_t(gub, win[j])
        x[at, :] = acc * live
        sums[8] += fold8(gmb.astype(F32))
        sums[2] += fold8(ga2 * n2)
        sums[3] += fold8(ga2)
        gx1 = gyb + norm_back(ga2, vecs[5:6, :], n2, r2)
        gy[at, :] = gx1
        for c in out_copies(i):
            c.start()
        gbb = gx1.astype(BF16)
        gb[at, :] = gbb
        sums[1] += fold8(gbb.astype(F32))
        go = mm_t(gbb, wout[...]).astype(BF16).astype(F32)
        prod = go * o[at, :].astype(F32)
        hi = prod.astype(BF16)
        lo = (prod - hi.astype(F32)).astype(BF16)
        dots[:, at] = mm_t(heads, hi) + mm_t(heads, lo)
        low = lax.rem(lax.broadcasted_iota(jnp.int32, (TB, D), 1), 128) < 64
        go0[at, :] = jnp.where(low, go, 0.0).astype(BF16)
        go1[at, :] = jnp.where(low, 0.0, go).astype(BF16)

    outs += [mv.start(gb, gb_h), mv.start(go0, go0_h), mv.start(go1, go1_h)]

    def tile_out(j, slot):
        return pltpu.make_async_copy(stage.at[slot], gdown_h.at[rows_at(j, D), :], so.at[18 + slot])

    def tile_in(j, slot):
        return pltpu.make_async_copy(stage.at[slot], gin_h.at[:, pl.ds(D * j, D)], so.at[18 + slot])

    pending = [None, None]
    for t in range(8):
        slot, j = t % 2, t % 4
        if pending[slot] is not None:
            pending[slot].wait()

        @pl.loop(0, D // TB)
        def _(r):
            if t < 4:
                stage[slot, rows_at(r, TB), :] = mm(ht[pl.ds(pl.multiple_of(D * j + r * TB, TB), TB), :], gm[...]).astype(BF16)
            else:
                stage[slot, rows_at(r, TB), :] = mm(a2t[rows_at(r, TB), :], gu[:, D * j : D * j + D]).astype(BF16)

        pending[slot] = tile_out(j, slot) if t < 4 else tile_in(j, slot)
        pending[slot].start()
    for c in pending:
        c.wait()
    for c in outs:
        c.wait()
    for i in range(blocks):
        for c in out_copies(i):
            c.wait()


def call_b(sid, x, o, gout, vecs, wout, win, wdown):
    out = [sds(TOK, F32), sds(TOK, F32)] + [sds(TOK, BF16)] * 3 + [sds((16, BLOCK), F32), sds((FF, D), BF16), sds((D, FF), BF16), sds((9, 8, D), F32)]
    return pl.pallas_call(
        kernel_b,
        name="part_b",
        out_shape=out,
        in_specs=[SMEM, ANY, ANY, ANY, VMEM, ANY, ANY, ANY],
        out_specs=[ANY] * 5 + [VMEM, ANY, ANY, VMEM],
        scratch_shapes=[vm(TOK, F32), vm(TOK, BF16), vm(TOK, F32), vm((D, D), BF16), vm((4, D, D), BF16), vm((4, D, D), BF16),
                        vm(TOK, BF16), vm(TOKT, BF16), vm((FF, BLOCK), BF16), vm((BLOCK, FF), BF16),
                        vm(TOK, BF16), vm(TOK, BF16), vm(TOK, BF16), vm((2, D, D), BF16), pltpu.SemaphoreType.DMA((20,))],
        compiler_params=pltpu.CompilerParams(vmem_limit_bytes=VMEM_LIMIT),
    )(sid, x, o, gout, vecs, wout, win, wdown)


def attention_back_step(step, q0, q1, k0, k1, v, kt, go0, go1, lse, dots, gk_acc, gv_acc, gqkv):
    parts = BLOCK // QB
    pair, part = step // parts, step % parts
    lanes, at = rows_at(pair, 128), rows_at(part, QB)
    gk_parts, gq_parts, pbs = [], [], []
    vv = v[:, lanes]
    for h, (q, k, go) in enumerate(((q0, k0, go0), (q1, k1, go1))):
        scores = mm_t(k[:, lanes], q[at, lanes])
        p = jnp.exp(scores - lse[pl.ds(2 * pair + h, 1), at])
        gp = mm_t(vv, go[at, lanes])
        gs = (p * (gp - dots[pl.ds(2 * pair + h, 1), at])).astype(BF16)
        pbs.append(mm(p.astype(BF16), go[at, lanes]))
        gk_parts.append(mm(gs, q[at, lanes]))
        gq_parts.append(mm(kt[lanes, :], gs))
    gk = jnp.where(low_lanes((BLOCK, 128)), gk_parts[0], gk_parts[1])
    gv = pbs[0] + pbs[1]
    gq = jnp.where(low_rows((128, QB)), gq_parts[0], gq_parts[1]) * (HEAD_DIM**-0.5)
    gqkv[0, at, lanes] = gq.T.astype(BF16)
    first = part == 0
    gk_acc[...] = jnp.where(first, gk, gk_acc[...] + gk)
    gv_acc[...] = jnp.where(first, gv, gv_acc[...] + gv)

    @pl.when(part == parts - 1)
    def _():
        gqkv[1, :, lanes] = gk_acc[...].astype(BF16)
        gqkv[2, :, lanes] = gv_acc[...].astype(BF16)


def kernel_c(sid, x_h, a1t_h, q0_h, q1_h, k0_h, k1_h, v_h, kt_h, ot_h, lse, gx1_h, gb_h, go0_h, go1_h, dots, vecs, wqkv_h,
             ig_h, tg, gqkvw_h, goutw_h, sums,
             x, a1t, q0, q1, k0, k1, v, kt, ot, gx1, gb, go0, go1, w, gqkv, gk_acc, gv_acc, gw, gwo, tsum, sems):
    mv = Mover(sems)
    early = [mv.start(s, d) for s, d in ((ot_h, ot), (gb_h, gb), (q0_h, q0), (q1_h, q1), (k0_h, k0), (k1_h, k1), (v_h, v), (kt_h, kt), (go0_h, go0), (go1_h, go1))]
    late = [mv.start(a1t_h, a1t), mv.start(x_h, x), mv.start(gx1_h, gx1)]
    late += [mv.start(wqkv_h.at[:, pl.ds(D * j, D)], w.at[j]) for j in range(3)]
    for c in early[:2]:
        c.wait()
    sums[...] = jnp.zeros_like(sums)

    @pl.loop(0, D // TB)
    def _(r):
        gwo[rows_at(r, TB), :] = mm(ot[rows_at(r, TB), :], gb[...]).astype(BF16)

    outs = [mv.start(gwo, goutw_h)]
    for c in early[2:]:
        c.wait()

    @pl.loop(0, PAIRS * (BLOCK // QB))
    def _(step):
        attention_back_step(step, q0, q1, k0, k1, v, kt, go0, go1, lse, dots, gk_acc, gv_acc, gqkv)

    for c in late:
        c.wait()
    for j in range(3):
        @pl.loop(0, D // TB)
        def _(r):
            gw[j, rows_at(r, TB), :] = mm(a1t[rows_at(r, TB), :], gqkv[j]).astype(BF16)

        outs.append(mv.start(gw.at[j], gqkvw_h.at[:, pl.ds(D * j, D)]))
    gain = vecs[0:1, :]

    @pl.loop(0, BLOCK // TB)
    def _(i):
        at = rows_at(i, TB)
        ga1 = mm_t(gqkv[0, at, :], w[0]) + mm_t(gqkv[1, at, :], w[1]) + mm_t(gqkv[2, at, :], w[2])
        sums[2] += fold8(gqkv[0, at, :].astype(F32))
        sums[3] += fold8(gqkv[2, at, :].astype(F32))
        n1, r1 = normalize(x[at, :])
        sums[0] += fold8(ga1 * n1)
        sums[1] += fold8(ga1)
        total = gx1[at, :] + norm_back(ga1, gain, n1, r1)
        for g in range(TB // SHORT):
            s = sid[(TB // SHORT) * i + g]
            live = (s >= 0).astype(F32)
            part = total[SHORT * g : SHORT * g + SHORT, :] * live
            x[rows_at((TB // SHORT) * i + g, SHORT), :] = part
            tsum[pl.ds((TB // SHORT) * i + g, 1), :] = jnp.sum(part, axis=0, keepdims=True)

    outs.append(mv.start(x, ig_h))
    row = lax.broadcasted_iota(jnp.int32, (GROUPS, D), 0)
    acc = jnp.zeros((GROUPS, D), F32)
    for g in range(GROUPS):
        acc = acc + jnp.where(row == sid[g], tsum[g : g + 1, :], 0.0)
    tg[...] = acc
    for c in outs:
        c.wait()


def call_c(sid, x, a1t, q0, q1, k0, k1, v, kt, ot, lse, gx1, gb, go0, go1, dots, vecs, wqkv):
    out = [sds(TOK, F32), sds((GROUPS, D), F32), sds((D, 3 * D), BF16), sds((D, D), BF16), sds((4, 8, D), F32)]
    return pl.pallas_call(
        kernel_c,
        name="part_c",
        out_shape=out,
        in_specs=[SMEM] + [ANY] * 9 + [VMEM] + [ANY] * 4 + [VMEM, VMEM, ANY],
        out_specs=[ANY, VMEM, ANY, ANY, VMEM],
        scratch_shapes=[vm(TOK, F32), vm(TOKT, BF16)] + [vm(TOK, BF16)] * 5 + [vm(TOKT, BF16)] * 2 + [vm(TOK, F32)] + [vm(TOK, BF16)] * 3
        + [vm((3, D, D), BF16), vm((3, BLOCK, D), BF16), vm((BLOCK, 128), F32), vm((BLOCK, 128), F32), vm((3, D, D), BF16), vm((D, D), BF16),
           vm((GROUPS, D), F32), pltpu.SemaphoreType.DMA((24,))],
        compiler_params=pltpu.CompilerParams(vmem_limit_bytes=VMEM_LIMIT),
    )(sid, x, a1t, q0, q1, k0, k1, v, kt, ot, lse, gx1, gb, go0, go1, dots, vecs, wqkv)


AXES = ("dp", "fsdp")
MESH = pl.DeviceIdType.MESH
SMALL = ((0, 24, 0), (24, 24, 1), (48, 48, 2), (96, 24, 4), (120, 24, 5), (144, 24, 6), (168, 96, 7), (264, 24, 11))
SMALL_LEN = 384


class Peers:
    def __init__(self):
        self.z, self.f = lax.axis_index("dp"), lax.axis_index("fsdp")
        self.c = self.f % 2
        self.yx = self.f // 2
        x, y = self.yx % 2, self.yx // 2
        self.partner = self.f + 1 - 2 * self.c
        self.fx, self.fy = self.f + 2 - 4 * x, self.f + 4 - 8 * y
        self.fd = self.fx + 4 - 8 * y
        self.qx, self.qy, self.qd = self.fx // 2, self.fy // 2, self.fd // 2
        self.dev = self.z * 8 + self.f

    def up(self, d):
        return (self.z + d) % 4

    def at(self, name, d=0):
        if name == "z":
            return (self.up(d), self.f)
        return (self.z, {"x": self.fx, "y": self.fy, "p": self.partner}[name])

    def greet(self):
        barrier = pltpu.get_barrier_semaphore()
        for target in [self.at("p"), self.at("x"), self.at("y")] + [self.at("z", d) for d in (1, 2, 3)]:
            pl.semaphore_signal(barrier, inc=1, device_id=target, device_id_type=MESH)
        pl.semaphore_wait(barrier, 6)


class Links:
    def __init__(self, peers, send, recv):
        self.peers, self.send, self.recv = peers, send, recv
        self.slots, self.sent = {}, []

    def slot(self, key):
        return self.slots.setdefault(key, len(self.slots))

    def start(self, key, src, dst, name, d=0):
        n = self.slot(key)
        copy = pltpu.make_async_remote_copy(
            src_ref=src, dst_ref=dst, send_sem=self.send.at[n], recv_sem=self.recv.at[n],
            device_id=self.peers.at(name, d), device_id_type=MESH)
        copy.start()
        self.sent.append(copy)

    def arrived(self, key, dst):
        n = self.slot(key)
        pltpu.make_async_remote_copy(
            src_ref=dst, dst_ref=dst, send_sem=self.send.at[n], recv_sem=self.recv.at[n],
            device_id=self.peers.at("p"), device_id_type=MESH).wait_recv()

    def finish(self):
        for copy in self.sent:
            copy.wait_send()
        self.sent = []


GATHER_SLOTS = 19


class Gather:
    def __init__(self, name, links, own, full, sem):
        self.name, self.links, self.own, self.full, self.sem = name, links, own, full, sem

    def key(self, *k):
        return (self.name,) + k

    def piece(self, d, f):
        return self.full.at[(self.links.peers.z + 4 - d) % 4, f]

    def begin(self):
        p = self.links.peers
        here = self.full.at[p.z, p.f]
        for d in (1, 3, 2):
            self.links.start(self.key("z", d), self.own, here, "z", d)
        self.local = pltpu.make_async_copy(self.own, here, self.sem)
        self.local.start()

    def first(self):
        p, links = self.links.peers, self.links
        for d in (0, 1, 3, 2):
            piece = self.piece(d, p.f)
            if d:
                links.arrived(self.key("z", d), piece)
            src = piece if d else self.own
            links.start(self.key("x", d), src, piece, "x")
            links.start(self.key("y", d), src, piece, "y")
        self.local.wait()
        mine = self.full.at[:, p.f]
        links.start(self.key("p", 0), mine, mine, "p")

    def second(self):
        p, links = self.links.peers, self.links
        for d in (0, 1, 3, 2):
            px, py = self.piece(d, p.fx), self.piece(d, p.fy)
            links.arrived(self.key("x", d), px)
            links.arrived(self.key("y", d), py)
            if d < 2:
                links.start(self.key("d", d), px, px, "y")
            else:
                links.start(self.key("d", d), py, py, "x")
        for n, f in ((1, p.fx), (2, p.fy)):
            part = self.full.at[:, f]
            links.start(self.key("p", n), part, part, "p")

    def third(self):
        p, links = self.links.peers, self.links
        for d in range(4):
            links.arrived(self.key("d", d), self.piece(d, p.fd))
        part = self.full.at[:, p.fd]
        links.start(self.key("p", 3), part, part, "p")

    def last(self):
        p, links = self.links.peers, self.links
        for n, f in enumerate((p.f, p.fx, p.fy, p.fd)):
            other = f + 1 - 2 * p.c
            links.arrived(self.key("p", n), self.full.at[:, other])


SCATTER_SLOTS = 10


class Scatter:
    def __init__(self, name, links, parts, out, bufs, sem):
        self.name, self.links, self.parts, self.out, self.sem = name, links, parts, out, sem
        self.t, self.p, self.dx, self.dy, self.xr, self.yr, self.zr = bufs

    def key(self, *k):
        return (self.name,) + k

    def begin(self):
        p = self.links.peers
        self.links.start(self.key("p"), self.parts.at[:, :, 1 - p.c], self.p, "p")
        self.local = pltpu.make_async_copy(self.parts.at[:, :, p.c], self.t, self.sem)
        self.local.start()

    def add(self, q, zs, ref, base=0):
        t = self.t

        @pl.loop(zs[0], zs[1])
        def _(i):
            t[i, q] = (t[i, q].astype(F32) + ref(i - base).astype(F32)).astype(BF16)

    def first(self):
        p, links, t = self.links.peers, self.links, self.t
        self.local.wait()
        links.arrived(self.key("p"), self.p)
        self.add(p.qd, (0, 4), lambda i: self.p[i, p.qd])
        links.start(self.key("dx"), t.at[pl.ds(0, 2), p.qd], self.dx, "x")
        links.start(self.key("dy"), t.at[pl.ds(2, 2), p.qd], self.dy, "y")
        self.add(p.qx, (0, 4), lambda i: self.p[i, p.qx])
        links.start(self.key("x", 0), t.at[pl.ds(0, 2), p.qx], self.xr.at[pl.ds(0, 2)], "x")
        self.add(p.qy, (0, 4), lambda i: self.p[i, p.qy])
        links.start(self.key("y", 1), t.at[pl.ds(2, 2), p.qy], self.yr.at[pl.ds(2, 2)], "y")
        self.add(p.yx, (0, 4), lambda i: self.p[i, p.yx])

    def second(self):
        p, links, t = self.links.peers, self.links, self.t
        links.arrived(self.key("dy"), self.dy)
        self.add(p.qx, (2, 4), lambda i: self.dy[i], 2)
        links.start(self.key("x", 1), t.at[pl.ds(2, 2), p.qx], self.xr.at[pl.ds(2, 2)], "x")
        links.arrived(self.key("dx"), self.dx)
        self.add(p.qy, (0, 2), lambda i: self.dx[i])
        links.start(self.key("y", 0), t.at[pl.ds(0, 2), p.qy], self.yr.at[pl.ds(0, 2)], "y")

    def third(self):
        p, links, t = self.links.peers, self.links, self.t
        for n in range(2):
            links.arrived(self.key("x", n), self.xr.at[pl.ds(2 * n, 2)])
            links.arrived(self.key("y", n), self.yr.at[pl.ds(2 * n, 2)])

        @pl.loop(0, 4)
        def _(i):
            t[i, p.yx] = (t[i, p.yx].astype(F32) + self.xr[i].astype(F32) + self.yr[i].astype(F32)).astype(BF16)

        for d in (2, 1, 3):
            links.start(self.key("z", d), t.at[p.up(d), p.yx], self.zr.at[d - 1], "z", d)

    def last(self):
        p, links = self.links.peers, self.links
        for d in (1, 2, 3):
            links.arrived(self.key("z", d), self.zr.at[d - 1])
        total = self.t[p.z, p.yx].astype(F32)
        for n in range(3):
            total = total + self.zr[n].astype(F32)
        self.out[...] = total


def scatter_bufs(rows, cols):
    return [pltpu.VMEM(lead + (rows, cols), BF16) for lead in ((4, 4), (4, 4), (2,), (2,), (4,), (4,), (3,))]


class SmallSum:
    def __init__(self, links, value, bufs):
        self.links, self.value, self.bufs = links, value, bufs

    def send(self, n, name):
        self.links.start(("s", n), self.value.at[n], self.bufs.at[n], name)

    def take(self, n):
        self.links.arrived(("s", n), self.bufs.at[n])
        self.value[n + 1] = self.value[n] + self.bufs[n]

    def spread(self):
        for d in (1, 2, 3):
            self.links.start(("s", 2 + d), self.value.at[3], self.bufs.at[2 + d], "z", d)

    def total(self):
        for d in (1, 2, 3):
            self.links.arrived(("s", 2 + d), self.bufs.at[2 + d])
        return self.value[3] + self.bufs[3] + self.bufs[4] + self.bufs[5]


def small_places(dev):
    i = lax.broadcasted_iota(jnp.int32, (1, SMALL_LEN), 1)
    row, col = jnp.full((1, SMALL_LEN), 15, jnp.int32), jnp.full((1, SMALL_LEN), -1, jnp.int32)
    for start, n, base in SMALL:
        here = (i >= start) & (i < start + n)
        row = jnp.where(here, base + (dev * n) // D, row)
        col = jnp.where(here, (dev * n) % D + i - start, col)
    return row, col


def small_select(col):
    return (lax.broadcasted_iota(jnp.int32, (D, SMALL_LEN), 0) == col).astype(F32)


def kernel_prep(small, wqkv, wout, win, wdown, small_o, qkv_o, out_o, in_o, down_o):
    row, col = small_places(lax.axis_index("dp") * 8 + lax.axis_index("fsdp"))
    at_row = lax.broadcasted_iota(jnp.int32, (16, SMALL_LEN), 0) == row
    values = jnp.where(at_row, small[...].astype(BF16).astype(F32), 0.0).astype(BF16)
    small_o[...] = mm_t(values, small_select(col).astype(BF16)).astype(BF16)
    qkv_o[...] = wqkv[...].astype(BF16)
    out_o[...] = wout[...].astype(BF16)
    in_o[...] = win[...].astype(BF16)
    down_o[...] = wdown[...].astype(BF16)


def call_prep(small, weights):
    return pl.pallas_call(
        kernel_prep, name="prep",
        out_shape=[sds((16, D), BF16)] + [sds(w.shape, BF16) for w in weights],
        in_specs=[VMEM] * 5, out_specs=[VMEM] * 5,
    )(small, *weights)


def sum_small(gathered, staged, sem, vecs):
    copy = pltpu.make_async_copy(gathered, staged, sem)
    copy.start()
    copy.wait()
    total = jnp.zeros((16, D), F32)
    for i in range(4):
        for j in range(8):
            total = total + staged[i, j].astype(F32)
    vecs[...] = total


def kernel_gather(small, wqkv, wout, win, wdown, vecs, small_f, qkv_f, out_f, in_f, down_f, staged, sems, send, recv):
    peers = Peers()
    links = Links(peers, send, recv)
    peers.greet()
    g = [Gather(n, links, own, full, sems.at[n])
         for n, (own, full) in enumerate(((small, small_f), (wqkv, qkv_f), (wout, out_f), (win, in_f), (wdown, down_f)))]
    for a in g:
        a.begin()
    for n, a in enumerate(g):
        a.first()
        if n:
            g[n - 1].second()
        if n > 1:
            g[n - 2].third()
    g[4].second()
    g[3].third()
    g[4].third()
    for a in g:
        a.last()
    links.finish()
    sum_small(small_f, staged, sems.at[5], vecs)


def call_gather(own):
    n = len(own)
    return pl.pallas_call(
        kernel_gather, name="gather",
        out_shape=[sds((16, D), F32)] + [sds((4, 8) + a.shape, BF16) for a in own],
        in_specs=[VMEM] * n, out_specs=[VMEM] + [ANY] * n,
        scratch_shapes=[vm((4, 8, 16, D), BF16), pltpu.SemaphoreType.DMA((n + 1,)),
                        pltpu.SemaphoreType.DMA((GATHER_SLOTS * n,)), pltpu.SemaphoreType.DMA((GATHER_SLOTS * n,))],
        compiler_params=pltpu.CompilerParams(vmem_limit_bytes=VMEM_LIMIT, collective_id=1, has_side_effects=True),
    )(*own)


def kernel_scatter(sums_b, sums_c, down, inn, out, qkv, small_o, down_o, in_o, out_o, qkv_o, value, small_b, *rest):
    bufs, (sems, send, recv) = rest[:28], rest[28:]
    peers = Peers()
    links = Links(peers, send, recv)
    pick = lambda ref, n: jnp.sum(ref[n], axis=0, keepdims=True)
    rows = [pick(sums_c, n) for n in range(4)] + [pick(sums_b, n) for n in range(1, 9)] + [jnp.zeros((4, D), F32)]
    value[0] = jnp.concatenate(rows, axis=0)
    peers.greet()
    small = SmallSum(links, value, small_b)
    s = [Scatter(n, links, parts, o, bufs[7 * n : 7 * n + 7], sems.at[n])
         for n, (parts, o) in enumerate(((down, down_o), (inn, in_o), (out, out_o), (qkv, qkv_o)))]
    for a in s:
        a.begin()
    small.send(0, "p")
    s[0].first()
    small.take(0)
    small.send(1, "x")
    s[1].first()
    small.take(1)
    small.send(2, "y")
    s[0].second()
    s[2].first()
    small.take(2)
    small.spread()
    s[0].third()
    s[1].second()
    s[3].first()
    s[1].third()
    s[2].second()
    s[0].last()
    s[3].second()
    s[2].third()
    total = small.total()
    row, col = small_places(peers.dev)
    picked = lax.dot_general(total, small_select(col), (((1,), (0,)), ((), ())),
                             precision=lax.Precision.HIGHEST, preferred_element_type=F32)
    at_row = lax.broadcasted_iota(jnp.int32, (16, SMALL_LEN), 0) == row
    small_o[...] = jnp.sum(jnp.where(at_row, picked, 0.0), axis=0, keepdims=True)
    s[1].last()
    s[3].third()
    s[2].last()
    s[3].last()
    links.finish()


def call_scatter(sums_b, sums_c, parts):
    shapes = [(p.shape[0] // 32, p.shape[1]) for p in parts]
    parts = [p.reshape(4, 4, 2, r, p.shape[1]) for p, (r, _) in zip(parts, shapes)]
    bufs = [b for s in shapes for b in scatter_bufs(*s)]
    slots = SCATTER_SLOTS * len(parts) + 6
    return pl.pallas_call(
        kernel_scatter, name="scatter",
        out_shape=[sds((1, SMALL_LEN), F32)] + [sds(s, F32) for s in shapes],
        in_specs=[VMEM, VMEM] + [ANY] * 4, out_specs=[VMEM] * 5,
        scratch_shapes=[vm((4, 16, D), F32), vm((6, 16, D), F32)] + bufs
        + [pltpu.SemaphoreType.DMA((4,)), pltpu.SemaphoreType.DMA((slots,)), pltpu.SemaphoreType.DMA((slots,))],
        compiler_params=pltpu.CompilerParams(vmem_limit_bytes=VMEM_LIMIT, collective_id=2, has_side_effects=True),
    )(sums_b, sums_c, *parts)


def gather_all(a):
    return lax.all_gather(a.astype(BF16), AXES, axis=0, tiled=True)


def scatter_sum(a):
    return lax.psum_scatter(a, AXES, scatter_dimension=0, tiled=True)


def split_small(row, small):
    parts, at = [], 0
    for s in small:
        parts.append(row[at : at + s.shape[0]])
        at += s.shape[0]
    return parts


def gather_plain(small, weights):
    every = lax.all_gather(jnp.concatenate([s.astype(BF16) for s in small]), AXES, axis=0, tiled=False)
    vecs, at = [], 0
    for s in small:
        vecs.append(every[:, at : at + s.shape[0]].reshape(-1, D))
        at += s.shape[0]
    vecs = jnp.concatenate(vecs + [jnp.zeros((4, D), BF16)], axis=0).astype(F32)
    return vecs, [gather_all(w) for w in weights]


def scatter_plain(sums_b, sums_c, grads, small):
    sb, sc = jnp.sum(sums_b, axis=1), jnp.sum(sums_c, axis=1)
    vectors = (sc[0], sc[1], sc[2:4].reshape(-1), sb[1], sb[2], sb[3], sb[4:8].reshape(-1), sb[8])
    devices = D // small[0].shape[0]
    packed = jnp.concatenate([g.reshape(devices, -1) for g in vectors], axis=1)
    return scatter_sum(packed).reshape(-1), [scatter_sum(g.astype(F32)) for g in grads]


def local(
    own_links,
    hidden_in, time_embed, seg_ids, pre_gain, pre_shift, qkv_weight, qv_bias, out_weight, out_bias,
    mid_gain, mid_shift, in_weight, in_bias, down_weight, down_bias, grad_out,
):
    sid = seg_ids.reshape(GROUPS, SHORT)[:, 0]
    small = (pre_gain, pre_shift, qv_bias, out_bias, mid_gain, mid_shift, in_bias, down_bias)
    weights = (qkv_weight, out_weight, in_weight, down_weight)
    if own_links:
        row = jnp.concatenate(small + (jnp.zeros((SMALL_LEN - 288,), F32),)).reshape(1, SMALL_LEN)
        vecs, _, *full = call_gather(call_prep(row, weights))
        wqkv, wout, win, wdown = [a.reshape(-1, a.shape[-1]) for a in full]
    else:
        vecs, (wqkv, wout, win, wdown) = gather_plain(small, weights)
    x, a1t, q0, q1, k0, k1, v, kt, o, ot, lse = call_a(sid, hidden_in, time_embed, vecs, wqkv)
    block_out, gx1, gb, go0, go1, dots, gdown, gin, sums_b = call_b(sid, x, o, grad_out, vecs, wout, win, wdown)
    input_grad, time_grad, gqkv, gout, sums_c = call_c(
        sid, x, a1t, q0, q1, k0, k1, v, kt, ot, lse, gx1, gb, go0, go1, dots, vecs, wqkv)
    if own_links:
        mine, gdown, gin, gout, gqkv = call_scatter(sums_b, sums_c, (gdown, gin, gout, gqkv))
        mine = mine.reshape(-1)
    else:
        mine, (gdown, gin, gout, gqkv) = scatter_plain(sums_b, sums_c, (gdown, gin, gout, gqkv), small)
    gpg, gps, gqvb, gob, gmg, gms, gib, gdb = split_small(mine, small)
    return (block_out, input_grad, time_grad, gpg, gps, gqkv, gqvb, gout, gob, gmg, gms, gin, gib, gdown, gdb)


def solution(mesh):
    rows, flat = P(AXES, None), P(AXES)
    own_links = dict(mesh.shape) == {"dp": 4, "fsdp": 8}
    return jax.shard_map(
        functools.partial(local, own_links),
        mesh=mesh,
        in_specs=(rows, rows, flat, flat, flat, rows, flat, rows, flat, flat, flat, rows, flat, rows, flat, rows),
        out_specs=(rows, rows, rows, flat, flat, rows, flat, rows, flat, flat, flat, rows, flat, rows, flat),
        check_vma=False,
    )
```

time: 928 us -> 360 us (0.39)
  Pallas kernels: 0 us -> 346 us
  waiting for transfers between devices: 328 us -> 0 us
  matrix products: 301 us -> 0 us
  other arithmetic: 110 us -> 0 us
  blocking collectives: 84.3 us -> 0 us
  local copies, waits for them, and re-layouts: 78.8 us -> 13.3 us
  between operations: 15.2 us -> 0.7 us
    pallas_call x0 -> x6, Pallas kernels: none -> 346 us  [the longest x1 84.9 us: call_scatter(): pl.pallas_call(kernel_scatter, name='scatter', out_shape=[sds((1, SMALL_L...]
    dot_general x28 -> x0, matrix products: 301 us -> none  [the longest x4 44.5 us: masked_scores(): jnp.einsum('qhd,khd->hqk', q_part, k, preferred_element_type=jnp.float32)]
    reduce_scatter x4 -> x0, waiting for transfers between devices: 288 us -> none  [the longest x1 142 us: local(): lax.psum_scatter(grad_down, ('dp', 'fsdp'), scatter_dimension=0, tiled=True)]
    unnamed x2 -> x0, blocking collectives: 84.3 us -> none
    convert_element_type x22 -> x0, other arithmetic: 57.9 us -> none  [the longest x2 43.2 us: backward_block(): grad_scores = (p * (grad_p - row_dot)).astype(jnp.bfloat16)]
    reduce_sum x12 -> x0, other arithmetic: 43 us -> none  [the longest x2 24.9 us: forward_block(): row_total = jnp.sum(exp_terms, axis=-1, keepdims=True)]
    all_gather x4 -> x0, waiting for transfers between devices: 40.8 us -> none  [the longest x1 27.2 us: local(): lax.all_gather(down_weight.astype(jnp.bfloat16), ('dp', 'fsdp'), axis=0,...]
    unnamed x135 -> x4, local copies, waits for them, and re-layouts: 33.3 us -> 6.54 us
  transfers between devices with their start and end apart: 8 -> 0, of which waited for: 5 -> 0; matrix products, arithmetic and copies ran while one was open for 45% -> 0% of each run, Pallas kernels for 0% -> 0%
where the time goes in v1:
time: 360 us
  Pallas kernels  346 us (96%)
  local copies, waits for them, and re-layouts  13.3 us (4%)
    pallas_call x1, Pallas kernels, call_scatter(): pl.pallas_call(kernel_scatter, name='scatter', out_shape=[sds((1, SMALL_L...  84.9 us
    pallas_call x1, Pallas kernels, call_gather(): pl.pallas_call(kernel_gather, name='gather', out_shape=[sds((16, D), F32)...  80.8 us
    pallas_call x1, Pallas kernels, call_c(): pl.pallas_call(kernel_c, name='part_c', out_shape=out, in_specs=[SMEM] +...  63.4 us
    pallas_call x1, Pallas kernels, call_b(): pl.pallas_call(kernel_b, name='part_b', out_shape=out, in_specs=[SMEM, AN...  62.1 us
    pallas_call x1, Pallas kernels, call_a(): pl.pallas_call(kernel_a, name='part_a', out_shape=out, in_specs=[SMEM, AN...  52.4 us

profile of v1, /device:TPU:0, one launch (start us, length us, event | category | flops | bytes accessed | tf_op | source)
XLA Modules:
  0.0 359.8 jit_solution(18023268531844530434)
XLA Ops:
  0.7 0.8 concatenate.3
  1.5 0.6 reshape.70.small
  2.1 0.8 reshape.69
  2.8 0.6 slice_reduce_fusion.sid
  3.5 2.2 prep.1
  5.6 80.8 %gather.1 = (f32[16,768]{1,0:T(8,128)}, bf16[4,8,16,768]{3,2,1,0:T(8,128)(2,1)}, bf16[4,8,24,2304]{3,2,1,0:T(8,128)(2,1)}, bf16[4,8,24,768]{3,2,1,0:T(8,128)(2,1...) custom-call(bf16[16,768]{1,0:T(8,128)(2,1)} %get-tuple-element.55.small, ...), custom_call_target="tpu_custom_call" | custom-call | tf_op jit(solution)/shard_map/gather/pallas_call | solution.py:752
  86.4 52.4 %part_a.1 = (f32[1024,768]{1,0:T(8,128)}, bf16[768,1024]{1,0:T(8,128)(2,1)}, bf16[1024,768]{1,0:T(8,128)(2,1)}, bf16[1024,768]{1,0:T(8,128)(2,1)}, bf16[1024,768...) custom-call(s32[16]{0:T(128)} %slice_reduce_fusion.sid, ...), custom_call_target="tpu_custom_call" | custom-call | tf_op jit(solution)/shard_map/part_a/pallas_call | solution.py:237
  138.9 62.1 %part_b.1 = (f32[1024,768]{1,0:T(8,128)}, f32[1024,768]{1,0:T(8,128)}, bf16[1024,768]{1,0:T(8,128)(2,1)}, bf16[1024,768]{1,0:T(8,128)(2,1)}, bf16[1024,768]{1,0:...) custom-call(s32[16]{0:T(128)} %slice_reduce_fusion.sid, ...), custom_call_target="tpu_custom_call" | custom-call | tf_op jit(solution)/shard_map/part_b/pallas_call | solution.py:350
  201.0 63.4 %part_c.1 = (f32[1024,768]{1,0:T(8,128)}, f32[16,768]{1,0:T(8,128)}, bf16[768,2304]{1,0:T(8,128)(2,1)}, bf16[768,768]{1,0:T(8,128)(2,1)}, f32[4,8,768]{2,1,0:T(8,128)}) custom-call(s32[16]{0:T(128)} %slice_reduce_fusion.sid, f32[1024,768]{1,0:T(8,128)} %get-tuple-element.62.x_h, bf16[768,1024]{1,0:T(8,128)(2,1)} %get-tuple-element.68.a1t_h, ...), custom_call_target="tpu_custom_call" | custom-call | tf_op jit(solution)/shard_map/part_c/pallas_call | solution.py:453
  264.4 84.9 %scatter.1 = (f32[1,384]{1,0:T(1,128)}, f32[96,768]{1,0:T(8,128)}, f32[24,3072]{1,0:T(8,128)}, f32[24,768]{1,0:T(8,128)}, f32[24,2304]{1,0:T(8,128)}) custom-call(f32[9,8,768]{2,1,0:T(8,128)} %get-tuple-element.84.sums_b, f32[4,8,768]{2,1,0:T(8,128)} %get-tuple-element.85.sums_c, bf16[4,4,2,96,768]{4,3,2,1,0:T(8,128)(2,1)} %bitcast.28, ...), custom_call_target="tpu_custom_call" | custom-call | tf_op jit(solution)/shard_map/scatter/pallas_call | solution.py:812
  349.3 1.3 slice_bitcast_fusion.5
  350.6 1.2 slice_bitcast_fusion.1
  351.8 1.4 slice_bitcast_fusion
  353.3 1.6 copy.35
  354.9 1.5 copy.36
  356.4 1.7 copy.37
  358.1 1.7 copy.38
  (1 shorter events, 0.0 us)

commit v2 on v1

--- a/solution.py
+++ b/solution.py
@@ -89,7 +89,12 @@
         return copy
 
 
-def stage_norm1(sid, time, vecs, x, a1, a1t):
+def run_hooks(step, hooks):
+    for n, action in hooks.items():
+        pl.when(step == n)(action)
+
+
+def stage_norm1(sid, time, vecs, x, a1, a1t, hooks):
     gain, shift = vecs[0:1, :], vecs[1:2, :]
 
     @pl.loop(0, BLOCK // 128)
@@ -107,6 +112,7 @@
         a = n * gain + shift
         a1[at, :] = a.astype(BF16)
         a1t[:, at] = a.T.astype(BF16)
+        run_hooks(i, hooks)
 
 
 def mask_rows(sid, i, groups):
@@ -193,31 +199,74 @@
     lse[pl.ds(2 * pair + 1, 1), at] = logs[1]
 
 
-def kernel_a(sid, hidden, time, vecs, wqkv, x_h, a1t_h, q0_h, q1_h, k0_h, k1_h, v_h, kt_h, o_h, ot_h, lse,
-             x, a1, a1t, q0, q1, k0, k1, v, kt, vt0, vt1, o, ot, w, sems):
+def kernel_a(linked, sid, hidden, time, *refs):
+    if linked:
+        own, refs = refs[:5], refs[5:]
+        vecs, refs = refs[0], refs[1:]
+    else:
+        (vecs, wqkv), refs = refs[:2], refs[2:]
+    (x_h, a1t_h, q0_h, q1_h, k0_h, k1_h, v_h, kt_h, o_h, ot_h, lse), refs = refs[:11], refs[11:]
+    if linked:
+        full, refs = refs[:5], refs[5:]
+        wqkv = full[1]
+    (x, a1, a1t, q0, q1, k0, k1, v, kt, vt0, vt1, o, ot, w, sems), refs = refs[:15], refs[15:]
     mv = Mover(sems)
     cx = mv.start(hidden, x)
-    cw = [mv.start(wqkv.at[:, pl.ds(D * j, D)], w.at[j]) for j in range(3)]
+    norm_hooks, attention_hooks, after = {}, {}, [[], [], [], []]
+    if linked:
+        staged, local_sems, send, recv = refs
+        peers = Peers()
+        links = Links(peers, send, recv)
+        peers.greet()
+        small, qkv, out, inn, down = [Gather(n, links, own[n], full[n], local_sems.at[n]) for n in range(5)]
+        for a in (small, qkv, out, inn, down):
+            a.begin()
+        small.first()
+        qkv.first()
+        small.second()
+        small.third()
+        out.first((0,))
+        small.last()
+        sum_small(full[0], staged, local_sems.at[5], vecs)
+        norm_hooks = {1: qkv.second, 3: out.first_rest, 5: qkv.third, 6: inn.first_own}
+        after = [[out.second, inn.first_rest], [out.third, down.first_own], [inn.second, down.first_rest], []]
+        attention_hooks = {4: inn.third, 9: down.second, 17: down.third}
     cx.wait()
-    stage_norm1(sid, time, vecs, x, a1, a1t)
+    stage_norm1(sid, time, vecs, x, a1, a1t, norm_hooks)
     outs = [mv.start(x, x_h), mv.start(a1t, a1t_h)]
-    cw[0].wait()
-    stage_q(sid, vecs, a1, w[0], q0, q1)
+    if linked:
+        qkv.last()
+    cw = [mv.start(wqkv.at[:, :, pl.ds(D * j, D)], w.at[j]) for j in range(3)]
+
+    def weight(j):
+        cw[j].wait()
+        return w[j].reshape(D, D)
+
+    stage_q(sid, vecs, a1, weight(0), q0, q1)
+    for action in after[0]:
+        action()
     outs += [mv.start(q0, q0_h), mv.start(q1, q1_h)]
-    cw[1].wait()
-    stage_k(sid, a1, w[1], k0, k1, kt)
+    stage_k(sid, a1, weight(1), k0, k1, kt)
+    for action in after[1]:
+        action()
     outs += [mv.start(k0, k0_h), mv.start(k1, k1_h), mv.start(kt, kt_h)]
-    cw[2].wait()
-    stage_v(vecs, a1, w[2], v, vt0, vt1)
+    stage_v(vecs, a1, weight(2), v, vt0, vt1)
+    for action in after[2]:
+        action()
     outs += [mv.start(v, v_h)]
 
     @pl.loop(0, PAIRS * (BLOCK // QB))
     def _(step):
         attention_step(step, q0, q1, k0, k1, vt0, vt1, o, ot, lse)
+        run_hooks(step, attention_hooks)
 
     outs += [mv.start(o, o_h), mv.start(ot, ot_h)]
-    for c in outs:
-        c.wait()
+    for copy in outs:
+        copy.wait()
+    if linked:
+        for a in (out, inn, down):
+            a.last()
+        links.finish()
 
 
 def sds(shape, dtype):
@@ -232,18 +281,35 @@
     return pltpu.VMEM(shape, dtype)
 
 
+OUT_A = [sds(TOK, F32), sds(TOKT, BF16)] + [sds(TOK, BF16)] * 5 + [sds(TOKT, BF16), sds(TOK, BF16), sds(TOKT, BF16), sds((16, BLOCK), F32)]
+SCRATCH_A = [vm(TOK, F32), vm(TOK, BF16), vm(TOKT, BF16)] + [vm(TOK, BF16)] * 5 + [vm(TOKT, BF16)] * 3 + [
+    vm(TOK, BF16), vm(TOKT, BF16), vm((3, 4, D // 4, D), BF16), pltpu.SemaphoreType.DMA((16,))]
+
+
 def call_a(sid, hidden, time, vecs, wqkv):
-    out = [sds(TOK, F32), sds(TOKT, BF16)] + [sds(TOK, BF16)] * 5 + [sds(TOKT, BF16), sds(TOK, BF16), sds(TOKT, BF16), sds((16, BLOCK), F32)]
     return pl.pallas_call(
-        kernel_a,
+        functools.partial(kernel_a, False),
         name="part_a",
-        out_shape=out,
+        out_shape=OUT_A,
         in_specs=[SMEM, ANY, VMEM, VMEM, ANY],
         out_specs=[ANY] * 10 + [VMEM],
-        scratch_shapes=[vm(TOK, F32), vm(TOK, BF16), vm(TOKT, BF16)] + [vm(TOK, BF16)] * 5 + [vm(TOKT, BF16)] * 3
-        + [vm(TOK, BF16), vm(TOKT, BF16), vm((3, D, D), BF16), pltpu.SemaphoreType.DMA((16,))],
+        scratch_shapes=SCRATCH_A,
         compiler_params=pltpu.CompilerParams(vmem_limit_bytes=VMEM_LIMIT),
-    )(sid, hidden, time, vecs, wqkv)
+    )(sid, hidden, time, vecs, wqkv.reshape(4, D // 4, 3 * D))
+
+
+def call_a_links(sid, hidden, time, own):
+    res = pl.pallas_call(
+        functools.partial(kernel_a, True),
+        name="part_a",
+        out_shape=[sds((16, D), F32)] + OUT_A + [sds((4, 8 * a.shape[0], a.shape[1]), BF16) for a in own],
+        in_specs=[SMEM, ANY, VMEM] + [VMEM] * 5,
+        out_specs=[VMEM] + [ANY] * 10 + [VMEM] + [ANY] * 5,
+        scratch_shapes=SCRATCH_A + [vm((4, 128, D), BF16), pltpu.SemaphoreType.DMA((6,)),
+                                    pltpu.SemaphoreType.DMA((GATHER_SLOTS * 5,)), pltpu.SemaphoreType.DMA((GATHER_SLOTS * 5,))],
+        compiler_params=pltpu.CompilerParams(vmem_limit_bytes=VMEM_LIMIT, collective_id=1, has_side_effects=True),
+    )(sid, hidden, time, *own)
+    return res[0], res[1:12], [a.reshape(-1, a.shape[-1]) for a in res[13:]]
 
 
 def kernel_b(sid, x_h, o_h, gout_h, vecs, wout_h, win_h, wdown_h,
@@ -388,9 +454,24 @@
         gqkv[2, :, lanes] = gv_acc[...].astype(BF16)
 
 
-def kernel_c(sid, x_h, a1t_h, q0_h, q1_h, k0_h, k1_h, v_h, kt_h, ot_h, lse, gx1_h, gb_h, go0_h, go1_h, dots, vecs, wqkv_h,
-             ig_h, tg, gqkvw_h, goutw_h, sums,
-             x, a1t, q0, q1, k0, k1, v, kt, ot, gx1, gb, go0, go1, w, gqkv, gk_acc, gv_acc, gw, gwo, tsum, sems):
+def kernel_c(linked, sid, x_h, a1t_h, q0_h, q1_h, k0_h, k1_h, v_h, kt_h, ot_h, lse, gx1_h, gb_h, go0_h, go1_h, dots, vecs, wqkv_h, *refs):
+    if linked:
+        parts, refs = refs[:2], refs[2:]
+    (ig_h, tg, gqkvw_h, goutw_h, sums), refs = refs[:5], refs[5:]
+    if linked:
+        owns, refs = refs[:2], refs[2:]
+    (x, a1t, q0, q1, k0, k1, v, kt, ot, gx1, gb, go0, go1, w, gqkv, gk_acc, gv_acc, gw, gwo, tsum, sems), refs = refs[:21], refs[21:]
+    hooks, rest = {}, []
+    if linked:
+        bufs, (local_sems, send, recv) = refs[:14], refs[14:]
+        peers = Peers()
+        links = Links(peers, send, recv)
+        peers.greet()
+        down, inn = [Scatter(n, links, parts[n], owns[n], bufs[7 * n : 7 * n + 7], local_sems.at[n]) for n in range(2)]
+        down.begin()
+        inn.begin()
+        hooks = {0: down.first, 2: inn.first, 5: down.second, 9: inn.second, 13: down.third, 17: inn.third}
+        rest = [down.last, inn.last, links.finish]
     mv = Mover(sems)
     early = [mv.start(s, d) for s, d in ((ot_h, ot), (gb_h, gb), (q0_h, q0), (q1_h, q1), (k0_h, k0), (k1_h, k1), (v_h, v), (kt_h, kt), (go0_h, go0), (go1_h, go1))]
     late = [mv.start(a1t_h, a1t), mv.start(x_h, x), mv.start(gx1_h, gx1)]
@@ -410,6 +491,7 @@
     @pl.loop(0, PAIRS * (BLOCK // QB))
     def _(step):
         attention_back_step(step, q0, q1, k0, k1, v, kt, go0, go1, lse, dots, gk_acc, gv_acc, gqkv)
+        run_hooks(step, hooks)
 
     for c in late:
         c.wait()
@@ -444,23 +526,39 @@
     for g in range(GROUPS):
         acc = acc + jnp.where(row == sid[g], tsum[g : g + 1, :], 0.0)
     tg[...] = acc
+    for action in rest:
+        action()
     for c in outs:
         c.wait()
 
 
-def call_c(sid, x, a1t, q0, q1, k0, k1, v, kt, ot, lse, gx1, gb, go0, go1, dots, vecs, wqkv):
+def call_c(linked, *args):
     out = [sds(TOK, F32), sds((GROUPS, D), F32), sds((D, 3 * D), BF16), sds((D, D), BF16), sds((4, 8, D), F32)]
+    in_specs = [SMEM] + [ANY] * 9 + [VMEM] + [ANY] * 4 + [VMEM, VMEM, ANY]
+    out_specs = [ANY, VMEM, ANY, ANY, VMEM]
+    scratch = [vm(TOK, F32), vm(TOKT, BF16)] + [vm(TOK, BF16)] * 5 + [vm(TOKT, BF16)] * 2 + [vm(TOK, F32)] + [vm(TOK, BF16)] * 3
+    scratch += [vm((3, D, D), BF16), vm((3, BLOCK, D), BF16), vm((BLOCK, 128), F32), vm((BLOCK, 128), F32), vm((3, D, D), BF16), vm((D, D), BF16),
+                vm((GROUPS, D), F32), pltpu.SemaphoreType.DMA((24,))]
+    extra = {}
+    if linked:
+        args, parts = args[:-2], args[-2:]
+        shapes = [(p.shape[0] // 32, p.shape[1]) for p in parts]
+        args = args + tuple(p.reshape(4, 4, 2, r, p.shape[1]) for p, (r, _) in zip(parts, shapes))
+        in_specs += [ANY] * 2
+        out += [sds(s, F32) for s in shapes]
+        out_specs += [VMEM] * 2
+        scratch += [b for s in shapes for b in scatter_bufs(*s)]
+        scratch += [pltpu.SemaphoreType.DMA((n,)) for n in (2, 2 * SCATTER_SLOTS, 2 * SCATTER_SLOTS)]
+        extra = dict(collective_id=3, has_side_effects=True)
     return pl.pallas_call(
-        kernel_c,
+        functools.partial(kernel_c, linked),
         name="part_c",
         out_shape=out,
-        in_specs=[SMEM] + [ANY] * 9 + [VMEM] + [ANY] * 4 + [VMEM, VMEM, ANY],
-        out_specs=[ANY, VMEM, ANY, ANY, VMEM],
-        scratch_shapes=[vm(TOK, F32), vm(TOKT, BF16)] + [vm(TOK, BF16)] * 5 + [vm(TOKT, BF16)] * 2 + [vm(TOK, F32)] + [vm(TOK, BF16)] * 3
-        + [vm((3, D, D), BF16), vm((3, BLOCK, D), BF16), vm((BLOCK, 128), F32), vm((BLOCK, 128), F32), vm((3, D, D), BF16), vm((D, D), BF16),
-           vm((GROUPS, D), F32), pltpu.SemaphoreType.DMA((24,))],
-        compiler_params=pltpu.CompilerParams(vmem_limit_bytes=VMEM_LIMIT),
-    )(sid, x, a1t, q0, q1, k0, k1, v, kt, ot, lse, gx1, gb, go0, go1, dots, vecs, wqkv)
+        in_specs=in_specs,
+        out_specs=out_specs,
+        scratch_shapes=scratch,
+        compiler_params=pltpu.CompilerParams(vmem_limit_bytes=VMEM_LIMIT, **extra),
+    )(*args)
 
 
 AXES = ("dp", "fsdp")
@@ -480,9 +578,11 @@
         self.fd = self.fx + 4 - 8 * y
         self.qx, self.qy, self.qd = self.fx // 2, self.fy // 2, self.fd // 2
         self.dev = self.z * 8 + self.f
+        self.other = 1 - self.c
+        self.ups = [(self.z + d) % 4 for d in range(4)]
 
     def up(self, d):
-        return (self.z + d) % 4
+        return self.ups[d]
 
     def at(self, name, d=0):
         if name == "z":
@@ -496,31 +596,36 @@
         pl.semaphore_wait(barrier, 6)
 
 
+class View:
+    def __init__(self, ref, *index):
+        self.ref, self.index = ref, index
+
+    def get(self):
+        return self.ref.at[self.index] if self.index else self.ref
+
+
 class Links:
     def __init__(self, peers, send, recv):
         self.peers, self.send, self.recv = peers, send, recv
         self.slots, self.sent = {}, []
 
-    def slot(self, key):
-        return self.slots.setdefault(key, len(self.slots))
+    def copy(self, key, src, dst, target):
+        n = self.slots.setdefault(key, len(self.slots))
+        return pltpu.make_async_remote_copy(
+            src_ref=src.get(), dst_ref=dst.get(), send_sem=self.send.at[n], recv_sem=self.recv.at[n],
+            device_id=target, device_id_type=MESH)
 
     def start(self, key, src, dst, name, d=0):
-        n = self.slot(key)
-        copy = pltpu.make_async_remote_copy(
-            src_ref=src, dst_ref=dst, send_sem=self.send.at[n], recv_sem=self.recv.at[n],
-            device_id=self.peers.at(name, d), device_id_type=MESH)
-        copy.start()
-        self.sent.append(copy)
+        args = (key, src, dst, self.peers.at(name, d))
+        self.copy(*args).start()
+        self.sent.append(args)
 
     def arrived(self, key, dst):
-        n = self.slot(key)
-        pltpu.make_async_remote_copy(
-            src_ref=dst, dst_ref=dst, send_sem=self.send.at[n], recv_sem=self.recv.at[n],
-            device_id=self.peers.at("p"), device_id_type=MESH).wait_recv()
+        self.copy(key, dst, dst, self.peers.at("p")).wait_recv()
 
     def finish(self):
-        for copy in self.sent:
-            copy.wait_send()
+        for args in self.sent:
+            self.copy(*args).wait_send()
         self.sent = []
 
 
@@ -529,61 +634,73 @@
 
 class Gather:
     def __init__(self, name, links, own, full, sem):
-        self.name, self.links, self.own, self.full, self.sem = name, links, own, full, sem
+        self.name, self.links, self.own, self.full, self.sem = name, links, View(own), full, sem
+        p, self.rows = links.peers, own.shape[0]
+        self.at = {n: pl.multiple_of(f * self.rows, 8) for n, f in (("f", p.f), ("x", p.fx), ("y", p.fy), ("d", p.fd))}
+        self.across = {n: pl.multiple_of((f + 1 - 2 * p.c) * self.rows, 8)
+                       for n, f in (("f", p.f), ("x", p.fx), ("y", p.fy), ("d", p.fd))}
 
     def key(self, *k):
         return (self.name,) + k
 
-    def piece(self, d, f):
-        return self.full.at[(self.links.peers.z + 4 - d) % 4, f]
+    def piece(self, d, n):
+        return View(self.full, self.links.peers.up((4 - d) % 4), pl.ds(self.at[n], self.rows))
+
+    def column(self, at):
+        return View(self.full, slice(None), pl.ds(at, self.rows))
 
     def begin(self):
-        p = self.links.peers
-        here = self.full.at[p.z, p.f]
+        here = self.piece(0, "f")
         for d in (1, 3, 2):
             self.links.start(self.key("z", d), self.own, here, "z", d)
-        self.local = pltpu.make_async_copy(self.own, here, self.sem)
-        self.local.start()
-
-    def first(self):
-        p, links = self.links.peers, self.links
-        for d in (0, 1, 3, 2):
-            piece = self.piece(d, p.f)
+        self.local_copy().start()
+
+    def local_copy(self):
+        return pltpu.make_async_copy(self.own.get(), self.piece(0, "f").get(), self.sem)
+
+    def first(self, ds=(0, 1, 3, 2)):
+        links = self.links
+        for d in ds:
+            piece = self.piece(d, "f")
             if d:
                 links.arrived(self.key("z", d), piece)
             src = piece if d else self.own
             links.start(self.key("x", d), src, piece, "x")
             links.start(self.key("y", d), src, piece, "y")
-        self.local.wait()
-        mine = self.full.at[:, p.f]
-        links.start(self.key("p", 0), mine, mine, "p")
+        if 2 in ds:
+            self.local_copy().wait()
+            mine = self.column(self.at["f"])
+            links.start(self.key("p", "f"), mine, mine, "p")
+
+    def first_own(self):
+        self.first((0,))
+
+    def first_rest(self):
+        self.first((1, 3, 2))
 
     def second(self):
-        p, links = self.links.peers, self.links
+        links = self.links
         for d in (0, 1, 3, 2):
-            px, py = self.piece(d, p.fx), self.piece(d, p.fy)
+            px, py = self.piece(d, "x"), self.piece(d, "y")
             links.arrived(self.key("x", d), px)
             links.arrived(self.key("y", d), py)
             if d < 2:
                 links.start(self.key("d", d), px, px, "y")
             else:
                 links.start(self.key("d", d), py, py, "x")
-        for n, f in ((1, p.fx), (2, p.fy)):
-            part = self.full.at[:, f]
+        for n in ("x", "y"):
+            part = self.column(self.at[n])
             links.start(self.key("p", n), part, part, "p")
 
     def third(self):
-        p, links = self.links.peers, self.links
         for d in range(4):
-            links.arrived(self.key("d", d), self.piece(d, p.fd))
-        part = self.full.at[:, p.fd]
-        links.start(self.key("p", 3), part, part, "p")
+            self.links.arrived(self.key("d", d), self.piece(d, "d"))
+        part = self.column(self.at["d"])
+        self.links.start(self.key("p", "d"), part, part, "p")
 
     def last(self):
-        p, links = self.links.peers, self.links
-        for n, f in enumerate((p.f, p.fx, p.fy, p.fd)):
-            other = f + 1 - 2 * p.c
-            links.arrived(self.key("p", n), self.full.at[:, other])
+        for n in ("f", "x", "y", "d"):
+            self.links.arrived(self.key("p", n), self.column(self.across[n]))
 
 
 SCATTER_SLOTS = 10
@@ -599,9 +716,11 @@
 
     def begin(self):
         p = self.links.peers
-        self.links.start(self.key("p"), self.parts.at[:, :, 1 - p.c], self.p, "p")
-        self.local = pltpu.make_async_copy(self.parts.at[:, :, p.c], self.t, self.sem)
-        self.local.start()
+        self.links.start(self.key("p"), View(self.parts, slice(None), slice(None), p.other), View(self.p), "p")
+        self.local_copy().start()
+
+    def local_copy(self):
+        return pltpu.make_async_copy(self.parts.at[:, :, self.links.peers.c], self.t, self.sem)
 
     def add(self, q, zs, ref, base=0):
         t = self.t
@@ -612,43 +731,43 @@
 
     def first(self):
         p, links, t = self.links.peers, self.links, self.t
-        self.local.wait()
-        links.arrived(self.key("p"), self.p)
+        self.local_copy().wait()
+        links.arrived(self.key("p"), View(self.p))
         self.add(p.qd, (0, 4), lambda i: self.p[i, p.qd])
-        links.start(self.key("dx"), t.at[pl.ds(0, 2), p.qd], self.dx, "x")
-        links.start(self.key("dy"), t.at[pl.ds(2, 2), p.qd], self.dy, "y")
+        links.start(self.key("dx"), View(t, pl.ds(0, 2), p.qd), View(self.dx), "x")
+        links.start(self.key("dy"), View(t, pl.ds(2, 2), p.qd), View(self.dy), "y")
         self.add(p.qx, (0, 4), lambda i: self.p[i, p.qx])
-        links.start(self.key("x", 0), t.at[pl.ds(0, 2), p.qx], self.xr.at[pl.ds(0, 2)], "x")
+        links.start(self.key("x", 0), View(t, pl.ds(0, 2), p.qx), View(self.xr, pl.ds(0, 2)), "x")
         self.add(p.qy, (0, 4), lambda i: self.p[i, p.qy])
-        links.start(self.key("y", 1), t.at[pl.ds(2, 2), p.qy], self.yr.at[pl.ds(2, 2)], "y")
+        links.start(self.key("y", 1), View(t, pl.ds(2, 2), p.qy), View(self.yr, pl.ds(2, 2)), "y")
         self.add(p.yx, (0, 4), lambda i: self.p[i, p.yx])
 
     def second(self):
         p, links, t = self.links.peers, self.links, self.t
-        links.arrived(self.key("dy"), self.dy)
+        links.arrived(self.key("dy"), View(self.dy))
         self.add(p.qx, (2, 4), lambda i: self.dy[i], 2)
-        links.start(self.key("x", 1), t.at[pl.ds(2, 2), p.qx], self.xr.at[pl.ds(2, 2)], "x")
-        links.arrived(self.key("dx"), self.dx)
+        links.start(self.key("x", 1), View(t, pl.ds(2, 2), p.qx), View(self.xr, pl.ds(2, 2)), "x")
+        links.arrived(self.key("dx"), View(self.dx))
         self.add(p.qy, (0, 2), lambda i: self.dx[i])
-        links.start(self.key("y", 0), t.at[pl.ds(0, 2), p.qy], self.yr.at[pl.ds(0, 2)], "y")
+        links.start(self.key("y", 0), View(t, pl.ds(0, 2), p.qy), View(self.yr, pl.ds(0, 2)), "y")
 
     def third(self):
         p, links, t = self.links.peers, self.links, self.t
         for n in range(2):
-            links.arrived(self.key("x", n), self.xr.at[pl.ds(2 * n, 2)])
-            links.arrived(self.key("y", n), self.yr.at[pl.ds(2 * n, 2)])
+            links.arrived(self.key("x", n), View(self.xr, pl.ds(2 * n, 2)))
+            links.arrived(self.key("y", n), View(self.yr, pl.ds(2 * n, 2)))
 
         @pl.loop(0, 4)
         def _(i):
             t[i, p.yx] = (t[i, p.yx].astype(F32) + self.xr[i].astype(F32) + self.yr[i].astype(F32)).astype(BF16)
 
         for d in (2, 1, 3):
-            links.start(self.key("z", d), t.at[p.up(d), p.yx], self.zr.at[d - 1], "z", d)
+            links.start(self.key("z", d), View(t, p.up(d), p.yx), View(self.zr, d - 1), "z", d)
 
     def last(self):
         p, links = self.links.peers, self.links
         for d in (1, 2, 3):
-            links.arrived(self.key("z", d), self.zr.at[d - 1])
+            links.arrived(self.key("z", d), View(self.zr, d - 1))
         total = self.t[p.z, p.yx].astype(F32)
         for n in range(3):
             total = total + self.zr[n].astype(F32)
@@ -664,19 +783,19 @@
         self.links, self.value, self.bufs = links, value, bufs
 
     def send(self, n, name):
-        self.links.start(("s", n), self.value.at[n], self.bufs.at[n], name)
+        self.links.start(("s", n), View(self.value, n), View(self.bufs, n), name)
 
     def take(self, n):
-        self.links.arrived(("s", n), self.bufs.at[n])
+        self.links.arrived(("s", n), View(self.bufs, n))
         self.value[n + 1] = self.value[n] + self.bufs[n]
 
     def spread(self):
         for d in (1, 2, 3):
-            self.links.start(("s", 2 + d), self.value.at[3], self.bufs.at[2 + d], "z", d)
+            self.links.start(("s", 2 + d), View(self.value, 3), View(self.bufs, 2 + d), "z", d)
 
     def total(self):
         for d in (1, 2, 3):
-            self.links.arrived(("s", 2 + d), self.bufs.at[2 + d])
+            self.links.arrived(("s", 2 + d), View(self.bufs, 2 + d))
         return self.value[3] + self.bufs[3] + self.bufs[4] + self.bufs[5]
 
 
@@ -720,47 +839,12 @@
     total = jnp.zeros((16, D), F32)
     for i in range(4):
         for j in range(8):
-            total = total + staged[i, j].astype(F32)
+            total = total + staged[i, 16 * j : 16 * j + 16, :].astype(F32)
     vecs[...] = total
 
 
-def kernel_gather(small, wqkv, wout, win, wdown, vecs, small_f, qkv_f, out_f, in_f, down_f, staged, sems, send, recv):
-    peers = Peers()
-    links = Links(peers, send, recv)
-    peers.greet()
-    g = [Gather(n, links, own, full, sems.at[n])
-         for n, (own, full) in enumerate(((small, small_f), (wqkv, qkv_f), (wout, out_f), (win, in_f), (wdown, down_f)))]
-    for a in g:
-        a.begin()
-    for n, a in enumerate(g):
-        a.first()
-        if n:
-            g[n - 1].second()
-        if n > 1:
-            g[n - 2].third()
-    g[4].second()
-    g[3].third()
-    g[4].third()
-    for a in g:
-        a.last()
-    links.finish()
-    sum_small(small_f, staged, sems.at[5], vecs)
-
-
-def call_gather(own):
-    n = len(own)
-    return pl.pallas_call(
-        kernel_gather, name="gather",
-        out_shape=[sds((16, D), F32)] + [sds((4, 8) + a.shape, BF16) for a in own],
-        in_specs=[VMEM] * n, out_specs=[VMEM] + [ANY] * n,
-        scratch_shapes=[vm((4, 8, 16, D), BF16), pltpu.SemaphoreType.DMA((n + 1,)),
-                        pltpu.SemaphoreType.DMA((GATHER_SLOTS * n,)), pltpu.SemaphoreType.DMA((GATHER_SLOTS * n,))],
-        compiler_params=pltpu.CompilerParams(vmem_limit_bytes=VMEM_LIMIT, collective_id=1, has_side_effects=True),
-    )(*own)
-
-
-def kernel_scatter(sums_b, sums_c, down, inn, out, qkv, small_o, down_o, in_o, out_o, qkv_o, value, small_b, *rest):
-    bufs, (sems, send, recv) = rest[:28], rest[28:]
+def kernel_scatter(sums_b, sums_c, out, qkv, small_o, out_o, qkv_o, value, small_b, *rest):
+    bufs, (sems, send, recv) = rest[:14], rest[14:]
     peers = Peers()
     links = Links(peers, send, recv)
     pick = lambda ref, n: jnp.sum(ref[n], axis=0, keepdims=True)
@@ -768,10 +852,9 @@
     value[0] = jnp.concatenate(rows, axis=0)
     peers.greet()
     small = SmallSum(links, value, small_b)
-    s = [Scatter(n, links, parts, o, bufs[7 * n : 7 * n + 7], sems.at[n])
-         for n, (parts, o) in enumerate(((down, down_o), (inn, in_o), (out, out_o), (qkv, qkv_o)))]
-    for a in s:
-        a.begin()
+    s = [Scatter(n, links, parts, o, bufs[7 * n : 7 * n + 7], sems.at[n]) for n, (parts, o) in enumerate(((out, out_o), (qkv, qkv_o)))]
+    s[0].begin()
+    s[1].begin()
     small.send(0, "p")
     s[0].first()
     small.take(0)
@@ -780,27 +863,19 @@
     small.take(1)
     small.send(2, "y")
     s[0].second()
-    s[2].first()
+    s[1].second()
     small.take(2)
     small.spread()
     s[0].third()
-    s[1].second()
-    s[3].first()
     s[1].third()
-    s[2].second()
-    s[0].last()
-    s[3].second()
-    s[2].third()
     total = small.total()
     row, col = small_places(peers.dev)
     picked = lax.dot_general(total, small_select(col), (((1,), (0,)), ((), ())),
                              precision=lax.Precision.HIGHEST, preferred_element_type=F32)
     at_row = lax.broadcasted_iota(jnp.int32, (16, SMALL_LEN), 0) == row
     small_o[...] = jnp.sum(jnp.where(at_row, picked, 0.0), axis=0, keepdims=True)
+    s[0].last()
     s[1].last()
-    s[3].third()
-    s[2].last()
-    s[3].last()
     links.finish()
 
 
@@ -812,9 +887,9 @@
     return pl.pallas_call(
         kernel_scatter, name="scatter",
         out_shape=[sds((1, SMALL_LEN), F32)] + [sds(s, F32) for s in shapes],
-        in_specs=[VMEM, VMEM] + [ANY] * 4, out_specs=[VMEM] * 5,
+        in_specs=[VMEM, VMEM] + [ANY] * 2, out_specs=[VMEM] * 3,
         scratch_shapes=[vm((4, 16, D), F32), vm((6, 16, D), F32)] + bufs
-        + [pltpu.SemaphoreType.DMA((4,)), pltpu.SemaphoreType.DMA((slots,)), pltpu.SemaphoreType.DMA((slots,))],
+        + [pltpu.SemaphoreType.DMA((2,)), pltpu.SemaphoreType.DMA((slots,)), pltpu.SemaphoreType.DMA((slots,))],
         compiler_params=pltpu.CompilerParams(vmem_limit_bytes=VMEM_LIMIT, collective_id=2, has_side_effects=True),
     )(sums_b, sums_c, *parts)
 
@@ -863,18 +938,19 @@
     weights = (qkv_weight, out_weight, in_weight, down_weight)
     if own_links:
         row = jnp.concatenate(small + (jnp.zeros((SMALL_LEN - 288,), F32),)).reshape(1, SMALL_LEN)
-        vecs, _, *full = call_gather(call_prep(row, weights))
-        wqkv, wout, win, wdown = [a.reshape(-1, a.shape[-1]) for a in full]
+        vecs, made, (wqkv, wout, win, wdown) = call_a_links(sid, hidden_in, time_embed, call_prep(row, weights))
     else:
         vecs, (wqkv, wout, win, wdown) = gather_plain(small, weights)
-    x, a1t, q0, q1, k0, k1, v, kt, o, ot, lse = call_a(sid, hidden_in, time_embed, vecs, wqkv)
+        made = call_a(sid, hidden_in, time_embed, vecs, wqkv)
+    x, a1t, q0, q1, k0, k1, v, kt, o, ot, lse = made
     block_out, gx1, gb, go0, go1, dots, gdown, gin, sums_b = call_b(sid, x, o, grad_out, vecs, wout, win, wdown)
-    input_grad, time_grad, gqkv, gout, sums_c = call_c(
-        sid, x, a1t, q0, q1, k0, k1, v, kt, ot, lse, gx1, gb, go0, go1, dots, vecs, wqkv)
+    args_c = (sid, x, a1t, q0, q1, k0, k1, v, kt, ot, lse, gx1, gb, go0, go1, dots, vecs, wqkv)
     if own_links:
-        mine, gdown, gin, gout, gqkv = call_scatter(sums_b, sums_c, (gdown, gin, gout, gqkv))
+        input_grad, time_grad, gqkv, gout, sums_c, gdown, gin = call_c(True, *args_c, gdown, gin)
+        mine, gout, gqkv = call_scatter(sums_b, sums_c, (gout, gqkv))
         mine = mine.reshape(-1)
     else:
+        input_grad, time_grad, gqkv, gout, sums_c = call_c(False, *args_c)
         mine, (gdown, gin, gout, gqkv) = scatter_plain(sums_b, sums_c, (gdown, gin, gout, gqkv), small)
     gpg, gps, gqvb, gob, gmg, gms, gib, gdb = split_small(mine, small)
     return (block_out, input_grad, time_grad, gpg, gps, gqkv, gqvb, gout, gob, gmg, gms, gin, gib, gdown, gdb)

time: 360 us -> 301 us (0.84)
  Pallas kernels: 346 us -> 286 us
    pallas_call x1, Pallas kernels: 84.9 us -> 38.4 us  [call_scatter(): pl.pallas_call(kernel_scatter, name='scatter', out_shape=[sds((1, SMALL_L...]
    pallas_call x3 -> x2, Pallas kernels: 197 us -> 183 us  [the longest x1 105 us: call_a_links(): pl.pallas_call(functools.partial(kernel_a, True), name='part_a', out_shap...]
    unnamed x4 -> x16, local copies, waits for them, and re-layouts: 6.54 us -> 7.22 us
where the time goes in v2:
time: 301 us; the launch traced here: 300 us
  Pallas kernels  286 us (95%)
  local copies, waits for them, and re-layouts  13.9 us (5%)
    pallas_call x1, Pallas kernels, call_a_links(): pl.pallas_call(functools.partial(kernel_a, True), name='part_a', out_shap...  105 us
    pallas_call x1, Pallas kernels, call_c(): pl.pallas_call(functools.partial(kernel_c, linked), name='part_c', out_sh...  77.7 us
    pallas_call x1, Pallas kernels, call_b(): pl.pallas_call(kernel_b, name='part_b', out_shape=out, in_specs=[SMEM, AN...  62.1 us
    pallas_call x1, Pallas kernels, call_scatter(): pl.pallas_call(kernel_scatter, name='scatter', out_shape=[sds((1, SMALL_L...  38.4 us
    unnamed x16, local copies, waits for them, and re-layouts  7.22 us

profile of v2, /device:TPU:0, one launch (start us, length us, event | category | flops | bytes accessed | tf_op | source)
XLA Modules:
  0.0 300.2 jit_solution(4080199045234543278)
XLA Ops:
  0.7 0.8 concatenate.3
  1.5 0.6 reshape.70.small
  2.1 0.8 reshape.69
  2.8 0.6 slice_reduce_fusion.sid
  3.5 2.2 prep.1
  5.6 105.1 %part_a.1 = (f32[16,768]{1,0:T(8,128)}, f32[1024,768]{1,0:T(8,128)}, bf16[768,1024]{1,0:T(8,128)(2,1)}, bf16[1024,768]{1,0:T(8,128)(2,1)}, bf16[1024,768]{1,0:T(...) custom-call(s32[16]{0:T(128)} %slice_reduce_fusion.sid, ...), custom_call_target="tpu_custom_call" | custom-call | tf_op jit(solution)/shard_map/part_a/pallas_call | solution.py:302
  110.8 62.1 %part_b.1 = (f32[1024,768]{1,0:T(8,128)}, f32[1024,768]{1,0:T(8,128)}, bf16[1024,768]{1,0:T(8,128)(2,1)}, bf16[1024,768]{1,0:T(8,128)(2,1)}, bf16[1024,768]{1,0:...) custom-call(s32[16]{0:T(128)} %slice_reduce_fusion.sid, ...), custom_call_target="tpu_custom_call" | custom-call | tf_op jit(solution)/shard_map/part_b/pallas_call | solution.py:416
  172.9 77.7 %part_c.1 = (f32[1024,768]{1,0:T(8,128)}, f32[16,768]{1,0:T(8,128)}, bf16[768,2304]{1,0:T(8,128)(2,1)}, bf16[768,768]{1,0:T(8,128)(2,1)}, f32[4,8,768]{2,1,0:T(8...) custom-call(s32[16]{0:T(128)} %slice_reduce_fusion.sid, f32[1024,768]{1,0:T(8,128)} %get-tuple-element.60.x_h, ...), custom_call_target="tpu_custom_call" | custom-call | tf_op jit(solution)/shard_map/part_c/pallas_call | solution.py:553
  250.6 38.4 %scatter.1 = (f32[1,384]{1,0:T(1,128)}, f32[24,768]{1,0:T(8,128)}, f32[24,2304]{1,0:T(8,128)}) custom-call(f32[9,8,768]{2,1,0:T(8,128)} %get-tuple-element.86.sums_b, f32[4,8,768]{2,1,0:T(8,128)} %get-tuple-element.87.sums_c, bf16[4,4,2,24,768]{4,3,2,1,0:T(8,128)(2,1)} %bitcast.31, bf16[4,4,2,24,2304]{4,3,2,1,0:T(8,128)(2,1)} %bitcast.28), custom_call_target="tpu_custom_call" | custom-call | tf_op jit(solution)/shard_map/scatter/pallas_call | solution.py:887
  289.0 1.2 slice_bitcast_fusion.5
  290.2 1.3 slice_bitcast_fusion.1
  291.5 1.4 slice_bitcast_fusion
  292.9 0.0 copy-start.3
  292.9 0.0 copy-start.1
  292.9 0.0 copy-start
  292.9 3.8 %copy.37 = f32[1024,768]{1,0:T(8,128)} copy(f32[1024,768]{1,0:T(8,128)} %get-tuple-element.117) | data formatting | bytes 6291456
  296.8 0.0 copy-done.4
  296.8 0.6 copy.38
  297.4 0.0 copy-done.2
  297.4 0.7 copy.39
  298.1 0.0 copy-done.3
  298.1 0.6 copy.40
  298.7 0.7 copy.41
  299.4 0.7 copy.42
  (5 shorter events, 0.0 us)
Async XLA Ops:
  292.9 3.9 %copy-start.4 = (f32[16,768]{1,0:T(8,128)S(1)}, f32[16,768]{1,0:T(8,128)}, u32[]{:S(2)}) copy-start(f32[16,768]{1,0:T(8,128)} %get-tuple-element.118) | copy-start | bytes 147460
  292.9 4.5 %copy-start.2 = (f32[24,2304]{1,0:T(8,128)S(1)}, f32[24,2304]{1,0:T(8,128)}, u32[]{:S(2)}) copy-start(f32[24,2304]{1,0:T(8,128)} %get-tuple-element.121) | copy-start | bytes 663556
  292.9 5.2 %copy-start.3 = (f32[24,768]{1,0:T(8,128)S(1)}, f32[24,768]{1,0:T(8,128)}, u32[]{:S(2)}) copy-start(f32[24,768]{1,0:T(8,128)} %get-tuple-element.123) | copy-start | bytes 221188
  292.9 5.8 %copy-start.1 = (f32[24,3072]{1,0:T(8,128)S(1)}, f32[24,3072]{1,0:T(8,128)}, u32[]{:S(2)}) copy-start(f32[24,3072]{1,0:T(8,128)} %get-tuple-element.127) | copy-start | bytes 884740
  292.9 6.5 %copy-start = (f32[96,768]{1,0:T(8,128)S(1)}, f32[96,768]{1,0:T(8,128)}, u32[]{:S(2)}) copy-start(f32[96,768]{1,0:T(8,128)} %get-tuple-element.129) | copy-start | bytes 884740

commit v3 on v2

--- a/solution.py
+++ b/solution.py
@@ -90,8 +90,14 @@
 
 
 def run_hooks(step, hooks):
-    for n, action in hooks.items():
-        pl.when(step == n)(action)
+    for n, actions in hooks.items():
+        if not actions:
+            continue
+
+        @pl.when(step == n)
+        def _():
+            for action in actions:
+                action()
 
 
 def stage_norm1(sid, time, vecs, x, a1, a1t, hooks):
@@ -135,7 +141,7 @@
     return lax.broadcasted_iota(jnp.int32, shape, 0) < 64
 
 
-def stage_q(sid, vecs, a1, w, q0, q1):
+def stage_q(sid, vecs, a1, w, q0, q1, hooks):
     @pl.loop(0, BLOCK // TB)
     def _(i):
         at = rows_at(i, TB)
@@ -147,9 +153,10 @@
             part = acc[:, 128 * p : 128 * p + 128]
             q0[at, 128 * p : 128 * p + 128] = jnp.where(low, part, mq).astype(BF16)
             q1[at, 128 * p : 128 * p + 128] = jnp.where(low, mq, part).astype(BF16)
-
-
-def stage_k(sid, a1, w, k0, k1, kt):
+        run_hooks(i, hooks)
+
+
+def stage_k(sid, a1, w, k0, k1, kt, hooks):
     @pl.loop(0, BLOCK // TB)
     def _(i):
         at = rows_at(i, TB)
@@ -161,9 +168,10 @@
             k0[at, 128 * p : 128 * p + 128] = jnp.where(low, part, mk).astype(BF16)
             k1[at, 128 * p : 128 * p + 128] = jnp.where(low, mk, part).astype(BF16)
         kt[:, at] = acc.T.astype(BF16)
-
-
-def stage_v(vecs, a1, w, v, vt0, vt1):
+        run_hooks(i, hooks)
+
+
+def stage_v(vecs, a1, w, v, vt0, vt1, hooks):
     @pl.loop(0, BLOCK // TB)
     def _(i):
         at = rows_at(i, TB)
@@ -175,6 +183,7 @@
             part = accT[128 * p : 128 * p + 128, :]
             vt0[128 * p : 128 * p + 128, at] = jnp.where(low, part, 1.0).astype(BF16)
             vt1[128 * p : 128 * p + 128, at] = jnp.where(low, 1.0, part).astype(BF16)
+        run_hooks(i, hooks)
 
 
 QB = 256
@@ -199,61 +208,138 @@
     lse[pl.ds(2 * pair + 1, 1), at] = logs[1]
 
 
+SCHEDULE_A = {
+    ("pre", 0): ("s.F0", "q.F0", "k.F0", "s.F1", "s.F3", "s.F2", "s.S0", "q.F1", "s.S1", "s.S3", "s.S2", "q.F3", "q.F2", "q.S0", "q.S1", "s.T", "k.F1", "q.S3", "k.F3", "s.L",),
+    ("norm", 0): ("q.S2",),
+    ("norm", 1): ("k.F2", "k.S0", "v.F0",),
+    ("norm", 3): ("v.F1",),
+    ("norm", 5): ("k.S1", "v.F3",),
+    ("norm", 6): ("k.S3",),
+    ("norm", 7): ("q.T", "v.F2", "o.F0",),
+    ("q", -1): ("k.S2", "o.F1", "v.S0", "o.F3", "q.L",),
+    ("q", 1): ("v.S1",),
+    ("q", 2): ("o.F2",),
+    ("k", -1): ("v.S3", "v.S2", "i.F0", "o.S0", "k.T", "o.S1", "i.F1", "k.L",),
+    ("k", 1): ("o.S3",),
+    ("v", -1): ("v.T", "o.S2", "i.F3", "v.L",),
+    ("att", 1): ("i.F2", "i.S0", "d.F0",),
+    ("att", 2): ("o.T", "i.S1",),
+    ("att", 4): ("o.L", "d.F1",),
+    ("att", 5): ("i.S3",),
+    ("att", 7): ("i.S2", "d.F3",),
+    ("att", 10): ("d.F2",),
+    ("att", 11): ("d.S0",),
+    ("att", 15): ("d.S1",),
+    ("att", 16): ("i.T",),
+    ("att", 18): ("d.S3",),
+    ("att", 19): ("i.L",),
+    ("att", 20): ("d.S2",),
+    ("end", 0): ("d.T", "d.L",),
+}
+SCHEDULE_B = {
+    ("gd", 1): ("x.B",),
+    ("gd", 2): ("y.B",),
+    ("wd", 0): ("z.B",),
+    ("p2", 0): ("x.F", "y.F", "z.F",),
+    ("p2", 1): ("x.S",),
+    ("p2", 3): ("y.S",),
+    ("p2", 4): ("z.S",),
+    ("p2", 6): ("x.T", "y.T",),
+    ("p2", 7): ("z.T",),
+    ("gi", 1): ("x.L",),
+    ("gi", 3): ("y.L",),
+    ("end", 0): ("z.L",),
+}
+SCHEDULE_C = {
+    ("pre", 0): ("0.B", "1.B", "2.B", "3.B",),
+    ("att", 0): ("0.F", "1.F", "2.F", "3.F",),
+    ("att", 1): ("o.B", "0.S",),
+    ("att", 3): ("o.F", "1.S",),
+    ("att", 4): ("2.S",),
+    ("att", 6): ("3.S",),
+    ("gw", 0): ("0.T",),
+    ("att", 8): ("o.S",),
+    ("att", 9): ("a.B", "1.T",),
+    ("att", 10): ("2.T",),
+    ("att", 11): ("a.F", "o.T", "0.L", "3.T",),
+    ("att", 12): ("1.L",),
+    ("att", 13): ("a.S",),
+    ("att", 14): ("2.L",),
+    ("gw", 1): ("a.T", "o.L",),
+    ("att", 16): ("3.L",),
+    ("att", 17): ("b.B",),
+    ("att", 19): ("a.L", "b.F",),
+    ("att", 22): ("b.S",),
+    ("gw", 3): ("b.T", "c.B",),
+    ("ln", 1): ("c.F",),
+    ("ln", 2): ("b.L",),
+    ("ln", 3): ("c.S",),
+    ("end", 0): ("c.T", "c.L",),
+}
+
+
+class Schedule:
+    def __init__(self, table):
+        self.table, self.units = table, {}
+
+    def actions(self, seg, step):
+        found = self.table.get((seg, step), ()) if self.units else ()
+        return [functools.partial(self.units[a[0]].do, a[2:]) for a in found]
+
+    def hooks(self, seg, first=0, last=24):
+        return {n: self.actions(seg, n) for n in range(first, last) if self.actions(seg, n)}
+
+    def run(self, seg, step, part=slice(None)):
+        for action in self.actions(seg, step)[part]:
+            action()
+
+
 def kernel_a(linked, sid, hidden, time, *refs):
     if linked:
         own, refs = refs[:5], refs[5:]
         vecs, refs = refs[0], refs[1:]
     else:
-        (vecs, wqkv), refs = refs[:2], refs[2:]
+        (vecs, *wq), refs = refs[:4], refs[4:]
     (x_h, a1t_h, q0_h, q1_h, k0_h, k1_h, v_h, kt_h, o_h, ot_h, lse), refs = refs[:11], refs[11:]
     if linked:
-        full, refs = refs[:5], refs[5:]
-        wqkv = full[1]
+        full, refs = refs[:7], refs[7:]
+        wq = full[1:4]
     (x, a1, a1t, q0, q1, k0, k1, v, kt, vt0, vt1, o, ot, w, sems), refs = refs[:15], refs[15:]
     mv = Mover(sems)
     cx = mv.start(hidden, x)
-    norm_hooks, attention_hooks, after = {}, {}, [[], [], [], []]
+    plan = Schedule(SCHEDULE_A)
     if linked:
         staged, local_sems, send, recv = refs
         peers = Peers()
         links = Links(peers, send, recv)
         peers.greet()
-        small, qkv, out, inn, down = [Gather(n, links, own[n], full[n], local_sems.at[n]) for n in range(5)]
-        for a in (small, qkv, out, inn, down):
-            a.begin()
-        small.first()
-        qkv.first()
-        small.second()
-        small.third()
-        out.first((0,))
-        small.last()
-        sum_small(full[0], staged, local_sems.at[5], vecs)
-        norm_hooks = {1: qkv.second, 3: out.first_rest, 5: qkv.third, 6: inn.first_own}
-        after = [[out.second, inn.first_rest], [out.third, down.first_own], [inn.second, down.first_rest], []]
-        attention_hooks = {4: inn.third, 9: down.second, 17: down.third}
+        small, qkv, out, inn, down = own
+        pieces = [View(small)] + [View(qkv, slice(None), pl.ds(D * n, D)) for n in range(3)] + [View(out), View(inn), View(down)]
+        rows = (small.shape[0], D // 32, D // 32, D // 32, D // 32, D // 32, FF // 32)
+        for n, name in enumerate("sqkvoid"):
+            plan.units[name] = Gather(n, links, pieces[n], rows[n], full[n], local_sems.at[n])
+            plan.units[name].begin()
+    run, hooks = plan.run, plan.hooks
+    run("pre", 0)
+    if linked:
+        build_table(full[0], staged, local_sems.at[7], vecs)
     cx.wait()
-    stage_norm1(sid, time, vecs, x, a1, a1t, norm_hooks)
+    stage_norm1(sid, time, vecs, x, a1, a1t, hooks("norm"))
     outs = [mv.start(x, x_h), mv.start(a1t, a1t_h)]
-    if linked:
-        qkv.last()
-    cw = [mv.start(wqkv.at[:, :, pl.ds(D * j, D)], w.at[j]) for j in range(3)]
-
-    def weight(j):
-        cw[j].wait()
+
+    def weight(name, j):
+        run(name, -1)
+        copy = mv.start(wq[j], w.at[j])
+        copy.wait()
         return w[j].reshape(D, D)
 
-    stage_q(sid, vecs, a1, weight(0), q0, q1)
-    for action in after[0]:
-        action()
+    stage_q(sid, vecs, a1, weight("q", 0), q0, q1, hooks("q"))
     outs += [mv.start(q0, q0_h), mv.start(q1, q1_h)]
-    stage_k(sid, a1, weight(1), k0, k1, kt)
-    for action in after[1]:
-        action()
+    stage_k(sid, a1, weight("k", 1), k0, k1, kt, hooks("k"))
     outs += [mv.start(k0, k0_h), mv.start(k1, k1_h), mv.start(kt, kt_h)]
-    stage_v(vecs, a1, weight(2), v, vt0, vt1)
-    for action in after[2]:
-        action()
+    stage_v(vecs, a1, weight("v", 2), v, vt0, vt1, hooks("v"))
     outs += [mv.start(v, v_h)]
+    attention_hooks = hooks("att")
 
     @pl.loop(0, PAIRS * (BLOCK // QB))
     def _(step):
@@ -261,11 +347,10 @@
         run_hooks(step, attention_hooks)
 
     outs += [mv.start(o, o_h), mv.start(ot, ot_h)]
+    run("end", 0)
     for copy in outs:
         copy.wait()
     if linked:
-        for a in (out, inn, down):
-            a.last()
         links.finish()
 
 
@@ -286,42 +371,56 @@
     vm(TOK, BF16), vm(TOKT, BF16), vm((3, 4, D // 4, D), BF16), pltpu.SemaphoreType.DMA((16,))]
 
 
-def call_a(sid, hidden, time, vecs, wqkv):
+def call_a(sid, hidden, time, vecs, wq):
     return pl.pallas_call(
         functools.partial(kernel_a, False),
         name="part_a",
         out_shape=OUT_A,
-        in_specs=[SMEM, ANY, VMEM, VMEM, ANY],
+        in_specs=[SMEM, ANY, VMEM, VMEM, ANY, ANY, ANY],
         out_specs=[ANY] * 10 + [VMEM],
         scratch_shapes=SCRATCH_A,
         compiler_params=pltpu.CompilerParams(vmem_limit_bytes=VMEM_LIMIT),
-    )(sid, hidden, time, vecs, wqkv.reshape(4, D // 4, 3 * D))
+    )(sid, hidden, time, vecs, *[a.reshape(4, D // 4, D) for a in wq])
 
 
 def call_a_links(sid, hidden, time, own):
+    small, qkv, out, inn, down = own
+    sizes = [small.shape] + [(D // 32, D)] * 4 + [inn.shape, down.shape]
+    slots = GATHER_SLOTS * 7
     res = pl.pallas_call(
         functools.partial(kernel_a, True),
         name="part_a",
-        out_shape=[sds((16, D), F32)] + OUT_A + [sds((4, 8 * a.shape[0], a.shape[1]), BF16) for a in own],
+        out_shape=[sds((16, D), F32)] + OUT_A + [sds((4, 8 * r, c), BF16) for r, c in sizes],
         in_specs=[SMEM, ANY, VMEM] + [VMEM] * 5,
-        out_specs=[VMEM] + [ANY] * 10 + [VMEM] + [ANY] * 5,
-        scratch_shapes=SCRATCH_A + [vm((4, 128, D), BF16), pltpu.SemaphoreType.DMA((6,)),
-                                    pltpu.SemaphoreType.DMA((GATHER_SLOTS * 5,)), pltpu.SemaphoreType.DMA((GATHER_SLOTS * 5,))],
+        out_specs=[VMEM] + [ANY] * 10 + [VMEM] + [ANY] * 7,
+        scratch_shapes=SCRATCH_A + [vm((4, 64, SMALL_LEN), BF16)] + [pltpu.SemaphoreType.DMA((n,)) for n in (8, slots, slots)],
         compiler_params=pltpu.CompilerParams(vmem_limit_bytes=VMEM_LIMIT, collective_id=1, has_side_effects=True),
     )(sid, hidden, time, *own)
-    return res[0], res[1:12], [a.reshape(-1, a.shape[-1]) for a in res[13:]]
-
-
-def kernel_b(sid, x_h, o_h, gout_h, vecs, wout_h, win_h, wdown_h,
-             out_h, gx1_h, gb_h, go0_h, go1_h, dots, gdown_h, gin_h, sums,
-             x, o, gy, wout, win, wdown, gm, a2t, ht, gu, gb, go0, go1, stage, sems):
+    full = [a.reshape(-1, a.shape[-1]) for a in res[13:]]
+    return res[0], res[1:12], full[:3], full[3:]
+
+
+def kernel_b(linked, sid, x_h, o_h, gout_h, vecs, wout_h, win_h, wdown_h,
+             out_h, gx1_h, gb_h, go0_h, go1_h, dots, gdown_h, gin_h, sums, *refs):
+    if linked:
+        gdown_o, refs = refs[0], refs[1:]
+    (x, o, gy, wout, win, wdown, gm, a2t, ht, h, gu, gb, go0, go1, stage_d, stage, sems), refs = refs[:17], refs[17:]
+    plan = Schedule(SCHEDULE_B)
+    if linked:
+        bufs, (local_sems, send, recv) = refs[:21], refs[21:]
+        peers = Peers()
+        links = Links(peers, send, recv)
+        peers.greet()
+        for n, name in enumerate("xyz"):
+            keep = functools.partial(store_lanes, gdown_o, ((0, DT * n, DT),))
+            plan.units[name] = Scatter(n, links, (gdown_h, n), keep, bufs[7 * n : 7 * n + 7], local_sems.at[n])
     mv = Mover(sems)
     cx, co, cg = mv.start(x_h, x), mv.start(o_h, o), mv.start(gout_h, gy)
     cwo = mv.start(wout_h, wout)
     cwi = [mv.start(win_h.at[:, pl.ds(D * j, D)], win.at[j]) for j in range(4)]
     cwd = [mv.start(wdown_h.at[pl.ds(D * j, D), :], wdown.at[j]) for j in range(4)]
     sums[...] = jnp.zeros_like(sums)
-    for c in [cx, co, cg, cwo] + cwi + cwd:
+    for c in [cx, co, cg, cwo] + cwi:
         c.wait()
     lane = lax.broadcasted_iota(jnp.int32, (16, D), 1) // HEAD_DIM
     heads = (lane == lax.broadcasted_iota(jnp.int32, (16, D), 0)).astype(BF16)
@@ -334,32 +433,65 @@
         return [pltpu.make_async_copy(x.at[at, :], out_h.at[at, :], so.at[16]),
                 pltpu.make_async_copy(gy.at[at, :], gx1_h.at[at, :], so.at[17])]
 
+    def live_rows(i):
+        return jnp.concatenate(
+            [jnp.full((SHORT, 1), (sid[(TB // SHORT) * i + g] >= 0).astype(F32), F32) for g in range(TB // SHORT)], axis=0)
+
     @pl.loop(0, blocks)
     def _(i):
         at = rows_at(i, TB)
-        live = jnp.concatenate(
-            [jnp.full((SHORT, 1), (sid[(TB // SHORT) * i + g] >= 0).astype(F32), F32) for g in range(TB // SHORT)], axis=0)
         x1 = x[at, :] + mm(o[at, :], wout[...]) + vecs[4:5, :]
-        n2, r2 = normalize(x1)
+        x[at, :] = x1
+        n2, _ = normalize(x1)
         a2f = n2 * vecs[5:6, :] + vecs[6:7, :]
         a2 = a2f.astype(BF16)
         a2t[:, at] = a2f.T.astype(BF16)
-        gyb = gy[at, :] * live
-        gmb = gyb.astype(BF16)
-        gm[at, :] = gmb
-        acc = x1 + vecs[11:12, :]
-        ga2 = jnp.zeros((TB, D), F32)
+        gyb = gy[at, :] * live_rows(i)
+        gy[at, :] = gyb
+        gm[at, :] = gyb.astype(BF16)
         for j in range(4):
             u = mm(a2, win[j]) + vecs[7 + j : 8 + j, :]
             hf, slope = gelu_parts(u)
             ht[D * j : D * j + D, at] = hf.T.astype(BF16)
-            acc = acc + mm(hf.astype(BF16), wdown[j])
-            guf = mm_t(gmb, wdown[j]) * slope
+            h[at, D * j : D * j + D] = hf.astype(BF16)
+            gu[at, D * j : D * j + D] = slope.astype(BF16)
+
+    pending = None
+    for t in range(D // DT):
+        if pending is not None:
+            pending.wait()
+
+        @pl.loop(0, FF // 384)
+        def _(r):
+            part = mm(ht[rows_at(r, 384), :], gm[:, DT * t : DT * t + DT]).astype(BF16)
+            stage_d[r // 2, pl.ds(2 * (r % 2), 2)] = part.reshape(2, 192, DT)
+
+        plan.run("gd", t)
+        pending = pltpu.make_async_copy(stage_d, gdown_h.at[t], so.at[18])
+        pending.start()
+    for c in cwd:
+        c.wait()
+    pending.wait()
+    plan.run("wd", 0)
+    first_hooks, second_hooks = ({n: plan.actions("p2", n) for n in range(k, 2 * blocks, 2)} for k in range(2))
+
+    @pl.loop(0, blocks)
+    def _(i):
+        at = rows_at(i, TB)
+        n2, r2 = normalize(x[at, :])
+        gmb = gm[at, :]
+        acc = x[at, :] + vecs[11:12, :]
+        ga2 = jnp.zeros((TB, D), F32)
+        for j in range(4):
+            acc = acc + mm(h[at, D * j : D * j + D], wdown[j])
+            guf = mm_t(gmb, wdown[j]) * gu[at, D * j : D * j + D].astype(F32)
             gub = guf.astype(BF16)
             gu[at, D * j : D * j + D] = gub
             sums[4 + j] += fold8(gub.astype(F32))
             ga2 = ga2 + mm_t(gub, win[j])
-        x[at, :] = acc * live
+        x[at, :] = acc * live_rows(i)
+        run_hooks(2 * i, first_hooks)
+        gyb = gy[at, :]
         sums[8] += fold8(gmb.astype(F32))
         sums[2] += fold8(ga2 * n2)
         sums[3] += fold8(ga2)
@@ -378,51 +510,61 @@
         low = lax.rem(lax.broadcasted_iota(jnp.int32, (TB, D), 1), 128) < 64
         go0[at, :] = jnp.where(low, go, 0.0).astype(BF16)
         go1[at, :] = jnp.where(low, 0.0, go).astype(BF16)
+        run_hooks(2 * i + 1, second_hooks)
 
     outs += [mv.start(gb, gb_h), mv.start(go0, go0_h), mv.start(go1, go1_h)]
-
-    def tile_out(j, slot):
-        return pltpu.make_async_copy(stage.at[slot], gdown_h.at[rows_at(j, D), :], so.at[18 + slot])
-
-    def tile_in(j, slot):
-        return pltpu.make_async_copy(stage.at[slot], gin_h.at[:, pl.ds(D * j, D)], so.at[18 + slot])
-
-    pending = [None, None]
-    for t in range(8):
-        slot, j = t % 2, t % 4
-        if pending[slot] is not None:
-            pending[slot].wait()
-
-        @pl.loop(0, D // TB)
+    copies = []
+    for j in range(4):
+        if j > 1:
+            copies[j - 2].wait()
+
+        @pl.loop(0, 2)
         def _(r):
-            if t < 4:
-                stage[slot, rows_at(r, TB), :] = mm(ht[pl.ds(pl.multiple_of(D * j + r * TB, TB), TB), :], gm[...]).astype(BF16)
-            else:
-                stage[slot, rows_at(r, TB), :] = mm(a2t[rows_at(r, TB), :], gu[:, D * j : D * j + D]).astype(BF16)
-
-        pending[slot] = tile_out(j, slot) if t < 4 else tile_in(j, slot)
-        pending[slot].start()
-    for c in pending:
-        c.wait()
-    for c in outs:
+            part = mm(a2t[rows_at(r, 384), :], gu[:, D * j : D * j + D]).astype(BF16)
+            stage[j % 2, pl.ds(2 * r, 2)] = part.reshape(2, 4, 48, D)
+
+        plan.run("gi", j)
+        copies.append(pltpu.make_async_copy(stage.at[j % 2], gin_h.at[j], so.at[19 + j % 2]))
+        copies[j].start()
+    plan.run("end", 0)
+    for c in copies[2:] + outs:
         c.wait()
     for i in range(blocks):
         for c in out_copies(i):
             c.wait()
-
-
-def call_b(sid, x, o, gout, vecs, wout, win, wdown):
-    out = [sds(TOK, F32), sds(TOK, F32)] + [sds(TOK, BF16)] * 3 + [sds((16, BLOCK), F32), sds((FF, D), BF16), sds((D, FF), BF16), sds((9, 8, D), F32)]
+    if linked:
+        links.finish()
+
+
+DT = 256
+
+
+def store_lanes(out, places, total):
+    for source, target, width in places:
+        out[:, target : target + width] = total[:, source : source + width]
+
+
+def call_b(linked, sid, x, o, gout, vecs, wout, win, wdown):
+    out = [sds(TOK, F32), sds(TOK, F32)] + [sds(TOK, BF16)] * 3 + [
+        sds((16, BLOCK), F32), sds((D // DT, 4, 4, 192, DT), BF16), sds((4, 4, 4, 48, D), BF16), sds((9, 8, D), F32)]
+    out_specs = [ANY] * 5 + [VMEM, ANY, ANY, VMEM]
+    scratch = [vm(TOK, F32), vm(TOK, BF16), vm(TOK, F32), vm((D, D), BF16), vm((4, D, D), BF16), vm((4, D, D), BF16),
+               vm(TOK, BF16), vm(TOKT, BF16), vm((FF, BLOCK), BF16), vm((BLOCK, FF), BF16), vm((BLOCK, FF), BF16),
+               vm(TOK, BF16), vm(TOK, BF16), vm(TOK, BF16), vm((4, 4, 192, DT), BF16), vm((2, 4, 4, 48, D), BF16), pltpu.SemaphoreType.DMA((21,))]
+    extra = {}
+    if linked:
+        out.append(sds((FF // 32, D), F32))
+        out_specs.append(VMEM)
+        scratch += 3 * scatter_bufs(FF // 32, DT) + [pltpu.SemaphoreType.DMA((n,)) for n in (3, 3 * SCATTER_SLOTS, 3 * SCATTER_SLOTS)]
+        extra = dict(collective_id=2, has_side_effects=True)
     return pl.pallas_call(
-        kernel_b,
+        functools.partial(kernel_b, linked),
         name="part_b",
         out_shape=out,
         in_specs=[SMEM, ANY, ANY, ANY, VMEM, ANY, ANY, ANY],
-        out_specs=[ANY] * 5 + [VMEM, ANY, ANY, VMEM],
-        scratch_shapes=[vm(TOK, F32), vm(TOK, BF16), vm(TOK, F32), vm((D, D), BF16), vm((4, D, D), BF16), vm((4, D, D), BF16),
-                        vm(TOK, BF16), vm(TOKT, BF16), vm((FF, BLOCK), BF16), vm((BLOCK, FF), BF16),
-                        vm(TOK, BF16), vm(TOK, BF16), vm(TOK, BF16), vm((2, D, D), BF16), pltpu.SemaphoreType.DMA((20,))],
-        compiler_params=pltpu.CompilerParams(vmem_limit_bytes=VMEM_LIMIT),
+        out_specs=out_specs,
+        scratch_shapes=scratch,
+        compiler_params=pltpu.CompilerParams(vmem_limit_bytes=VMEM_LIMIT, **extra),
     )(sid, x, o, gout, vecs, wout, win, wdown)
 
 
@@ -454,54 +596,74 @@
         gqkv[2, :, lanes] = gv_acc[...].astype(BF16)
 
 
-def kernel_c(linked, sid, x_h, a1t_h, q0_h, q1_h, k0_h, k1_h, v_h, kt_h, ot_h, lse, gx1_h, gb_h, go0_h, go1_h, dots, vecs, wqkv_h, *refs):
-    if linked:
-        parts, refs = refs[:2], refs[2:]
-    (ig_h, tg, gqkvw_h, goutw_h, sums), refs = refs[:5], refs[5:]
-    if linked:
-        owns, refs = refs[:2], refs[2:]
+UNITS_C = "0123oabc"
+
+
+def kernel_c(linked, sid, x_h, a1t_h, q0_h, q1_h, k0_h, k1_h, v_h, kt_h, ot_h, lse, gx1_h, gb_h, go0_h, go1_h, dots, vecs, wq_h, wk_h, wv_h, *refs):
+    if linked:
+        (gin_h, sums_b), refs = refs[:2], refs[2:]
+    (ig_h, tg, gqkv_h, gwo_h, sums), refs = refs[:5], refs[5:]
+    if linked:
+        (gin_o, gout_o, gqkv_o, small_o), refs = refs[:4], refs[4:]
     (x, a1t, q0, q1, k0, k1, v, kt, ot, gx1, gb, go0, go1, w, gqkv, gk_acc, gv_acc, gw, gwo, tsum, sems), refs = refs[:21], refs[21:]
-    hooks, rest = {}, []
-    if linked:
-        bufs, (local_sems, send, recv) = refs[:14], refs[14:]
+    plan = Schedule(SCHEDULE_C)
+    if linked:
+        bufs, (value, small_b, local_sems, send, recv) = refs[:56], refs[56:]
         peers = Peers()
         links = Links(peers, send, recv)
         peers.greet()
-        down, inn = [Scatter(n, links, parts[n], owns[n], bufs[7 * n : 7 * n + 7], local_sems.at[n]) for n in range(2)]
-        down.begin()
-        inn.begin()
-        hooks = {0: down.first, 2: inn.first, 5: down.second, 9: inn.second, 13: down.third, 17: inn.third}
-        rest = [down.last, inn.last, links.finish]
+        third = D // 3
+        for n, name in enumerate(UNITS_C):
+            if n < 4:
+                parts, keep = (gin_h, n), functools.partial(store_lanes, gin_o, ((0, D * n, D),))
+            elif n == 4:
+                parts, keep = (gwo_h,), functools.partial(store_lanes, gout_o, ((0, 0, D),))
+            else:
+                places = tuple((third * m, D * m + third * (n - 5), third) for m in range(3))
+                parts, keep = (gqkv_h, n - 5), functools.partial(store_lanes, gqkv_o, places)
+            plan.units[name] = Scatter(n, links, parts, keep, bufs[7 * n : 7 * n + 7], local_sems.at[n])
+        plan.run("pre", 0)
     mv = Mover(sems)
     early = [mv.start(s, d) for s, d in ((ot_h, ot), (gb_h, gb), (q0_h, q0), (q1_h, q1), (k0_h, k0), (k1_h, k1), (v_h, v), (kt_h, kt), (go0_h, go0), (go1_h, go1))]
     late = [mv.start(a1t_h, a1t), mv.start(x_h, x), mv.start(gx1_h, gx1)]
-    late += [mv.start(wqkv_h.at[:, pl.ds(D * j, D)], w.at[j]) for j in range(3)]
+    late += [mv.start(part, w.at[j]) for j, part in enumerate((wq_h, wk_h, wv_h))]
     for c in early[:2]:
         c.wait()
     sums[...] = jnp.zeros_like(sums)
 
-    @pl.loop(0, D // TB)
+    @pl.loop(0, 2)
     def _(r):
-        gwo[rows_at(r, TB), :] = mm(ot[rows_at(r, TB), :], gb[...]).astype(BF16)
-
-    outs = [mv.start(gwo, goutw_h)]
+        gwo[pl.ds(2 * r, 2)] = mm(ot[rows_at(r, 384), :], gb[...]).astype(BF16).reshape(2, 4, 48, D)
+
+    gwo_copy = mv.start(gwo, gwo_h)
     for c in early[2:]:
         c.wait()
-
-    @pl.loop(0, PAIRS * (BLOCK // QB))
-    def _(step):
-        attention_back_step(step, q0, q1, k0, k1, v, kt, go0, go1, lse, dots, gk_acc, gv_acc, gqkv)
-        run_hooks(step, hooks)
-
-    for c in late:
+    gwo_copy.wait()
+    plan.run("gwo", 0)
+    steps = 2 * (BLOCK // QB)
+    gw_copies = []
+    for chunk in range(3):
+        hooks = plan.hooks("att", steps * chunk, steps * chunk + steps)
+
+        @pl.loop(steps * chunk, steps * chunk + steps)
+        def _(step):
+            attention_back_step(step, q0, q1, k0, k1, v, kt, go0, go1, lse, dots, gk_acc, gv_acc, gqkv)
+            run_hooks(step, hooks)
+
+        if chunk == 0:
+            late[0].wait()
+        for j in range(3):
+            for r in range(2):
+                part = mm(a1t[384 * r : 384 * r + 384, :], gqkv[j, :, 256 * chunk : 256 * chunk + 256]).astype(BF16)
+                gw[chunk, 2 * r : 2 * r + 2, :, :, 256 * j : 256 * j + 256] = part.reshape(2, 4, 48, 256)
+        gw_copies.append(mv.start(gw.at[chunk], gqkv_h.at[chunk]))
+        plan.run("gw", chunk)
+        gw_copies[chunk].wait()
+    for c in late[1:]:
         c.wait()
-    for j in range(3):
-        @pl.loop(0, D // TB)
-        def _(r):
-            gw[j, rows_at(r, TB), :] = mm(a1t[rows_at(r, TB), :], gqkv[j]).astype(BF16)
-
-        outs.append(mv.start(gw.at[j], gqkvw_h.at[:, pl.ds(D * j, D)]))
+    plan.run("gw", 3)
     gain = vecs[0:1, :]
+    ln_hooks = plan.hooks("ln")
 
     @pl.loop(0, BLOCK // TB)
     def _(i):
@@ -519,36 +681,55 @@
             part = total[SHORT * g : SHORT * g + SHORT, :] * live
             x[rows_at((TB // SHORT) * i + g, SHORT), :] = part
             tsum[pl.ds((TB // SHORT) * i + g, 1), :] = jnp.sum(part, axis=0, keepdims=True)
-
-    outs.append(mv.start(x, ig_h))
+        run_hooks(i, ln_hooks)
+
+    ig_copy = mv.start(x, ig_h)
+    if linked:
+        pick = lambda ref, n: jnp.sum(ref[n], axis=0, keepdims=True)
+        rows = [pick(sums, n) for n in range(4)] + [pick(sums_b, n) for n in range(1, 9)] + [jnp.zeros((4, D), F32)]
+        value[0] = jnp.concatenate(rows, axis=0)
+        small = SmallSum(links, value, small_b)
+        small.send(0, "p")
     row = lax.broadcasted_iota(jnp.int32, (GROUPS, D), 0)
     acc = jnp.zeros((GROUPS, D), F32)
     for g in range(GROUPS):
         acc = acc + jnp.where(row == sid[g], tsum[g : g + 1, :], 0.0)
     tg[...] = acc
-    for action in rest:
-        action()
-    for c in outs:
-        c.wait()
+    if linked:
+        small.take(0)
+        small.send(1, "x")
+        small.take(1)
+        small.send(2, "y")
+        plan.run("end", 0, slice(0, -1))
+        small.take(2)
+        small.spread()
+        row, col = small_places(peers.dev)
+        select = small_select(col)
+        plan.run("end", 0, slice(-1, None))
+        picked = lax.dot_general(small.total(), select, (((1,), (0,)), ((), ())),
+                                 precision=lax.Precision.HIGHEST, preferred_element_type=F32)
+        at_row = lax.broadcasted_iota(jnp.int32, (16, SMALL_LEN), 0) == row
+        small_o[...] = jnp.sum(jnp.where(at_row, picked, 0.0), axis=0, keepdims=True)
+        links.finish()
+    ig_copy.wait()
 
 
 def call_c(linked, *args):
-    out = [sds(TOK, F32), sds((GROUPS, D), F32), sds((D, 3 * D), BF16), sds((D, D), BF16), sds((4, 8, D), F32)]
-    in_specs = [SMEM] + [ANY] * 9 + [VMEM] + [ANY] * 4 + [VMEM, VMEM, ANY]
+    out = [sds(TOK, F32), sds((GROUPS, D), F32), sds((3, 4, 4, 48, D), BF16), sds((4, 4, 48, D), BF16), sds((4, 8, D), F32)]
+    in_specs = [SMEM] + [ANY] * 9 + [VMEM] + [ANY] * 4 + [VMEM, VMEM, ANY, ANY, ANY]
     out_specs = [ANY, VMEM, ANY, ANY, VMEM]
     scratch = [vm(TOK, F32), vm(TOKT, BF16)] + [vm(TOK, BF16)] * 5 + [vm(TOKT, BF16)] * 2 + [vm(TOK, F32)] + [vm(TOK, BF16)] * 3
-    scratch += [vm((3, D, D), BF16), vm((3, BLOCK, D), BF16), vm((BLOCK, 128), F32), vm((BLOCK, 128), F32), vm((3, D, D), BF16), vm((D, D), BF16),
+    scratch += [vm((3, D, D), BF16), vm((3, BLOCK, D), BF16), vm((BLOCK, 128), F32), vm((BLOCK, 128), F32), vm((3, 4, 4, 48, D), BF16), vm((4, 4, 48, D), BF16),
                 vm((GROUPS, D), F32), pltpu.SemaphoreType.DMA((24,))]
     extra = {}
     if linked:
-        args, parts = args[:-2], args[-2:]
-        shapes = [(p.shape[0] // 32, p.shape[1]) for p in parts]
-        args = args + tuple(p.reshape(4, 4, 2, r, p.shape[1]) for p, (r, _) in zip(parts, shapes))
-        in_specs += [ANY] * 2
-        out += [sds(s, F32) for s in shapes]
-        out_specs += [VMEM] * 2
-        scratch += [b for s in shapes for b in scatter_bufs(*s)]
-        scratch += [pltpu.SemaphoreType.DMA((n,)) for n in (2, 2 * SCATTER_SLOTS, 2 * SCATTER_SLOTS)]
+        in_specs += [ANY, VMEM]
+        out += [sds((D // 32, n * D), F32) for n in (4, 1, 3)] + [sds((1, SMALL_LEN), F32)]
+        out_specs += [VMEM] * 4
+        units = len(UNITS_C)
+        slots = SCATTER_SLOTS * units + 6
+        scratch += units * scatter_bufs(D // 32, D) + [vm((4, 16, D), F32), vm((6, 16, D), F32)]
+        scratch += [pltpu.SemaphoreType.DMA((n,)) for n in (units, slots, slots)]
         extra = dict(collective_id=3, has_side_effects=True)
     return pl.pallas_call(
         functools.partial(kernel_c, linked),
@@ -563,7 +744,8 @@
 
 AXES = ("dp", "fsdp")
 MESH = pl.DeviceIdType.MESH
-SMALL = ((0, 24, 0), (24, 24, 1), (48, 48, 2), (96, 24, 4), (120, 24, 5), (144, 24, 6), (168, 96, 7), (264, 24, 11))
+SMALL = ((0, 24, 0), (24, 24, 1), (48, 24, 4), (72, 24, 5), (96, 24, 6), (120, 24, 11), (144, 48, 2), (192, 96, 7))
+SMALL_ORDER = (0, 1, 3, 4, 5, 7, 2, 6)
 SMALL_LEN = 384
 
 
@@ -633,9 +815,9 @@
 
 
 class Gather:
-    def __init__(self, name, links, own, full, sem):
-        self.name, self.links, self.own, self.full, self.sem = name, links, View(own), full, sem
-        p, self.rows = links.peers, own.shape[0]
+    def __init__(self, name, links, own, rows, full, sem):
+        self.name, self.links, self.own, self.rows, self.full, self.sem = name, links, own, rows, full, sem
+        p = links.peers
         self.at = {n: pl.multiple_of(f * self.rows, 8) for n, f in (("f", p.f), ("x", p.fx), ("y", p.fy), ("d", p.fd))}
         self.across = {n: pl.multiple_of((f + 1 - 2 * p.c) * self.rows, 8)
                        for n, f in (("f", p.f), ("x", p.fx), ("y", p.fy), ("d", p.fd))}
@@ -658,69 +840,65 @@
     def local_copy(self):
         return pltpu.make_async_copy(self.own.get(), self.piece(0, "f").get(), self.sem)
 
-    def first(self, ds=(0, 1, 3, 2)):
-        links = self.links
-        for d in ds:
+    def do(self, action):
+        links, kind, d = self.links, action[0], int(action[1:] or 0)
+        if kind == "F":
             piece = self.piece(d, "f")
             if d:
                 links.arrived(self.key("z", d), piece)
             src = piece if d else self.own
             links.start(self.key("x", d), src, piece, "x")
             links.start(self.key("y", d), src, piece, "y")
-        if 2 in ds:
-            self.local_copy().wait()
-            mine = self.column(self.at["f"])
-            links.start(self.key("p", "f"), mine, mine, "p")
-
-    def first_own(self):
-        self.first((0,))
-
-    def first_rest(self):
-        self.first((1, 3, 2))
-
-    def second(self):
-        links = self.links
-        for d in (0, 1, 3, 2):
+            if d == 2:
+                self.local_copy().wait()
+                mine = self.column(self.at["f"])
+                links.start(self.key("p", "f"), mine, mine, "p")
+        elif kind == "S":
             px, py = self.piece(d, "x"), self.piece(d, "y")
             links.arrived(self.key("x", d), px)
             links.arrived(self.key("y", d), py)
-            if d < 2:
-                links.start(self.key("d", d), px, px, "y")
-            else:
-                links.start(self.key("d", d), py, py, "x")
-        for n in ("x", "y"):
-            part = self.column(self.at[n])
-            links.start(self.key("p", n), part, part, "p")
-
-    def third(self):
-        for d in range(4):
-            self.links.arrived(self.key("d", d), self.piece(d, "d"))
-        part = self.column(self.at["d"])
-        self.links.start(self.key("p", "d"), part, part, "p")
-
-    def last(self):
-        for n in ("f", "x", "y", "d"):
-            self.links.arrived(self.key("p", n), self.column(self.across[n]))
+            via, part = ("y", px) if d < 2 else ("x", py)
+            links.start(self.key("d", d), part, part, via)
+            if d == 2:
+                for n in ("x", "y"):
+                    part = self.column(self.at[n])
+                    links.start(self.key("p", n), part, part, "p")
+        elif kind == "T":
+            for n in range(4):
+                links.arrived(self.key("d", n), self.piece(n, "d"))
+            part = self.column(self.at["d"])
+            links.start(self.key("p", "d"), part, part, "p")
+        else:
+            for n in ("f", "x", "y", "d"):
+                links.arrived(self.key("p", n), self.column(self.across[n]))
 
 
 SCATTER_SLOTS = 10
 
 
 class Scatter:
-    def __init__(self, name, links, parts, out, bufs, sem):
-        self.name, self.links, self.parts, self.out, self.sem = name, links, parts, out, sem
+    def __init__(self, name, links, parts, keep, bufs, sem):
+        self.name, self.links, self.parts, self.keep, self.sem = name, links, parts, keep, sem
         self.t, self.p, self.dx, self.dy, self.xr, self.yr, self.zr = bufs
+        p, self.rows = links.peers, self.t.shape[2]
+        self.here, self.there = (pl.multiple_of(c * self.rows, 8) for c in (p.c, p.other))
+
+    def half(self, at):
+        return View(self.parts[0], *self.parts[1:], slice(None), slice(None), pl.ds(at, self.rows))
+
+    def do(self, action):
+        {"B": self.begin, "F": self.first, "S": self.second, "T": self.third, "L": self.last}[action]()
 
     def key(self, *k):
         return (self.name,) + k
 
     def begin(self):
         p = self.links.peers
-        self.links.start(self.key("p"), View(self.parts, slice(None), slice(None), p.other), View(self.p), "p")
+        self.links.start(self.key("p"), self.half(self.there), View(self.p), "p")
         self.local_copy().start()
 
     def local_copy(self):
-        return pltpu.make_async_copy(self.parts.at[:, :, self.links.peers.c], self.t, self.sem)
+        return pltpu.make_async_copy(self.half(self.here).get(), self.t, self.sem)
 
     def add(self, q, zs, ref, base=0):
         t = self.t
@@ -771,7 +949,7 @@
         total = self.t[p.z, p.yx].astype(F32)
         for n in range(3):
             total = total + self.zr[n].astype(F32)
-        self.out[...] = total
+        self.keep(total)
 
 
 def scatter_bufs(rows, cols):
@@ -814,10 +992,7 @@
 
 
 def kernel_prep(small, wqkv, wout, win, wdown, small_o, qkv_o, out_o, in_o, down_o):
-    row, col = small_places(lax.axis_index("dp") * 8 + lax.axis_index("fsdp"))
-    at_row = lax.broadcasted_iota(jnp.int32, (16, SMALL_LEN), 0) == row
-    values = jnp.where(at_row, small[...].astype(BF16).astype(F32), 0.0).astype(BF16)
-    small_o[...] = mm_t(values, small_select(col).astype(BF16)).astype(BF16)
+    small_o[...] = jnp.broadcast_to(small[...], (8, SMALL_LEN)).astype(BF16)
     qkv_o[...] = wqkv[...].astype(BF16)
     out_o[...] = wout[...].astype(BF16)
     in_o[...] = win[...].astype(BF16)
@@ -827,71 +1002,29 @@
 def call_prep(small, weights):
     return pl.pallas_call(
         kernel_prep, name="prep",
-        out_shape=[sds((16, D), BF16)] + [sds(w.shape, BF16) for w in weights],
+        out_shape=[sds((8, SMALL_LEN), BF16)] + [sds(w.shape, BF16) for w in weights],
         in_specs=[VMEM] * 5, out_specs=[VMEM] * 5,
     )(small, *weights)
 
 
-def sum_small(gathered, staged, sem, vecs):
+def build_table(gathered, staged, sem, vecs):
     copy = pltpu.make_async_copy(gathered, staged, sem)
     copy.start()
     copy.wait()
-    total = jnp.zeros((16, D), F32)
-    for i in range(4):
-        for j in range(8):
-            total = total + staged[i, 16 * j : 16 * j + 16, :].astype(F32)
-    vecs[...] = total
-
-
-def kernel_scatter(sums_b, sums_c, out, qkv, small_o, out_o, qkv_o, value, small_b, *rest):
-    bufs, (sems, send, recv) = rest[:14], rest[14:]
-    peers = Peers()
-    links = Links(peers, send, recv)
-    pick = lambda ref, n: jnp.sum(ref[n], axis=0, keepdims=True)
-    rows = [pick(sums_c, n) for n in range(4)] + [pick(sums_b, n) for n in range(1, 9)] + [jnp.zeros((4, D), F32)]
-    value[0] = jnp.concatenate(rows, axis=0)
-    peers.greet()
-    small = SmallSum(links, value, small_b)
-    s = [Scatter(n, links, parts, o, bufs[7 * n : 7 * n + 7], sems.at[n]) for n, (parts, o) in enumerate(((out, out_o), (qkv, qkv_o)))]
-    s[0].begin()
-    s[1].begin()
-    small.send(0, "p")
-    s[0].first()
-    small.take(0)
-    small.send(1, "x")
-    s[1].first()
-    small.take(1)
-    small.send(2, "y")
-    s[0].second()
-    s[1].second()
-    small.take(2)
-    small.spread()
-    s[0].third()
-    s[1].third()
-    total = small.total()
-    row, col = small_places(peers.dev)
-    picked = lax.dot_general(total, small_select(col), (((1,), (0,)), ((), ())),
-                             precision=lax.Precision.HIGHEST, preferred_element_type=F32)
-    at_row = lax.broadcasted_iota(jnp.int32, (16, SMALL_LEN), 0) == row
-    small_o[...] = jnp.sum(jnp.where(at_row, picked, 0.0), axis=0, keepdims=True)
-    s[0].last()
-    s[1].last()
-    links.finish()
-
-
-def call_scatter(sums_b, sums_c, parts):
-    shapes = [(p.shape[0] // 32, p.shape[1]) for p in parts]
-    parts = [p.reshape(4, 4, 2, r, p.shape[1]) for p, (r, _) in zip(parts, shapes)]
-    bufs = [b for s in shapes for b in scatter_bufs(*s)]
-    slots = SCATTER_SLOTS * len(parts) + 6
-    return pl.pallas_call(
-        kernel_scatter, name="scatter",
-        out_shape=[sds((1, SMALL_LEN), F32)] + [sds(s, F32) for s in shapes],
-        in_specs=[VMEM, VMEM] + [ANY] * 2, out_specs=[VMEM] * 3,
-        scratch_shapes=[vm((4, 16, D), F32), vm((6, 16, D), F32)] + bufs
-        + [pltpu.SemaphoreType.DMA((2,)), pltpu.SemaphoreType.DMA((slots,)), pltpu.SemaphoreType.DMA((slots,))],
-        compiler_params=pltpu.CompilerParams(vmem_limit_bytes=VMEM_LIMIT, collective_id=2, has_side_effects=True),
-    )(sums_b, sums_c, *parts)
+    rows = staged[...].reshape(256, SMALL_LEN).astype(F32).T
+    r = lax.broadcasted_iota(jnp.int32, (256, D), 0)
+    lane = lax.broadcasted_iota(jnp.int32, (256, D), 1)
+    vecs[...] = jnp.zeros_like(vecs)
+    for n in (24, 48, 96):
+        part = [(start, base) for start, size, base in SMALL if size == n]
+        values = rows[part[0][0] : part[-1][0] + n, :].astype(BF16)
+        own = lax.broadcasted_iota(jnp.int32, (n, D), 0) == lax.rem(lax.broadcasted_iota(jnp.int32, (n, D), 1), n)
+        for line in range(n // 24):
+            source = ((lane + line * D) // n) * 8
+            spread = mm(values, (r == source).astype(BF16))
+            for m, (_, base) in enumerate(part):
+                picked = jnp.where(own, spread[n * m : n * m + n, :], 0.0)
+                vecs[base + line : base + line + 1, :] = jnp.sum(picked, axis=0, keepdims=True)
 
 
 def gather_all(a):
@@ -937,22 +1070,29 @@
     small = (pre_gain, pre_shift, qv_bias, out_bias, mid_gain, mid_shift, in_bias, down_bias)
     weights = (qkv_weight, out_weight, in_weight, down_weight)
     if own_links:
-        row = jnp.concatenate(small + (jnp.zeros((SMALL_LEN - 288,), F32),)).reshape(1, SMALL_LEN)
-        vecs, made, (wqkv, wout, win, wdown) = call_a_links(sid, hidden_in, time_embed, call_prep(row, weights))
+        ordered = tuple(small[n] for n in SMALL_ORDER)
+        row = jnp.concatenate(ordered + (jnp.zeros((SMALL_LEN - 288,), F32),)).reshape(1, SMALL_LEN)
+        vecs, made, wq, (wout, win, wdown) = call_a_links(sid, hidden_in, time_embed, call_prep(row, weights))
     else:
         vecs, (wqkv, wout, win, wdown) = gather_plain(small, weights)
-        made = call_a(sid, hidden_in, time_embed, vecs, wqkv)
+        wq = [wqkv[:, D * n : D * n + D] for n in range(3)]
+        made = call_a(sid, hidden_in, time_embed, vecs, wq)
     x, a1t, q0, q1, k0, k1, v, kt, o, ot, lse = made
-    block_out, gx1, gb, go0, go1, dots, gdown, gin, sums_b = call_b(sid, x, o, grad_out, vecs, wout, win, wdown)
-    args_c = (sid, x, a1t, q0, q1, k0, k1, v, kt, ot, lse, gx1, gb, go0, go1, dots, vecs, wqkv)
+    block_out, gx1, gb, go0, go1, dots, gdown, gin, sums_b, *more = call_b(own_links, sid, x, o, grad_out, vecs, wout, win, wdown)
+    args_c = (sid, x, a1t, q0, q1, k0, k1, v, kt, ot, lse, gx1, gb, go0, go1, dots, vecs, *wq)
     if own_links:
-        input_grad, time_grad, gqkv, gout, sums_c, gdown, gin = call_c(True, *args_c, gdown, gin)
-        mine, gout, gqkv = call_scatter(sums_b, sums_c, (gout, gqkv))
-        mine = mine.reshape(-1)
+        input_grad, time_grad, _, _, _, gin, gout, gqkv, mine = call_c(True, *args_c, gin, sums_b)
+        gdown = more[0]
+        parts = split_small(mine.reshape(-1), ordered)
+        parts = [parts[SMALL_ORDER.index(n)] for n in range(8)]
     else:
         input_grad, time_grad, gqkv, gout, sums_c = call_c(False, *args_c)
-        mine, (gdown, gin, gout, gqkv) = scatter_plain(sums_b, sums_c, (gdown, gin, gout, gqkv), small)
-    gpg, gps, gqvb, gob, gmg, gms, gib, gdb = split_small(mine, small)
+        gdown = gdown.reshape(D // DT, FF, DT).transpose(1, 0, 2).reshape(FF, D)
+        gin = gin.reshape(4, D, D).transpose(1, 0, 2).reshape(D, FF)
+        gqkv = gqkv.reshape(3, D, 3, D // 3).transpose(1, 2, 0, 3).reshape(D, 3 * D)
+        mine, (gdown, gin, gout, gqkv) = scatter_plain(sums_b, sums_c, (gdown, gin, gout.reshape(D, D), gqkv), small)
+        parts = split_small(mine, small)
+    gpg, gps, gqvb, gob, gmg, gms, gib, gdb = parts
     return (block_out, input_grad, time_grad, gpg, gps, gqkv, gqvb, gout, gob, gmg, gms, gin, gib, gdown, gdb)
 
 

time: 301 us -> 280 us (0.930)
  Pallas kernels: 286 us -> 264 us
    pallas_call x1, Pallas kernels: 105 us -> 87.4 us  [call_a_links(): pl.pallas_call(functools.partial(kernel_a, True), name='part_a', out_shap...]
    pallas_call x3 -> x2, Pallas kernels: 103 us -> 87.3 us  [the longest x1 85.4 us: call_b(): pl.pallas_call(functools.partial(kernel_b, linked), name='part_b', out_sh...]
    pallas_call x1, Pallas kernels: 77.7 us -> 88.9 us  [call_c(): pl.pallas_call(functools.partial(kernel_c, linked), name='part_c', out_sh...]
    unnamed x16 -> x19, local copies, waits for them, and re-layouts: 7.22 us -> 8.96 us
where the time goes in v3:
time: 280 us
  Pallas kernels  264 us (94%)
  local copies, waits for them, and re-layouts  15.6 us (6%)
    pallas_call x1, Pallas kernels, call_c(): pl.pallas_call(functools.partial(kernel_c, linked), name='part_c', out_sh...  88.9 us
    pallas_call x1, Pallas kernels, call_a_links(): pl.pallas_call(functools.partial(kernel_a, True), name='part_a', out_shap...  87.4 us
    pallas_call x1, Pallas kernels, call_b(): pl.pallas_call(functools.partial(kernel_b, linked), name='part_b', out_sh...  85.4 us
    unnamed x19, local copies, waits for them, and re-layouts  8.96 us

profile of v3, /device:TPU:0, one launch (start us, length us, event | category | flops | bytes accessed | tf_op | source)
XLA Modules:
  0.0 279.9 jit_solution(4030345457147845994)
XLA Ops:
  0.7 0.9 concatenate.3
  1.5 0.6 reshape.64.small
  2.1 0.8 reshape.63
  2.8 0.6 slice_reduce_fusion.sid
  3.5 2.0 prep.1
  5.5 87.4 %part_a.1 = (f32[16,768]{1,0:T(8,128)}, f32[1024,768]{1,0:T(8,128)}, bf16[768,1024]{1,0:T(8,128)(2,1)}, bf16[1024,768]{1,0:T(8,128)(2,1)}, bf16[1024,768]{1,0:T(...) custom-call(s32[16]{0:T(128)} %slice_reduce_fusion.sid, ...), custom_call_target="tpu_custom_call" | custom-call | tf_op jit(solution)/shard_map/part_a/pallas_call | solution.py:390
  92.8 85.4 %part_b.1 = (f32[1024,768]{1,0:T(8,128)}, f32[1024,768]{1,0:T(8,128)}, bf16[1024,768]{1,0:T(8,128)(2,1)}, bf16[1024,768]{1,0:T(8,128)(2,1)}, bf16[1024,768]{1,0:...) custom-call(s32[16]{0:T(128)} %slice_reduce_fusion.sid, ...), custom_call_target="tpu_custom_call" | custom-call | tf_op jit(solution)/shard_map/part_b/pallas_call | solution.py:560
  178.2 88.9 %part_c.1 = (f32[1024,768]{1,0:T(8,128)}, f32[16,768]{1,0:T(8,128)}, bf16[3,4,4,48,768]{4,3,2,1,0:T(8,128)(2,1)}, bf16[4,4,48,768]{3,2,1,0:T(8,128)(2,1)}, f32[4...) custom-call(s32[16]{0:T(128)} %slice_reduce_fusion.sid, ...), custom_call_target="tpu_custom_call" | custom-call | tf_op jit(solution)/shard_map/part_c/pallas_call | solution.py:734
  267.1 1.2 slice_bitcast_fusion.5
  268.3 1.2 slice_bitcast_fusion.1
  269.5 1.4 slice_bitcast_fusion
  270.9 3.9 %copy.38 = f32[1024,768]{1,0:T(8,128)} copy(f32[1024,768]{1,0:T(8,128)} %get-tuple-element.112) | data formatting | bytes 6291456
  274.8 0.0 copy-done
  274.8 0.0 copy-start.2
  274.8 0.0 copy-start.1
  274.9 1.7 copy.39
  276.5 0.0 copy-done.5
  276.5 0.6 copy.40
  277.1 0.0 copy-done.3
  277.1 0.7 copy.41
  277.8 0.0 copy-done.4
  277.8 0.6 copy.42
  278.5 0.7 copy.43
  279.2 0.7 copy.44
  (7 shorter events, 0.0 us)
Async XLA Ops:
  270.9 3.9 %copy-start = (f32[1024,768]{1,0:T(8,128)S(1)}, f32[1024,768]{1,0:T(8,128)}, u32[]{:S(2)}) copy-start(f32[1024,768]{1,0:T(8,128)} %get-tuple-element.113) | copy-start | bytes 9437188
  274.8 1.7 copy-start.5
  274.8 2.3 copy-start.3
  274.8 3.0 %copy-start.4 = (f32[24,768]{1,0:T(8,128)S(1)}, f32[24,768]{1,0:T(8,128)}, u32[]{:S(2)}) copy-start(f32[24,768]{1,0:T(8,128)} %get-tuple-element.119) | copy-start | bytes 221188
  274.8 3.6 %copy-start.2 = (f32[24,3072]{1,0:T(8,128)S(1)}, f32[24,3072]{1,0:T(8,128)}, u32[]{:S(2)}) copy-start(f32[24,3072]{1,0:T(8,128)} %get-tuple-element.123) | copy-start | bytes 884740
  274.8 4.3 %copy-start.1 = (f32[96,768]{1,0:T(8,128)S(1)}, f32[96,768]{1,0:T(8,128)}, u32[]{:S(2)}) copy-start(f32[96,768]{1,0:T(8,128)} %get-tuple-element.125) | copy-start | bytes 884740

commit v4 on v3

--- a/solution.py
+++ b/solution.py
@@ -189,92 +189,117 @@
 QB = 256
 
 
-def attention_step(step, q0, q1, k0, k1, vt0, vt1, o, ot, lse):
-    pair, part = step // (BLOCK // QB), step % (BLOCK // QB)
-    lanes, at = rows_at(pair, 128), rows_at(part, QB)
-    outs, logs = [], []
-    for q, k, vt, total_row in ((q0, k0, vt0, 64), (q1, k1, vt1, 0)):
+STEPS = PAIRS * (BLOCK // QB)
+
+
+def step_place(step):
+    return rows_at(step // (BLOCK // QB), 128), rows_at(lax.rem(step, BLOCK // QB), QB)
+
+
+def attention_scores(step, q0, q1, k0, k1, s_ref, m_ref):
+    lanes, at = step_place(step)
+    for h, (q, k) in enumerate(((q0, k0), (q1, k1))):
         scores = mm_t(k[:, lanes], q[at, lanes])
-        top = jnp.max(scores, axis=0, keepdims=True)
-        e = jnp.exp(scores - top).astype(BF16)
+        s_ref[h] = scores
+        m_ref[h : h + 1, :] = jnp.max(scores, axis=0, keepdims=True)
+
+
+def attention_apply(step, s_ref, m_ref, vt0, vt1, o, ot, lse):
+    lanes, at = step_place(step)
+    outs = []
+    for h, (vt, total_row) in enumerate(((vt0, 64), (vt1, 0))):
+        top = m_ref[h : h + 1, :]
+        e = jnp.exp(s_ref[h] - top).astype(BF16)
         res = mm(vt[lanes, :], e)
         total = res[total_row : total_row + 1, :]
         outs.append(res * (1.0 / total))
-        logs.append(top + jnp.log(total))
+        lse[pl.ds(2 * (step // (BLOCK // QB)) + h, 1), at] = top + jnp.log(total)
     both = jnp.where(low_rows((128, QB)), outs[0], outs[1])
     ot[lanes, at] = both.astype(BF16)
     o[at, lanes] = both.T.astype(BF16)
-    lse[pl.ds(2 * pair, 1), at] = logs[0]
-    lse[pl.ds(2 * pair + 1, 1), at] = logs[1]
+
+
+def paired_steps(first, count, slots, ahead, apply, hooks):
+    parity = [{n: a for n, a in hooks.items() if n % 2 == k} for k in range(2)]
+
+    @pl.loop(0, count // 2)
+    def _(i):
+        for k in range(2):
+            step = first + 2 * i + k
+            ahead(jnp.minimum(step + 1, STEPS - 1), slots[1 - k])
+            apply(step, slots[k])
+            run_hooks(step, parity[k])
 
 
 SCHEDULE_A = {
-    ("pre", 0): ("s.F0", "q.F0", "k.F0", "s.F1", "s.F3", "s.F2", "s.S0", "q.F1", "s.S1", "s.S3", "s.S2", "q.F3", "q.F2", "q.S0", "q.S1", "s.T", "k.F1", "q.S3", "k.F3", "s.L",),
-    ("norm", 0): ("q.S2",),
-    ("norm", 1): ("k.F2", "k.S0", "v.F0",),
-    ("norm", 3): ("v.F1",),
-    ("norm", 5): ("k.S1", "v.F3",),
-    ("norm", 6): ("k.S3",),
-    ("norm", 7): ("q.T", "v.F2", "o.F0",),
-    ("q", -1): ("k.S2", "o.F1", "v.S0", "o.F3", "q.L",),
-    ("q", 1): ("v.S1",),
-    ("q", 2): ("o.F2",),
-    ("k", -1): ("v.S3", "v.S2", "i.F0", "o.S0", "k.T", "o.S1", "i.F1", "k.L",),
-    ("k", 1): ("o.S3",),
-    ("v", -1): ("v.T", "o.S2", "i.F3", "v.L",),
-    ("att", 1): ("i.F2", "i.S0", "d.F0",),
-    ("att", 2): ("o.T", "i.S1",),
-    ("att", 4): ("o.L", "d.F1",),
-    ("att", 5): ("i.S3",),
-    ("att", 7): ("i.S2", "d.F3",),
-    ("att", 10): ("d.F2",),
-    ("att", 11): ("d.S0",),
-    ("att", 15): ("d.S1",),
-    ("att", 16): ("i.T",),
-    ("att", 18): ("d.S3",),
-    ("att", 19): ("i.L",),
-    ("att", 20): ("d.S2",),
-    ("end", 0): ("d.T", "d.L",),
+    ("pre", 0): ("s.F0", "q.F0", "k.F0", "s.F1", "s.F3", "s.F2", "s.S0", "q.F1", "s.S1", "q.F3", "s.S3", "s.S2", "q.F2", "q.S0", "q.S1", "k.F1", "k.F3", "q.S3", "s.T", "q.S2", "k.F2", "k.S0", "v.F0", "s.L",),
+    ("norm", 0): ("v.F1",),
+    ("norm", 2): ("v.F3",),
+    ("norm", 3): ("k.S1",),
+    ("norm", 4): ("k.S3", "v.F2", "o.F0",),
+    ("norm", 5): ("q.T",),
+    ("norm", 7): ("k.S2", "o.F1",),
+    ("q", -1): ("o.F3", "v.S0", "v.S1", "q.L",),
+    ("q", 0): ("o.F2",),
+    ("q", 2): ("v.S3",),
+    ("k", -1): ("v.S2", "i.F0", "o.S0", "k.T", "i.F1", "o.S1", "o.S3", "k.L",),
+    ("k", 3): ("o.S2",),
+    ("v", -1): ("v.T", "i.F3", "v.L",),
+    ("att", 0): ("i.F2", "i.S0",),
+    ("att", 2): ("i.S1",),
+    ("att", 3): ("o.T",),
+    ("att", 7): ("o.L",),
+    ("att", 8): ("i.S3",),
+    ("att", 12): ("i.S2",),
+    ("att", 21): ("i.T",),
+    ("end", 0): ("i.L",),
 }
 SCHEDULE_B = {
+    ("pre", 0): ("d.F0",),
+    ("p1", 2): ("d.F1",),
+    ("p1", 3): ("d.F3",),
+    ("p1", 5): ("d.F2", "d.S0", "d.S1",),
+    ("p1", 6): ("d.S3",),
+    ("gd", 0): ("d.S2",),
     ("gd", 1): ("x.B",),
     ("gd", 2): ("y.B",),
-    ("wd", 0): ("z.B",),
-    ("p2", 0): ("x.F", "y.F", "z.F",),
-    ("p2", 1): ("x.S",),
-    ("p2", 3): ("y.S",),
-    ("p2", 4): ("z.S",),
-    ("p2", 6): ("x.T", "y.T",),
-    ("p2", 7): ("z.T",),
-    ("gi", 1): ("x.L",),
-    ("gi", 3): ("y.L",),
+    ("wd", 0): ("z.B", "d.T", "x.F", "y.F", "z.F", "d.L",),
+    ("wd", 1): ("x.S",),
+    ("p2", 1): ("y.S",),
+    ("p2", 2): ("z.S",),
+    ("p2", 4): ("x.T",),
+    ("p2", 5): ("y.T", "z.T",),
+    ("p2", 7): ("x.L",),
+    ("gi", 2): ("y.L",),
     ("end", 0): ("z.L",),
 }
 SCHEDULE_C = {
     ("pre", 0): ("0.B", "1.B", "2.B", "3.B",),
-    ("att", 0): ("0.F", "1.F", "2.F", "3.F",),
-    ("att", 1): ("o.B", "0.S",),
-    ("att", 3): ("o.F", "1.S",),
-    ("att", 4): ("2.S",),
-    ("att", 6): ("3.S",),
-    ("gw", 0): ("0.T",),
-    ("att", 8): ("o.S",),
-    ("att", 9): ("a.B", "1.T",),
-    ("att", 10): ("2.T",),
-    ("att", 11): ("a.F", "o.T", "0.L", "3.T",),
-    ("att", 12): ("1.L",),
-    ("att", 13): ("a.S",),
-    ("att", 14): ("2.L",),
-    ("gw", 1): ("a.T", "o.L",),
-    ("att", 16): ("3.L",),
+    ("att", 0): ("0.F",),
+    ("att", 1): ("o.B", "1.F", "2.F",),
+    ("att", 2): ("3.F",),
+    ("att", 3): ("o.F", "0.S",),
+    ("att", 5): ("1.S",),
+    ("att", 7): ("2.S",),
+    ("att", 8): ("3.S",),
+    ("att", 9): ("a.B",),
+    ("att", 10): ("o.S",),
+    ("att", 12): ("a.F", "0.T",),
+    ("att", 13): ("1.T",),
+    ("att", 14): ("2.T",),
+    ("att", 15): ("3.T",),
+    ("gw", 1): ("o.T",),
+    ("att", 16): ("a.S", "0.L",),
     ("att", 17): ("b.B",),
-    ("att", 19): ("a.L", "b.F",),
-    ("att", 22): ("b.S",),
-    ("gw", 3): ("b.T", "c.B",),
-    ("ln", 1): ("c.F",),
-    ("ln", 2): ("b.L",),
-    ("ln", 3): ("c.S",),
-    ("end", 0): ("c.T", "c.L",),
+    ("att", 18): ("1.L",),
+    ("att", 19): ("a.T",),
+    ("att", 20): ("b.F", "2.L",),
+    ("att", 22): ("3.L",),
+    ("gw", 2): ("b.S", "o.L",),
+    ("gw", 3): ("c.B",),
+    ("ln", 0): ("a.L",),
+    ("ln", 1): ("b.T", "c.F",),
+    ("end", 0): ("c.S", "b.L", "c.T", "c.L",),
 }
 
 
@@ -296,15 +321,15 @@
 
 def kernel_a(linked, sid, hidden, time, *refs):
     if linked:
-        own, refs = refs[:5], refs[5:]
+        own, refs = refs[:4], refs[4:]
         vecs, refs = refs[0], refs[1:]
     else:
         (vecs, *wq), refs = refs[:4], refs[4:]
     (x_h, a1t_h, q0_h, q1_h, k0_h, k1_h, v_h, kt_h, o_h, ot_h, lse), refs = refs[:11], refs[11:]
     if linked:
-        full, refs = refs[:7], refs[7:]
+        full, refs = refs[:6], refs[6:]
         wq = full[1:4]
-    (x, a1, a1t, q0, q1, k0, k1, v, kt, vt0, vt1, o, ot, w, sems), refs = refs[:15], refs[15:]
+    (x, a1, a1t, q0, q1, k0, k1, v, kt, vt0, vt1, o, ot, w, s0, m0, s1, m1, sems), refs = refs[:19], refs[19:]
     mv = Mover(sems)
     cx = mv.start(hidden, x)
     plan = Schedule(SCHEDULE_A)
@@ -313,10 +338,10 @@
         peers = Peers()
         links = Links(peers, send, recv)
         peers.greet()
-        small, qkv, out, inn, down = own
-        pieces = [View(small)] + [View(qkv, slice(None), pl.ds(D * n, D)) for n in range(3)] + [View(out), View(inn), View(down)]
-        rows = (small.shape[0], D // 32, D // 32, D // 32, D // 32, D // 32, FF // 32)
-        for n, name in enumerate("sqkvoid"):
+        small, qkv, out, inn = own
+        pieces = [View(small)] + [View(qkv, slice(None), pl.ds(D * n, D)) for n in range(3)] + [View(out), View(inn)]
+        rows = (small.shape[0],) + 5 * (D // 32,)
+        for n, name in enumerate("sqkvoi"):
             plan.units[name] = Gather(n, links, pieces[n], rows[n], full[n], local_sems.at[n])
             plan.units[name].begin()
     run, hooks = plan.run, plan.hooks
@@ -341,11 +366,16 @@
     outs += [mv.start(v, v_h)]
     attention_hooks = hooks("att")
 
-    @pl.loop(0, PAIRS * (BLOCK // QB))
-    def _(step):
-        attention_step(step, q0, q1, k0, k1, vt0, vt1, o, ot, lse)
-        run_hooks(step, attention_hooks)
-
+    slots = ((s0, m0), (s1, m1))
+
+    def ahead(step, slot):
+        attention_scores(step, q0, q1, k0, k1, *slot)
+
+    def apply(step, slot):
+        attention_apply(step, *slot, vt0, vt1, o, ot, lse)
+
+    ahead(0, slots[0])
+    paired_steps(0, STEPS, slots, ahead, apply, attention_hooks)
     outs += [mv.start(o, o_h), mv.start(ot, ot_h)]
     run("end", 0)
     for copy in outs:
@@ -368,7 +398,7 @@
 
 OUT_A = [sds(TOK, F32), sds(TOKT, BF16)] + [sds(TOK, BF16)] * 5 + [sds(TOKT, BF16), sds(TOK, BF16), sds(TOKT, BF16), sds((16, BLOCK), F32)]
 SCRATCH_A = [vm(TOK, F32), vm(TOK, BF16), vm(TOKT, BF16)] + [vm(TOK, BF16)] * 5 + [vm(TOKT, BF16)] * 3 + [
-    vm(TOK, BF16), vm(TOKT, BF16), vm((3, 4, D // 4, D), BF16), pltpu.SemaphoreType.DMA((16,))]
+    vm(TOK, BF16), vm(TOKT, BF16), vm((3, 4, D // 4, D), BF16)] + 2 * [vm((2, BLOCK, QB), F32), vm((8, QB), F32)] + [pltpu.SemaphoreType.DMA((16,))]
 
 
 def call_a(sid, hidden, time, vecs, wq):
@@ -384,15 +414,15 @@
 
 
 def call_a_links(sid, hidden, time, own):
-    small, qkv, out, inn, down = own
-    sizes = [small.shape] + [(D // 32, D)] * 4 + [inn.shape, down.shape]
-    slots = GATHER_SLOTS * 7
+    small, qkv, out, inn = own
+    sizes = [small.shape] + [(D // 32, D)] * 4 + [inn.shape]
+    slots = GATHER_SLOTS * 6
     res = pl.pallas_call(
         functools.partial(kernel_a, True),
         name="part_a",
         out_shape=[sds((16, D), F32)] + OUT_A + [sds((4, 8 * r, c), BF16) for r, c in sizes],
-        in_specs=[SMEM, ANY, VMEM] + [VMEM] * 5,
-        out_specs=[VMEM] + [ANY] * 10 + [VMEM] + [ANY] * 7,
+        in_specs=[SMEM, ANY, VMEM] + [VMEM] * 4,
+        out_specs=[VMEM] + [ANY] * 10 + [VMEM] + [ANY] * 6,
         scratch_shapes=SCRATCH_A + [vm((4, 64, SMALL_LEN), BF16)] + [pltpu.SemaphoreType.DMA((n,)) for n in (8, slots, slots)],
         compiler_params=pltpu.CompilerParams(vmem_limit_bytes=VMEM_LIMIT, collective_id=1, has_side_effects=True),
     )(sid, hidden, time, *own)
@@ -403,7 +433,7 @@
 def kernel_b(linked, sid, x_h, o_h, gout_h, vecs, wout_h, win_h, wdown_h,
              out_h, gx1_h, gb_h, go0_h, go1_h, dots, gdown_h, gin_h, sums, *refs):
     if linked:
-        gdown_o, refs = refs[0], refs[1:]
+        (gdown_o, down_f), refs = refs[:2], refs[2:]
     (x, o, gy, wout, win, wdown, gm, a2t, ht, h, gu, gb, go0, go1, stage_d, stage, sems), refs = refs[:17], refs[17:]
     plan = Schedule(SCHEDULE_B)
     if linked:
@@ -411,14 +441,18 @@
         peers = Peers()
         links = Links(peers, send, recv)
         peers.greet()
+        plan.units["d"] = Gather(3, links, View(wdown_h), FF // 32, down_f, local_sems.at[3])
+        plan.units["d"].begin()
         for n, name in enumerate("xyz"):
             keep = functools.partial(store_lanes, gdown_o, ((0, DT * n, DT),))
             plan.units[name] = Scatter(n, links, (gdown_h, n), keep, bufs[7 * n : 7 * n + 7], local_sems.at[n])
+        plan.run("pre", 0)
     mv = Mover(sems)
     cx, co, cg = mv.start(x_h, x), mv.start(o_h, o), mv.start(gout_h, gy)
     cwo = mv.start(wout_h, wout)
     cwi = [mv.start(win_h.at[:, pl.ds(D * j, D)], win.at[j]) for j in range(4)]
-    cwd = [mv.start(wdown_h.at[pl.ds(D * j, D), :], wdown.at[j]) for j in range(4)]
+    down_parts = [down_f.at[j] if linked else wdown_h.at[pl.ds(D * j, D), :] for j in range(4)]
+    p1_hooks = [{n: plan.actions("p1", n) for n in range(k, 8, 2)} for k in range(2)]
     sums[...] = jnp.zeros_like(sums)
     for c in [cx, co, cg, cwo] + cwi:
         c.wait()
@@ -455,6 +489,8 @@
             ht[D * j : D * j + D, at] = hf.T.astype(BF16)
             h[at, D * j : D * j + D] = hf.astype(BF16)
             gu[at, D * j : D * j + D] = slope.astype(BF16)
+            if j % 2:
+                run_hooks(2 * i + j // 2, p1_hooks[j // 2])
 
     pending = None
     for t in range(D // DT):
@@ -469,10 +505,12 @@
         plan.run("gd", t)
         pending = pltpu.make_async_copy(stage_d, gdown_h.at[t], so.at[18])
         pending.start()
+    pending.wait()
+    plan.run("wd", 0)
+    cwd = [mv.start(part, wdown.at[j]) for j, part in enumerate(down_parts)]
+    plan.run("wd", 1)
     for c in cwd:
         c.wait()
-    pending.wait()
-    plan.run("wd", 0)
     first_hooks, second_hooks = ({n: plan.actions("p2", n) for n in range(k, 2 * blocks, 2)} for k in range(2))
 
     @pl.loop(0, blocks)
@@ -553,44 +591,51 @@
                vm(TOK, BF16), vm(TOK, BF16), vm(TOK, BF16), vm((4, 4, 192, DT), BF16), vm((2, 4, 4, 48, D), BF16), pltpu.SemaphoreType.DMA((21,))]
     extra = {}
     if linked:
-        out.append(sds((FF // 32, D), F32))
-        out_specs.append(VMEM)
-        scratch += 3 * scatter_bufs(FF // 32, DT) + [pltpu.SemaphoreType.DMA((n,)) for n in (3, 3 * SCATTER_SLOTS, 3 * SCATTER_SLOTS)]
+        out += [sds((FF // 32, D), F32), sds((4, FF // 4, D), BF16)]
+        out_specs += [VMEM, ANY]
+        slots = 3 * SCATTER_SLOTS + GATHER_SLOTS
+        scratch += 3 * scatter_bufs(FF // 32, DT) + [pltpu.SemaphoreType.DMA((n,)) for n in (4, slots, slots)]
         extra = dict(collective_id=2, has_side_effects=True)
     return pl.pallas_call(
         functools.partial(kernel_b, linked),
         name="part_b",
         out_shape=out,
-        in_specs=[SMEM, ANY, ANY, ANY, VMEM, ANY, ANY, ANY],
+        in_specs=[SMEM, ANY, ANY, ANY, VMEM, ANY, ANY, VMEM if linked else ANY],
         out_specs=out_specs,
         scratch_shapes=scratch,
         compiler_params=pltpu.CompilerParams(vmem_limit_bytes=VMEM_LIMIT, **extra),
     )(sid, x, o, gout, vecs, wout, win, wdown)
 
 
-def attention_back_step(step, q0, q1, k0, k1, v, kt, go0, go1, lse, dots, gk_acc, gv_acc, gqkv):
-    parts = BLOCK // QB
-    pair, part = step // parts, step % parts
-    lanes, at = rows_at(pair, 128), rows_at(part, QB)
-    gk_parts, gq_parts, pbs = [], [], []
+def attention_back_scores(step, q0, q1, k0, k1, v, go0, go1, lse, dots, p_ref, g_ref):
+    lanes, at = step_place(step)
+    row = 2 * (step // (BLOCK // QB))
     vv = v[:, lanes]
     for h, (q, k, go) in enumerate(((q0, k0, go0), (q1, k1, go1))):
         scores = mm_t(k[:, lanes], q[at, lanes])
-        p = jnp.exp(scores - lse[pl.ds(2 * pair + h, 1), at])
+        p = jnp.exp(scores - lse[pl.ds(row + h, 1), at])
         gp = mm_t(vv, go[at, lanes])
-        gs = (p * (gp - dots[pl.ds(2 * pair + h, 1), at])).astype(BF16)
-        pbs.append(mm(p.astype(BF16), go[at, lanes]))
-        gk_parts.append(mm(gs, q[at, lanes]))
-        gq_parts.append(mm(kt[lanes, :], gs))
+        g_ref[h] = (p * (gp - dots[pl.ds(row + h, 1), at])).astype(BF16)
+        p_ref[h] = p.astype(BF16)
+
+
+def attention_back_apply(step, p_ref, g_ref, q0, q1, kt, go0, go1, gk_acc, gv_acc, gqkv):
+    lanes, at = step_place(step)
+    part = lax.rem(step, BLOCK // QB)
+    gk_parts, gq_parts, gv_parts = [], [], []
+    for h, (q, go) in enumerate(((q0, go0), (q1, go1))):
+        gv_parts.append(mm(p_ref[h], go[at, lanes]))
+        gk_parts.append(mm(g_ref[h], q[at, lanes]))
+        gq_parts.append(mm(kt[lanes, :], g_ref[h]))
     gk = jnp.where(low_lanes((BLOCK, 128)), gk_parts[0], gk_parts[1])
-    gv = pbs[0] + pbs[1]
+    gv = gv_parts[0] + gv_parts[1]
     gq = jnp.where(low_rows((128, QB)), gq_parts[0], gq_parts[1]) * (HEAD_DIM**-0.5)
     gqkv[0, at, lanes] = gq.T.astype(BF16)
     first = part == 0
     gk_acc[...] = jnp.where(first, gk, gk_acc[...] + gk)
     gv_acc[...] = jnp.where(first, gv, gv_acc[...] + gv)
 
-    @pl.when(part == parts - 1)
+    @pl.when(part == BLOCK // QB - 1)
     def _():
         gqkv[1, :, lanes] = gk_acc[...].astype(BF16)
         gqkv[2, :, lanes] = gv_acc[...].astype(BF16)
@@ -605,7 +650,7 @@
     (ig_h, tg, gqkv_h, gwo_h, sums), refs = refs[:5], refs[5:]
     if linked:
         (gin_o, gout_o, gqkv_o, small_o), refs = refs[:4], refs[4:]
-    (x, a1t, q0, q1, k0, k1, v, kt, ot, gx1, gb, go0, go1, w, gqkv, gk_acc, gv_acc, gw, gwo, tsum, sems), refs = refs[:21], refs[21:]
+    (x, a1t, q0, q1, k0, k1, v, kt, ot, gx1, gb, go0, go1, w, gqkv, gk_acc, gv_acc, gw, gwo, tsum, p0, g0, p1, g1, sems), refs = refs[:25], refs[25:]
     plan = Schedule(SCHEDULE_C)
     if linked:
         bufs, (value, small_b, local_sems, send, recv) = refs[:56], refs[56:]
@@ -641,24 +686,30 @@
     gwo_copy.wait()
     plan.run("gwo", 0)
     steps = 2 * (BLOCK // QB)
-    gw_copies = []
-    for chunk in range(3):
-        hooks = plan.hooks("att", steps * chunk, steps * chunk + steps)
-
-        @pl.loop(steps * chunk, steps * chunk + steps)
-        def _(step):
-            attention_back_step(step, q0, q1, k0, k1, v, kt, go0, go1, lse, dots, gk_acc, gv_acc, gqkv)
-            run_hooks(step, hooks)
-
-        if chunk == 0:
-            late[0].wait()
+    slots = ((p0, g0), (p1, g1))
+
+    def ahead(step, slot):
+        attention_back_scores(step, q0, q1, k0, k1, v, go0, go1, lse, dots, *slot)
+
+    def apply(step, slot):
+        attention_back_apply(step, *slot, q0, q1, kt, go0, go1, gk_acc, gv_acc, gqkv)
+
+    ahead(0, slots[0])
+    late[0].wait()
+    step_hooks, chunk_hooks = plan.hooks("att"), plan.hooks("gw", 0, 3)
+
+    @pl.loop(0, 3)
+    def _(chunk):
+        paired_steps(steps * chunk, steps, slots, ahead, apply, step_hooks)
         for j in range(3):
             for r in range(2):
-                part = mm(a1t[384 * r : 384 * r + 384, :], gqkv[j, :, 256 * chunk : 256 * chunk + 256]).astype(BF16)
+                part = mm(a1t[384 * r : 384 * r + 384, :], gqkv[j, :, rows_at(chunk, 256)]).astype(BF16)
                 gw[chunk, 2 * r : 2 * r + 2, :, :, 256 * j : 256 * j + 256] = part.reshape(2, 4, 48, 256)
-        gw_copies.append(mv.start(gw.at[chunk], gqkv_h.at[chunk]))
-        plan.run("gw", chunk)
-        gw_copies[chunk].wait()
+        copy = pltpu.make_async_copy(gw.at[chunk], gqkv_h.at[chunk], sems.at[23])
+        copy.start()
+        run_hooks(chunk, chunk_hooks)
+        copy.wait()
+
     for c in late[1:]:
         c.wait()
     plan.run("gw", 3)
@@ -720,7 +771,7 @@
     out_specs = [ANY, VMEM, ANY, ANY, VMEM]
     scratch = [vm(TOK, F32), vm(TOKT, BF16)] + [vm(TOK, BF16)] * 5 + [vm(TOKT, BF16)] * 2 + [vm(TOK, F32)] + [vm(TOK, BF16)] * 3
     scratch += [vm((3, D, D), BF16), vm((3, BLOCK, D), BF16), vm((BLOCK, 128), F32), vm((BLOCK, 128), F32), vm((3, 4, 4, 48, D), BF16), vm((4, 4, 48, D), BF16),
-                vm((GROUPS, D), F32), pltpu.SemaphoreType.DMA((24,))]
+                vm((GROUPS, D), F32)] + 4 * [vm((2, BLOCK, QB), BF16)] + [pltpu.SemaphoreType.DMA((24,))]
     extra = {}
     if linked:
         in_specs += [ANY, VMEM]
@@ -1072,7 +1123,9 @@
     if own_links:
         ordered = tuple(small[n] for n in SMALL_ORDER)
         row = jnp.concatenate(ordered + (jnp.zeros((SMALL_LEN - 288,), F32),)).reshape(1, SMALL_LEN)
-        vecs, made, wq, (wout, win, wdown) = call_a_links(sid, hidden_in, time_embed, call_prep(row, weights))
+        own = call_prep(row, weights)
+        vecs, made, wq, (wout, win) = call_a_links(sid, hidden_in, time_embed, own[:4])
+        wdown = own[4]
     else:
         vecs, (wqkv, wout, win, wdown) = gather_plain(small, weights)
         wq = [wqkv[:, D * n : D * n + D] for n in range(3)]

time: 280 us -> 250 us (0.89)
  Pallas kernels: 264 us -> 233 us
    pallas_call x1, Pallas kernels: 87.4 us -> 67.2 us  [call_a_links(): pl.pallas_call(functools.partial(kernel_a, True), name='part_a', out_shap...]
    pallas_call x1, Pallas kernels: 88.9 us -> 83.6 us  [call_c(): pl.pallas_call(functools.partial(kernel_c, linked), name='part_c', out_sh...]
    pallas_call x1, Pallas kernels: 85.4 us -> 80.2 us  [call_b(): pl.pallas_call(functools.partial(kernel_b, linked), name='part_b', out_sh...]
where the time goes in v4:
time: 250 us; the launch traced here: 249 us
  Pallas kernels  233 us (93%)
  local copies, waits for them, and re-layouts  15.6 us (6%)
    pallas_call x1, Pallas kernels, call_c(): pl.pallas_call(functools.partial(kernel_c, linked), name='part_c', out_sh...  83.6 us
    pallas_call x1, Pallas kernels, call_b(): pl.pallas_call(functools.partial(kernel_b, linked), name='part_b', out_sh...  80.2 us
    pallas_call x1, Pallas kernels, call_a_links(): pl.pallas_call(functools.partial(kernel_a, True), name='part_a', out_shap...  67.2 us
    unnamed x19, local copies, waits for them, and re-layouts  8.96 us

profile of v4, /device:TPU:0, one launch (start us, length us, event | category | flops | bytes accessed | tf_op | source)
XLA Modules:
  0.0 249.3 jit_solution(7329193293464472908)
XLA Ops:
  0.7 0.9 concatenate.3
  1.5 0.6 reshape.61.small
  2.1 0.8 reshape.60
  2.8 0.6 slice_reduce_fusion.sid
  3.5 2.0 prep.1
  5.5 67.2 %part_a.1 = (f32[16,768]{1,0:T(8,128)}, f32[1024,768]{1,0:T(8,128)}, bf16[768,1024]{1,0:T(8,128)(2,1)}, bf16[1024,768]{1,0:T(8,128)(2,1)}, bf16[1024,768]{1,0:T(...) custom-call(s32[16]{0:T(128)} %slice_reduce_fusion.sid, ...), custom_call_target="tpu_custom_call" | custom-call | tf_op jit(solution)/shard_map/part_a/pallas_call | solution.py:420
  72.7 80.2 %part_b.1 = (f32[1024,768]{1,0:T(8,128)}, f32[1024,768]{1,0:T(8,128)}, bf16[1024,768]{1,0:T(8,128)(2,1)}, bf16[1024,768]{1,0:T(8,128)(2,1)}, bf16[1024,768]{1,0:...) custom-call(s32[16]{0:T(128)} %slice_reduce_fusion.sid, ...), custom_call_target="tpu_custom_call" | custom-call | tf_op jit(solution)/shard_map/part_b/pallas_call | solution.py:599
  152.9 83.6 %part_c.1 = (f32[1024,768]{1,0:T(8,128)}, f32[16,768]{1,0:T(8,128)}, bf16[3,4,4,48,768]{4,3,2,1,0:T(8,128)(2,1)}, bf16[4,4,48,768]{3,2,1,0:T(8,128)(2,1)}, f32[4...) custom-call(s32[16]{0:T(128)} %slice_reduce_fusion.sid, ...), custom_call_target="tpu_custom_call" | custom-call | tf_op jit(solution)/shard_map/part_c/pallas_call | solution.py:785
  236.5 1.2 slice_bitcast_fusion.5
  237.7 1.2 slice_bitcast_fusion.1
  238.9 1.4 slice_bitcast_fusion
  240.3 3.9 %copy.38 = f32[1024,768]{1,0:T(8,128)} copy(f32[1024,768]{1,0:T(8,128)} %get-tuple-element.110) | data formatting | bytes 6291456
  244.2 0.0 copy-done
  244.2 0.0 copy-start.2
  244.3 0.0 copy-start.1
  244.3 1.7 copy.39
  245.9 0.0 copy-done.5
  245.9 0.6 copy.40
  246.6 0.0 copy-done.3
  246.6 0.7 copy.41
  247.2 0.0 copy-done.4
  247.2 0.6 copy.42
  247.9 0.7 copy.43
  248.6 0.7 copy.44
  (7 shorter events, 0.0 us)
Async XLA Ops:
  240.3 3.9 %copy-start = (f32[1024,768]{1,0:T(8,128)S(1)}, f32[1024,768]{1,0:T(8,128)}, u32[]{:S(2)}) copy-start(f32[1024,768]{1,0:T(8,128)} %get-tuple-element.111) | copy-start | bytes 9437188
  244.2 1.7 copy-start.5
  244.2 2.3 copy-start.3
  244.2 3.0 %copy-start.4 = (f32[24,768]{1,0:T(8,128)S(1)}, f32[24,768]{1,0:T(8,128)}, u32[]{:S(2)}) copy-start(f32[24,768]{1,0:T(8,128)} %get-tuple-element.117) | copy-start | bytes 221188
  244.2 3.6 %copy-start.2 = (f32[24,3072]{1,0:T(8,128)S(1)}, f32[24,3072]{1,0:T(8,128)}, u32[]{:S(2)}) copy-start(f32[24,3072]{1,0:T(8,128)} %get-tuple-element.121) | copy-start | bytes 884740
  244.3 4.3 %copy-start.1 = (f32[96,768]{1,0:T(8,128)S(1)}, f32[96,768]{1,0:T(8,128)}, u32[]{:S(2)}) copy-start(f32[96,768]{1,0:T(8,128)} %get-tuple-element.123) | copy-start | bytes 884740

commit v5 on v4

--- a/solution.py
+++ b/solution.py
@@ -67,15 +67,15 @@
 
 
 def gelu_parts(u):
-    z = jnp.abs(u) * 0.7071067811865476
-    t = 1.0 / (1.0 + ERFC_SCALE * z)
-    poly = jnp.full_like(t, ERFC_POLY[-1])
-    for c in ERFC_POLY[-2::-1]:
-        poly = poly * t + c
-    e = jnp.exp(-(z * z))
-    tail = 0.5 * poly * t * e
-    phi = jnp.where(u >= 0, 1.0 - tail, tail)
-    return u * phi, phi + u * e * 0.3989422804014327
+    v = jnp.abs(u)
+    t = 1.0 / (1.0 + (ERFC_SCALE * 0.7071067811865476) * v)
+    poly = t * (0.5 * ERFC_POLY[-1]) + 0.5 * ERFC_POLY[-2]
+    for c in ERFC_POLY[-3::-1]:
+        poly = poly * t + 0.5 * c
+    e = jnp.exp2((u * u) * -0.7213475204444817)
+    tail = poly * t * e
+    inner = tail - v * e * 0.3989422804014327
+    return jnp.maximum(u, 0.0) - v * tail, jnp.where(u >= 0, 1.0 - inner, inner)
 
 
 class Mover:
@@ -141,48 +141,30 @@
     return lax.broadcasted_iota(jnp.int32, shape, 0) < 64
 
 
-def stage_q(sid, vecs, a1, w, q0, q1, hooks):
+def stage_qkv(c, sid, vecs, a1, w, q0, q1, k0, k1, kt, v, vt0, vt1, hooks):
+    lo = 256 * c
+
     @pl.loop(0, BLOCK // TB)
     def _(i):
         at = rows_at(i, TB)
-        mq, _ = mask_rows(sid, i, TB // SHORT)
-        acc = mm(a1[at, :], w) + vecs[2:3, :]
-        acc = acc.astype(BF16).astype(F32) * (HEAD_DIM**-0.5)
-        low = low_lanes((TB, 128))
-        for p in range(PAIRS):
-            part = acc[:, 128 * p : 128 * p + 128]
-            q0[at, 128 * p : 128 * p + 128] = jnp.where(low, part, mq).astype(BF16)
-            q1[at, 128 * p : 128 * p + 128] = jnp.where(low, mq, part).astype(BF16)
-        run_hooks(i, hooks)
-
-
-def stage_k(sid, a1, w, k0, k1, kt, hooks):
-    @pl.loop(0, BLOCK // TB)
-    def _(i):
-        at = rows_at(i, TB)
-        _, mk = mask_rows(sid, i, TB // SHORT)
+        mq, mk = mask_rows(sid, i, TB // SHORT)
         acc = mm(a1[at, :], w)
-        low = low_lanes((TB, 128))
-        for p in range(PAIRS):
-            part = acc[:, 128 * p : 128 * p + 128]
-            k0[at, 128 * p : 128 * p + 128] = jnp.where(low, part, mk).astype(BF16)
-            k1[at, 128 * p : 128 * p + 128] = jnp.where(low, mk, part).astype(BF16)
-        kt[:, at] = acc.T.astype(BF16)
-        run_hooks(i, hooks)
-
-
-def stage_v(vecs, a1, w, v, vt0, vt1, hooks):
-    @pl.loop(0, BLOCK // TB)
-    def _(i):
-        at = rows_at(i, TB)
-        acc = mm(a1[at, :], w) + vecs[3:4, :]
-        v[at, :] = acc.astype(BF16)
-        accT = acc.T
-        low = low_rows((128, TB))
-        for p in range(PAIRS):
-            part = accT[128 * p : 128 * p + 128, :]
-            vt0[128 * p : 128 * p + 128, at] = jnp.where(low, part, 1.0).astype(BF16)
-            vt1[128 * p : 128 * p + 128, at] = jnp.where(low, 1.0, part).astype(BF16)
+        q = (acc[:, :256] + vecs[2:3, lo : lo + 256]).astype(BF16).astype(F32) * (HEAD_DIM**-0.5)
+        k = acc[:, 256:512]
+        value = acc[:, 512:] + vecs[3:4, lo : lo + 256]
+        kt[lo : lo + 256, at] = k.T.astype(BF16)
+        v[at, lo : lo + 256] = value.astype(BF16)
+        value_t = value.T
+        low, low_t = low_lanes((TB, 128)), low_rows((128, TB))
+        for p in range(2):
+            here = slice(128 * p, 128 * p + 128)
+            to = slice(lo + 128 * p, lo + 128 * p + 128)
+            q0[at, to] = jnp.where(low, q[:, here], mq).astype(BF16)
+            q1[at, to] = jnp.where(low, mq, q[:, here]).astype(BF16)
+            k0[at, to] = jnp.where(low, k[:, here], mk).astype(BF16)
+            k1[at, to] = jnp.where(low, mk, k[:, here]).astype(BF16)
+            vt0[to, at] = jnp.where(low_t, value_t[here, :], 1.0).astype(BF16)
+            vt1[to, at] = jnp.where(low_t, 1.0, value_t[here, :]).astype(BF16)
         run_hooks(i, hooks)
 
 
@@ -219,86 +201,86 @@
     o[at, lanes] = both.T.astype(BF16)
 
 
-def paired_steps(first, count, slots, ahead, apply, hooks):
+def paired_steps(first, count, end, slots, ahead, apply, hooks):
     parity = [{n: a for n, a in hooks.items() if n % 2 == k} for k in range(2)]
 
     @pl.loop(0, count // 2)
     def _(i):
         for k in range(2):
             step = first + 2 * i + k
-            ahead(jnp.minimum(step + 1, STEPS - 1), slots[1 - k])
+            ahead(jnp.minimum(step + 1, end - 1), slots[1 - k])
             apply(step, slots[k])
             run_hooks(step, parity[k])
 
 
 SCHEDULE_A = {
     ("pre", 0): ("s.F0", "q.F0", "k.F0", "s.F1", "s.F3", "s.F2", "s.S0", "q.F1", "s.S1", "q.F3", "s.S3", "s.S2", "q.F2", "q.S0", "q.S1", "k.F1", "k.F3", "q.S3", "s.T", "q.S2", "k.F2", "k.S0", "v.F0", "s.L",),
-    ("norm", 0): ("v.F1",),
-    ("norm", 2): ("v.F3",),
-    ("norm", 3): ("k.S1",),
-    ("norm", 4): ("k.S3", "v.F2", "o.F0",),
-    ("norm", 5): ("q.T",),
-    ("norm", 7): ("k.S2", "o.F1",),
-    ("q", -1): ("o.F3", "v.S0", "v.S1", "q.L",),
-    ("q", 0): ("o.F2",),
-    ("q", 2): ("v.S3",),
-    ("k", -1): ("v.S2", "i.F0", "o.S0", "k.T", "i.F1", "o.S1", "o.S3", "k.L",),
-    ("k", 3): ("o.S2",),
-    ("v", -1): ("v.T", "i.F3", "v.L",),
-    ("att", 0): ("i.F2", "i.S0",),
-    ("att", 2): ("i.S1",),
-    ("att", 3): ("o.T",),
-    ("att", 7): ("o.L",),
-    ("att", 8): ("i.S3",),
-    ("att", 12): ("i.S2",),
+    ("pre", 1): ("v.F1",),
+    ("norm", 1): ("v.F3", "k.S1",),
+    ("norm", 3): ("k.S3", "v.F2", "o.F0",),
+    ("norm", 4): ("q.T",),
+    ("norm", 5): ("o.F1",),
+    ("norm", 6): ("k.S2",),
+    ("q", -1): ("v.S0", "o.F3", "v.S1", "o.F2", "q.L",),
+    ("q", 0): ("v.S3",),
+    ("q", 2): ("v.S2", "i.F0",),
+    ("q", 3): ("o.S0",),
+    ("att", 0): ("k.T", "o.S1", "i.F1",),
+    ("att", 2): ("o.S3",),
+    ("att", 4): ("k.L", "v.T", "o.S2",),
+    ("att", 6): ("i.F3",),
+    ("k", 0): ("v.L",),
+    ("k", 2): ("i.F2", "i.S0",),
+    ("att", 9): ("o.T", "i.S1",),
+    ("att", 13): ("o.L", "i.S3",),
+    ("v", 0): ("i.S2",),
+    ("att", 17): ("d.Z",),
     ("att", 21): ("i.T",),
     ("end", 0): ("i.L",),
 }
 SCHEDULE_B = {
-    ("pre", 0): ("d.F0",),
-    ("p1", 2): ("d.F1",),
-    ("p1", 3): ("d.F3",),
-    ("p1", 5): ("d.F2", "d.S0", "d.S1",),
-    ("p1", 6): ("d.S3",),
-    ("gd", 0): ("d.S2",),
-    ("gd", 1): ("x.B",),
+    ("pre", 0): ("d.F0", "d.F1", "d.F3", "d.F2",),
+    ("p1", 1): ("d.S0",),
+    ("p1", 2): ("d.S1",),
+    ("p1", 3): ("d.S3",),
+    ("p1", 4): ("d.S2",),
+    ("p1", 7): ("d.T",),
+    ("gd", 1): ("d.L", "x.B",),
     ("gd", 2): ("y.B",),
-    ("wd", 0): ("z.B", "d.T", "x.F", "y.F", "z.F", "d.L",),
-    ("wd", 1): ("x.S",),
-    ("p2", 1): ("y.S",),
-    ("p2", 2): ("z.S",),
-    ("p2", 4): ("x.T",),
-    ("p2", 5): ("y.T", "z.T",),
-    ("p2", 7): ("x.L",),
-    ("gi", 2): ("y.L",),
-    ("end", 0): ("z.L",),
+    ("p2", 0): ("x.F", "y.F",),
+    ("p2", 2): ("x.S",),
+    ("p2", 4): ("y.S",),
+    ("p2", 5): ("x.T",),
+    ("p2", 6): ("y.T",),
+    ("gi", 1): ("x.L",),
+    ("end", 0): ("y.L",),
 }
 SCHEDULE_C = {
-    ("pre", 0): ("0.B", "1.B", "2.B", "3.B",),
-    ("att", 0): ("0.F",),
-    ("att", 1): ("o.B", "1.F", "2.F",),
-    ("att", 2): ("3.F",),
-    ("att", 3): ("o.F", "0.S",),
-    ("att", 5): ("1.S",),
-    ("att", 7): ("2.S",),
-    ("att", 8): ("3.S",),
+    ("pre", 0): ("z.B", "0.B", "1.B", "2.B", "3.B",),
+    ("att", 0): ("z.F",),
+    ("att", 1): ("o.B", "0.F",),
+    ("att", 2): ("1.F", "2.F",),
+    ("att", 3): ("z.S", "3.F", "o.F",),
+    ("att", 5): ("0.S",),
+    ("att", 7): ("1.S",),
+    ("att", 8): ("2.S",),
     ("att", 9): ("a.B",),
-    ("att", 10): ("o.S",),
-    ("att", 12): ("a.F", "0.T",),
-    ("att", 13): ("1.T",),
-    ("att", 14): ("2.T",),
-    ("att", 15): ("3.T",),
-    ("gw", 1): ("o.T",),
-    ("att", 16): ("a.S", "0.L",),
-    ("att", 17): ("b.B",),
-    ("att", 18): ("1.L",),
-    ("att", 19): ("a.T",),
-    ("att", 20): ("b.F", "2.L",),
-    ("att", 22): ("3.L",),
-    ("gw", 2): ("b.S", "o.L",),
+    ("att", 11): ("z.T",),
+    ("att", 12): ("a.F", "3.S",),
+    ("att", 14): ("o.S",),
+    ("gw", 1): ("0.T",),
+    ("att", 16): ("z.L", "1.T",),
+    ("att", 17): ("b.B", "2.T",),
+    ("att", 18): ("a.S",),
+    ("att", 20): ("b.F", "0.L", "3.T",),
+    ("att", 21): ("o.T",),
+    ("att", 22): ("a.T", "1.L",),
+    ("att", 23): ("b.S",),
+    ("gw", 2): ("2.L",),
     ("gw", 3): ("c.B",),
-    ("ln", 0): ("a.L",),
-    ("ln", 1): ("b.T", "c.F",),
+    ("ln", 0): ("3.L",),
+    ("ln", 1): ("b.T", "c.F", "o.L",),
+    ("ln", 3): ("a.L",),
     ("end", 0): ("c.S", "b.L", "c.T", "c.L",),
 }
 
@@ -321,13 +303,13 @@
 
 def kernel_a(linked, sid, hidden, time, *refs):
     if linked:
-        own, refs = refs[:4], refs[4:]
+        own, refs = refs[:5], refs[5:]
         vecs, refs = refs[0], refs[1:]
     else:
         (vecs, *wq), refs = refs[:4], refs[4:]
     (x_h, a1t_h, q0_h, q1_h, k0_h, k1_h, v_h, kt_h, o_h, ot_h, lse), refs = refs[:11], refs[11:]
     if linked:
-        full, refs = refs[:6], refs[6:]
+        full, refs = refs[:7], refs[7:]
         wq = full[1:4]
     (x, a1, a1t, q0, q1, k0, k1, v, kt, vt0, vt1, o, ot, w, s0, m0, s1, m1, sems), refs = refs[:19], refs[19:]
     mv = Mover(sems)
@@ -338,16 +320,18 @@
         peers = Peers()
         links = Links(peers, send, recv)
         peers.greet()
-        small, qkv, out, inn = own
-        pieces = [View(small)] + [View(qkv, slice(None), pl.ds(D * n, D)) for n in range(3)] + [View(out), View(inn)]
-        rows = (small.shape[0],) + 5 * (D // 32,)
-        for n, name in enumerate("sqkvoi"):
-            plan.units[name] = Gather(n, links, pieces[n], rows[n], full[n], local_sems.at[n])
+        small, qkv, out, inn, down = own
+        pieces = [View(small)] + [View(qkv, slice(None), pl.ds(D * n, D)) for n in range(3)] + [View(out), View(inn), View(down)]
+        rows = (small.shape[0],) + 5 * (D // 32,) + (FF // 32,)
+        for n, name in enumerate("sqkvoid"):
+            kind = Line if name == "d" else Gather
+            plan.units[name] = kind(n, links, pieces[n], rows[n], full[n], local_sems.at[n])
             plan.units[name].begin()
     run, hooks = plan.run, plan.hooks
     run("pre", 0)
     if linked:
         build_table(full[0], staged, local_sems.at[7], vecs)
+    run("pre", 1)
     cx.wait()
     stage_norm1(sid, time, vecs, x, a1, a1t, hooks("norm"))
     outs = [mv.start(x, x_h), mv.start(a1t, a1t_h)]
@@ -358,14 +342,6 @@
         copy.wait()
         return w[j].reshape(D, D)
 
-    stage_q(sid, vecs, a1, weight("q", 0), q0, q1, hooks("q"))
-    outs += [mv.start(q0, q0_h), mv.start(q1, q1_h)]
-    stage_k(sid, a1, weight("k", 1), k0, k1, kt, hooks("k"))
-    outs += [mv.start(k0, k0_h), mv.start(k1, k1_h), mv.start(kt, kt_h)]
-    stage_v(vecs, a1, weight("v", 2), v, vt0, vt1, hooks("v"))
-    outs += [mv.start(v, v_h)]
-    attention_hooks = hooks("att")
-
     slots = ((s0, m0), (s1, m1))
 
     def ahead(step, slot):
@@ -374,8 +350,13 @@
     def apply(step, slot):
         attention_apply(step, *slot, vt0, vt1, o, ot, lse)
 
-    ahead(0, slots[0])
-    paired_steps(0, STEPS, slots, ahead, apply, attention_hooks)
+    steps = STEPS // 3
+    for c, name in enumerate("qkv"):
+        stage_qkv(c, sid, vecs, a1, weight(name, c), q0, q1, k0, k1, kt, v, vt0, vt1, hooks(name))
+        if c == 2:
+            outs += [mv.start(a, b) for a, b in ((q0, q0_h), (q1, q1_h), (k0, k0_h), (k1, k1_h), (kt, kt_h), (v, v_h))]
+        ahead(steps * c, slots[0])
+        paired_steps(steps * c, steps, steps * (c + 1), slots, ahead, apply, plan.hooks("att", steps * c, steps * (c + 1)))
     outs += [mv.start(o, o_h), mv.start(ot, ot_h)]
     run("end", 0)
     for copy in outs:
@@ -414,36 +395,35 @@
 
 
 def call_a_links(sid, hidden, time, own):
-    small, qkv, out, inn = own
+    small, qkv, out, inn, down = own
     sizes = [small.shape] + [(D // 32, D)] * 4 + [inn.shape]
-    slots = GATHER_SLOTS * 6
+    slots = GATHER_SLOTS * 7
     res = pl.pallas_call(
         functools.partial(kernel_a, True),
         name="part_a",
-        out_shape=[sds((16, D), F32)] + OUT_A + [sds((4, 8 * r, c), BF16) for r, c in sizes],
-        in_specs=[SMEM, ANY, VMEM] + [VMEM] * 4,
-        out_specs=[VMEM] + [ANY] * 10 + [VMEM] + [ANY] * 6,
+        out_shape=[sds((16, D), F32)] + OUT_A + [sds((4, 8 * r, c), BF16) for r, c in sizes] + [sds((4, FF // 32, D), BF16)],
+        in_specs=[SMEM, ANY, VMEM] + [VMEM] * 5,
+        out_specs=[VMEM] + [ANY] * 10 + [VMEM] + [ANY] * 7,
         scratch_shapes=SCRATCH_A + [vm((4, 64, SMALL_LEN), BF16)] + [pltpu.SemaphoreType.DMA((n,)) for n in (8, slots, slots)],
         compiler_params=pltpu.CompilerParams(vmem_limit_bytes=VMEM_LIMIT, collective_id=1, has_side_effects=True),
     )(sid, hidden, time, *own)
-    full = [a.reshape(-1, a.shape[-1]) for a in res[13:]]
-    return res[0], res[1:12], full[:3], full[3:]
+    full = [a.reshape(-1, a.shape[-1]) for a in res[13:18]]
+    return res[0], res[1:12], full[:3], full[3:], res[18]
 
 
 def kernel_b(linked, sid, x_h, o_h, gout_h, vecs, wout_h, win_h, wdown_h,
              out_h, gx1_h, gb_h, go0_h, go1_h, dots, gdown_h, gin_h, sums, *refs):
     if linked:
         (gdown_o, down_f), refs = refs[:2], refs[2:]
-    (x, o, gy, wout, win, wdown, gm, a2t, ht, h, gu, gb, go0, go1, stage_d, stage, sems), refs = refs[:17], refs[17:]
+    (x, o, gy, wout, win, wdown, gm, a2t, ht, h, gu, gb, go0, go1, stage_d, stage, *u_refs, sems), refs = refs[:19], refs[19:]
     plan = Schedule(SCHEDULE_B)
     if linked:
-        bufs, (local_sems, send, recv) = refs[:21], refs[21:]
+        bufs, (local_sems, send, recv) = refs[:14], refs[14:]
         peers = Peers()
         links = Links(peers, send, recv)
         peers.greet()
-        plan.units["d"] = Gather(3, links, View(wdown_h), FF // 32, down_f, local_sems.at[3])
-        plan.units["d"].begin()
-        for n, name in enumerate("xyz"):
+        plan.units["d"] = Plane(3, links, View(wdown_h), FF // 32, down_f, local_sems.at[3])
+        for n, name in enumerate("xy"):
             keep = functools.partial(store_lanes, gdown_o, ((0, DT * n, DT),))
             plan.units[name] = Scatter(n, links, (gdown_h, n), keep, bufs[7 * n : 7 * n + 7], local_sems.at[n])
         plan.run("pre", 0)
@@ -451,7 +431,6 @@
     cx, co, cg = mv.start(x_h, x), mv.start(o_h, o), mv.start(gout_h, gy)
     cwo = mv.start(wout_h, wout)
     cwi = [mv.start(win_h.at[:, pl.ds(D * j, D)], win.at[j]) for j in range(4)]
-    down_parts = [down_f.at[j] if linked else wdown_h.at[pl.ds(D * j, D), :] for j in range(4)]
     p1_hooks = [{n: plan.actions("p1", n) for n in range(k, 8, 2)} for k in range(2)]
     sums[...] = jnp.zeros_like(sums)
     for c in [cx, co, cg, cwo] + cwi:
@@ -464,8 +443,8 @@
 
     def out_copies(i):
         at = rows_at(i, TB)
-        return [pltpu.make_async_copy(x.at[at, :], out_h.at[at, :], so.at[16]),
-                pltpu.make_async_copy(gy.at[at, :], gx1_h.at[at, :], so.at[17])]
+        return [pltpu.make_async_copy(x.at[at, :], out_h.at[at, :], so.at[24]),
+                pltpu.make_async_copy(gy.at[at, :], gx1_h.at[at, :], so.at[25])]
 
     def live_rows(i):
         return jnp.concatenate(
@@ -483,9 +462,11 @@
         gyb = gy[at, :] * live_rows(i)
         gy[at, :] = gyb
         gm[at, :] = gyb.astype(BF16)
+        u_refs[0][...] = mm(a2, win[0]) + vecs[7:8, :]
         for j in range(4):
-            u = mm(a2, win[j]) + vecs[7 + j : 8 + j, :]
-            hf, slope = gelu_parts(u)
+            if j < 3:
+                u_refs[1 - j % 2][...] = mm(a2, win[j + 1]) + vecs[8 + j : 9 + j, :]
+            hf, slope = gelu_parts(u_refs[j % 2][...])
             ht[D * j : D * j + D, at] = hf.T.astype(BF16)
             h[at, D * j : D * j + D] = hf.astype(BF16)
             gu[at, D * j : D * j + D] = slope.astype(BF16)
@@ -497,17 +478,23 @@
         if pending is not None:
             pending.wait()
 
-        @pl.loop(0, FF // 384)
+        @pl.loop(0, FF // D)
         def _(r):
-            part = mm(ht[rows_at(r, 384), :], gm[:, DT * t : DT * t + DT]).astype(BF16)
-            stage_d[r // 2, pl.ds(2 * (r % 2), 2)] = part.reshape(2, 192, DT)
+            part = mm(ht[rows_at(r, D), :], gm[:, DT * t : DT * t + DT]).astype(BF16)
+            stage_d[r] = part.reshape(4, 192, DT)
 
         plan.run("gd", t)
-        pending = pltpu.make_async_copy(stage_d, gdown_h.at[t], so.at[18])
+        pending = pltpu.make_async_copy(stage_d, gdown_h.at[t], so.at[26])
         pending.start()
     pending.wait()
     plan.run("wd", 0)
-    cwd = [mv.start(part, wdown.at[j]) for j, part in enumerate(down_parts)]
+    if linked:
+        cwd = [mv.start(wdown_h, wdown.at[:, peers.f])]
+        for n in range(1, 8):
+            f = (peers.f + n) % 8
+            cwd.append(mv.start(down_f.at[:, f], wdown.at[:, f]))
+    else:
+        cwd = [mv.start(wdown_h, wdown)]
     plan.run("wd", 1)
     for c in cwd:
         c.wait()
@@ -521,8 +508,8 @@
         acc = x[at, :] + vecs[11:12, :]
         ga2 = jnp.zeros((TB, D), F32)
         for j in range(4):
-            acc = acc + mm(h[at, D * j : D * j + D], wdown[j])
-            guf = mm_t(gmb, wdown[j]) * gu[at, D * j : D * j + D].astype(F32)
+            acc = acc + mm(h[at, D * j : D * j + D], wdown[j].reshape(D, D))
+            guf = mm_t(gmb, wdown[j].reshape(D, D)) * gu[at, D * j : D * j + D].astype(F32)
             gub = guf.astype(BF16)
             gu[at, D * j : D * j + D] = gub
             sums[4 + j] += fold8(gub.astype(F32))
@@ -556,13 +543,10 @@
         if j > 1:
             copies[j - 2].wait()
 
-        @pl.loop(0, 2)
-        def _(r):
-            part = mm(a2t[rows_at(r, 384), :], gu[:, D * j : D * j + D]).astype(BF16)
-            stage[j % 2, pl.ds(2 * r, 2)] = part.reshape(2, 4, 48, D)
-
+        part = mm(a2t[...], gu[:, D * j : D * j + D]).astype(BF16)
+        stage[j % 2] = part.reshape(4, 4, 48, D)
         plan.run("gi", j)
-        copies.append(pltpu.make_async_copy(stage.at[j % 2], gin_h.at[j], so.at[19 + j % 2]))
+        copies.append(pltpu.make_async_copy(stage.at[j % 2], gin_h.at[j], so.at[27 + j % 2]))
         copies[j].start()
     plan.run("end", 0)
     for c in copies[2:] + outs:
@@ -586,21 +570,21 @@
     out = [sds(TOK, F32), sds(TOK, F32)] + [sds(TOK, BF16)] * 3 + [
         sds((16, BLOCK), F32), sds((D // DT, 4, 4, 192, DT), BF16), sds((4, 4, 4, 48, D), BF16), sds((9, 8, D), F32)]
     out_specs = [ANY] * 5 + [VMEM, ANY, ANY, VMEM]
-    scratch = [vm(TOK, F32), vm(TOK, BF16), vm(TOK, F32), vm((D, D), BF16), vm((4, D, D), BF16), vm((4, D, D), BF16),
+    scratch = [vm(TOK, F32), vm(TOK, BF16), vm(TOK, F32), vm((D, D), BF16), vm((4, D, D), BF16), vm((4, 8, FF // 32, D), BF16),
                vm(TOK, BF16), vm(TOKT, BF16), vm((FF, BLOCK), BF16), vm((BLOCK, FF), BF16), vm((BLOCK, FF), BF16),
-               vm(TOK, BF16), vm(TOK, BF16), vm(TOK, BF16), vm((4, 4, 192, DT), BF16), vm((2, 4, 4, 48, D), BF16), pltpu.SemaphoreType.DMA((21,))]
+               vm(TOK, BF16), vm(TOK, BF16), vm(TOK, BF16), vm((4, 4, 192, DT), BF16), vm((2, 4, 4, 48, D), BF16), vm((TB, D), F32), vm((TB, D), F32), pltpu.SemaphoreType.DMA((29,))]
     extra = {}
     if linked:
-        out += [sds((FF // 32, D), F32), sds((4, FF // 4, D), BF16)]
+        out += [sds((FF // 32, 2 * DT), F32), sds((4, 8, FF // 32, D), BF16)]
         out_specs += [VMEM, ANY]
-        slots = 3 * SCATTER_SLOTS + GATHER_SLOTS
-        scratch += 3 * scatter_bufs(FF // 32, DT) + [pltpu.SemaphoreType.DMA((n,)) for n in (4, slots, slots)]
+        slots = 2 * SCATTER_SLOTS + GATHER_SLOTS
+        scratch += 2 * scatter_bufs(FF // 32, DT) + [pltpu.SemaphoreType.DMA((n,)) for n in (4, slots, slots)]
         extra = dict(collective_id=2, has_side_effects=True)
     return pl.pallas_call(
         functools.partial(kernel_b, linked),
         name="part_b",
         out_shape=out,
-        in_specs=[SMEM, ANY, ANY, ANY, VMEM, ANY, ANY, VMEM if linked else ANY],
+        in_specs=[SMEM, ANY, ANY, ANY, VMEM, ANY, ANY, ANY],
         out_specs=out_specs,
         scratch_shapes=scratch,
         compiler_params=pltpu.CompilerParams(vmem_limit_bytes=VMEM_LIMIT, **extra),
@@ -641,19 +625,19 @@
         gqkv[2, :, lanes] = gv_acc[...].astype(BF16)
 
 
-UNITS_C = "0123oabc"
-
-
-def kernel_c(linked, sid, x_h, a1t_h, q0_h, q1_h, k0_h, k1_h, v_h, kt_h, ot_h, lse, gx1_h, gb_h, go0_h, go1_h, dots, vecs, wq_h, wk_h, wv_h, *refs):
-    if linked:
-        (gin_h, sums_b), refs = refs[:2], refs[2:]
+UNITS_C = "0123oabcz"
+
+
+def kernel_c(linked, sid, x_h, a1t_h, q0_h, q1_h, k0_h, k1_h, v_h, kt_h, ot_h, lse, gx1_h, gb_h, go0_h, go1_h, dots, vecs, w0_h, w1_h, w2_h, *refs):
+    if linked:
+        (gin_h, sums_b, gdown_h, down_part), refs = refs[:4], refs[4:]
     (ig_h, tg, gqkv_h, gwo_h, sums), refs = refs[:5], refs[5:]
     if linked:
-        (gin_o, gout_o, gqkv_o, small_o), refs = refs[:4], refs[4:]
+        (gin_o, gout_o, gqkv_o, small_o, gdown_o), refs = refs[:5], refs[5:]
     (x, a1t, q0, q1, k0, k1, v, kt, ot, gx1, gb, go0, go1, w, gqkv, gk_acc, gv_acc, gw, gwo, tsum, p0, g0, p1, g1, sems), refs = refs[:25], refs[25:]
     plan = Schedule(SCHEDULE_C)
     if linked:
-        bufs, (value, small_b, local_sems, send, recv) = refs[:56], refs[56:]
+        bufs, (value, small_b, local_sems, send, recv) = refs[:63], refs[63:]
         peers = Peers()
         links = Links(peers, send, recv)
         peers.greet()
@@ -663,15 +647,18 @@
                 parts, keep = (gin_h, n), functools.partial(store_lanes, gin_o, ((0, D * n, D),))
             elif n == 4:
                 parts, keep = (gwo_h,), functools.partial(store_lanes, gout_o, ((0, 0, D),))
+            elif n == 8:
+                parts, keep = (gdown_h, 2), functools.partial(store_lanes, gdown_o, ((0, 2 * DT, DT),))
             else:
                 places = tuple((third * m, D * m + third * (n - 5), third) for m in range(3))
                 parts, keep = (gqkv_h, n - 5), functools.partial(store_lanes, gqkv_o, places)
             plan.units[name] = Scatter(n, links, parts, keep, bufs[7 * n : 7 * n + 7], local_sems.at[n])
         plan.run("pre", 0)
+        gdown_o[:, : 2 * DT] = down_part[...]
     mv = Mover(sems)
     early = [mv.start(s, d) for s, d in ((ot_h, ot), (gb_h, gb), (q0_h, q0), (q1_h, q1), (k0_h, k0), (k1_h, k1), (v_h, v), (kt_h, kt), (go0_h, go0), (go1_h, go1))]
     late = [mv.start(a1t_h, a1t), mv.start(x_h, x), mv.start(gx1_h, gx1)]
-    late += [mv.start(part, w.at[j]) for j, part in enumerate((wq_h, wk_h, wv_h))]
+    late += [mv.start(part.at[:, pl.ds(256 * j, 256)], w.at[j, :, pl.ds(256 * n, 256)]) for n, part in enumerate((w0_h, w1_h, w2_h)) for j in range(3)]
     for c in early[:2]:
         c.wait()
     sums[...] = jnp.zeros_like(sums)
@@ -700,12 +687,12 @@
 
     @pl.loop(0, 3)
     def _(chunk):
-        paired_steps(steps * chunk, steps, slots, ahead, apply, step_hooks)
+        paired_steps(steps * chunk, steps, STEPS, slots, ahead, apply, step_hooks)
         for j in range(3):
             for r in range(2):
                 part = mm(a1t[384 * r : 384 * r + 384, :], gqkv[j, :, rows_at(chunk, 256)]).astype(BF16)
                 gw[chunk, 2 * r : 2 * r + 2, :, :, 256 * j : 256 * j + 256] = part.reshape(2, 4, 48, 256)
-        copy = pltpu.make_async_copy(gw.at[chunk], gqkv_h.at[chunk], sems.at[23])
+        copy = pltpu.make_async_copy(gw.at[chunk], gqkv_h.at[chunk], sems.at[31])
         copy.start()
         run_hooks(chunk, chunk_hooks)
         copy.wait()
@@ -755,10 +742,13 @@
         small.take(2)
         small.spread()
         row, col = small_places(peers.dev)
-        select = small_select(col)
+        select = small_select(col).astype(BF16)
         plan.run("end", 0, slice(-1, None))
-        picked = lax.dot_general(small.total(), select, (((1,), (0,)), ((), ())),
-                                 precision=lax.Precision.HIGHEST, preferred_element_type=F32)
+        left, picked = small.total(), 0.0
+        for _ in range(3):
+            part = left.astype(BF16)
+            picked = picked + mm(part, select)
+            left = left - part.astype(F32)
         at_row = lax.broadcasted_iota(jnp.int32, (16, SMALL_LEN), 0) == row
         small_o[...] = jnp.sum(jnp.where(at_row, picked, 0.0), axis=0, keepdims=True)
         links.finish()
@@ -771,15 +761,15 @@
     out_specs = [ANY, VMEM, ANY, ANY, VMEM]
     scratch = [vm(TOK, F32), vm(TOKT, BF16)] + [vm(TOK, BF16)] * 5 + [vm(TOKT, BF16)] * 2 + [vm(TOK, F32)] + [vm(TOK, BF16)] * 3
     scratch += [vm((3, D, D), BF16), vm((3, BLOCK, D), BF16), vm((BLOCK, 128), F32), vm((BLOCK, 128), F32), vm((3, 4, 4, 48, D), BF16), vm((4, 4, 48, D), BF16),
-                vm((GROUPS, D), F32)] + 4 * [vm((2, BLOCK, QB), BF16)] + [pltpu.SemaphoreType.DMA((24,))]
+                vm((GROUPS, D), F32)] + 4 * [vm((2, BLOCK, QB), BF16)] + [pltpu.SemaphoreType.DMA((32,))]
     extra = {}
     if linked:
-        in_specs += [ANY, VMEM]
-        out += [sds((D // 32, n * D), F32) for n in (4, 1, 3)] + [sds((1, SMALL_LEN), F32)]
-        out_specs += [VMEM] * 4
+        in_specs += [ANY, VMEM, ANY, VMEM]
+        out += [sds((D // 32, n * D), F32) for n in (4, 1, 3)] + [sds((1, SMALL_LEN), F32), sds((FF // 32, D), F32)]
+        out_specs += [VMEM] * 5
         units = len(UNITS_C)
         slots = SCATTER_SLOTS * units + 6
-        scratch += units * scatter_bufs(D // 32, D) + [vm((4, 16, D), F32), vm((6, 16, D), F32)]
+        scratch += (units - 1) * scatter_bufs(D // 32, D) + scatter_bufs(FF // 32, DT) + [vm((4, 16, D), F32), vm((6, 16, D), F32)]
         scratch += [pltpu.SemaphoreType.DMA((n,)) for n in (units, slots, slots)]
         extra = dict(collective_id=3, has_side_effects=True)
     return pl.pallas_call(
@@ -868,19 +858,23 @@
 class Gather:
     def __init__(self, name, links, own, rows, full, sem):
         self.name, self.links, self.own, self.rows, self.full, self.sem = name, links, own, rows, full, sem
-        p = links.peers
-        self.at = {n: pl.multiple_of(f * self.rows, 8) for n, f in (("f", p.f), ("x", p.fx), ("y", p.fy), ("d", p.fd))}
-        self.across = {n: pl.multiple_of((f + 1 - 2 * p.c) * self.rows, 8)
+        p, self.deep = links.peers, len(full.shape) == 4
+        place = (lambda f: f) if self.deep else (lambda f: pl.multiple_of(f * self.rows, 8))
+        self.at = {n: place(f) for n, f in (("f", p.f), ("x", p.fx), ("y", p.fy), ("d", p.fd))}
+        self.across = {n: place(f + 1 - 2 * p.c)
                        for n, f in (("f", p.f), ("x", p.fx), ("y", p.fy), ("d", p.fd))}
 
     def key(self, *k):
         return (self.name,) + k
 
     def piece(self, d, n):
-        return View(self.full, self.links.peers.up((4 - d) % 4), pl.ds(self.at[n], self.rows))
+        return View(self.full, self.links.peers.up((4 - d) % 4), self.window(self.at[n]))
 
     def column(self, at):
-        return View(self.full, slice(None), pl.ds(at, self.rows))
+        return View(self.full, slice(None), self.window(at))
+
+    def window(self, at):
+        return at if self.deep else pl.ds(at, self.rows)
 
     def begin(self):
         here = self.piece(0, "f")
@@ -924,6 +918,30 @@
                 links.arrived(self.key("p", n), self.column(self.across[n]))
 
 
+class Line(Gather):
+    def piece(self, d, n):
+        return View(self.full, self.links.peers.up((4 - d) % 4))
+
+    def do(self, action):
+        for d in (1, 2, 3):
+            self.links.arrived(self.key("z", d), self.piece(d, "f"))
+        self.local_copy().wait()
+
+
+class Plane(Gather):
+    def mine(self, d):
+        return View(self.own.ref, self.links.peers.up((4 - d) % 4))
+
+    def do(self, action):
+        if action[0] != "F":
+            return Gather.do(self, action)
+        d = int(action[1:])
+        for name in ("x", "y"):
+            self.links.start(self.key(name, d), self.mine(d), self.piece(d, "f"), name)
+        if d == 2:
+            self.links.start(self.key("p", "f"), self.own, self.column(self.at["f"]), "p")
+
+
 SCATTER_SLOTS = 10
 
 
@@ -1044,7 +1062,9 @@
 
 def kernel_prep(small, wqkv, wout, win, wdown, small_o, qkv_o, out_o, in_o, down_o):
     small_o[...] = jnp.broadcast_to(small[...], (8, SMALL_LEN)).astype(BF16)
-    qkv_o[...] = wqkv[...].astype(BF16)
+    for c in range(3):
+        for j in range(3):
+            qkv_o[:, D * c + 256 * j : D * c + 256 * j + 256] = wqkv[:, D * j + 256 * c : D * j + 256 * c + 256].astype(BF16)
     out_o[...] = wout[...].astype(BF16)
     in_o[...] = win[...].astype(BF16)
     down_o[...] = wdown[...].astype(BF16)
@@ -1064,15 +1084,15 @@
     copy.wait()
     rows = staged[...].reshape(256, SMALL_LEN).astype(F32).T
     r = lax.broadcasted_iota(jnp.int32, (256, D), 0)
-    lane = lax.broadcasted_iota(jnp.int32, (256, D), 1)
+    lane = lax.broadcasted_iota(jnp.int32, (1, D), 1)
     vecs[...] = jnp.zeros_like(vecs)
     for n in (24, 48, 96):
         part = [(start, base) for start, size, base in SMALL if size == n]
         values = rows[part[0][0] : part[-1][0] + n, :].astype(BF16)
-        own = lax.broadcasted_iota(jnp.int32, (n, D), 0) == lax.rem(lax.broadcasted_iota(jnp.int32, (n, D), 1), n)
+        own = lax.broadcasted_iota(jnp.int32, (n, D), 0) == lax.rem(lane, n)
+        first = (lane // n) * 8
         for line in range(n // 24):
-            source = ((lane + line * D) // n) * 8
-            spread = mm(values, (r == source).astype(BF16))
+            spread = mm(values, (r == first + 8 * line * (D // n)).astype(BF16))
             for m, (_, base) in enumerate(part):
                 picked = jnp.where(own, spread[n * m : n * m + n, :], 0.0)
                 vecs[base + line : base + line + 1, :] = jnp.sum(picked, axis=0, keepdims=True)
@@ -1124,18 +1144,17 @@
         ordered = tuple(small[n] for n in SMALL_ORDER)
         row = jnp.concatenate(ordered + (jnp.zeros((SMALL_LEN - 288,), F32),)).reshape(1, SMALL_LEN)
         own = call_prep(row, weights)
-        vecs, made, wq, (wout, win) = call_a_links(sid, hidden_in, time_embed, own[:4])
-        wdown = own[4]
+        vecs, made, wq, (wout, win), wdown = call_a_links(sid, hidden_in, time_embed, own)
     else:
         vecs, (wqkv, wout, win, wdown) = gather_plain(small, weights)
-        wq = [wqkv[:, D * n : D * n + D] for n in range(3)]
+        wq = list(wqkv.reshape(D, 3, 3, 256).transpose(2, 0, 1, 3).reshape(3, D, D))
+        wdown = wdown.reshape(4, 8, FF // 32, D)
         made = call_a(sid, hidden_in, time_embed, vecs, wq)
     x, a1t, q0, q1, k0, k1, v, kt, o, ot, lse = made
     block_out, gx1, gb, go0, go1, dots, gdown, gin, sums_b, *more = call_b(own_links, sid, x, o, grad_out, vecs, wout, win, wdown)
     args_c = (sid, x, a1t, q0, q1, k0, k1, v, kt, ot, lse, gx1, gb, go0, go1, dots, vecs, *wq)
     if own_links:
-        input_grad, time_grad, _, _, _, gin, gout, gqkv, mine = call_c(True, *args_c, gin, sums_b)
-        gdown = more[0]
+        input_grad, time_grad, _, _, _, gin, gout, gqkv, mine, gdown = call_c(True, *args_c, gin, sums_b, gdown, more[0])
         parts = split_small(mine.reshape(-1), ordered)
         parts = [parts[SMALL_ORDER.index(n)] for n in range(8)]
     else:

time: 250 us -> 245 us (0.980)
  Pallas kernels: 233 us -> 229 us
    pallas_call x1, Pallas kernels: 67.2 us -> 62.8 us  [call_a_links(): pl.pallas_call(functools.partial(kernel_a, True), name='part_a', out_shap...]
where the time goes in v5:
time: 245 us
  Pallas kernels  229 us (93%)
  local copies, waits for them, and re-layouts  15.6 us (6%)
    pallas_call x1, Pallas kernels, call_c(): pl.pallas_call(functools.partial(kernel_c, linked), name='part_c', out_sh...  85.1 us
    pallas_call x1, Pallas kernels, call_b(): pl.pallas_call(functools.partial(kernel_b, linked), name='part_b', out_sh...  78.7 us
    pallas_call x1, Pallas kernels, call_a_links(): pl.pallas_call(functools.partial(kernel_a, True), name='part_a', out_shap...  62.8 us
    unnamed x19, local copies, waits for them, and re-layouts  8.96 us

profile of v5, /device:TPU:0, one launch (start us, length us, event | category | flops | bytes accessed | tf_op | source)
XLA Modules:
  0.0 244.9 jit_solution(10616260791735851255)
XLA Ops:
  0.7 0.9 concatenate.3
  1.5 0.6 reshape.61.small
  2.1 0.8 reshape.60
  2.8 0.6 slice_reduce_fusion.sid
  3.5 2.0 prep.1
  5.5 62.8 %part_a.1 = (f32[16,768]{1,0:T(8,128)}, f32[1024,768]{1,0:T(8,128)}, bf16[768,1024]{1,0:T(8,128)(2,1)}, bf16[1024,768]{1,0:T(8,128)(2,1)}, bf16[1024,768]{1,0:T(...) custom-call(s32[16]{0:T(128)} %slice_reduce_fusion.sid, ...), custom_call_target="tpu_custom_call" | custom-call | tf_op jit(solution)/shard_map/part_a/pallas_call | solution.py:401
  68.3 78.7 %part_b.1 = (f32[1024,768]{1,0:T(8,128)}, f32[1024,768]{1,0:T(8,128)}, bf16[1024,768]{1,0:T(8,128)(2,1)}, bf16[1024,768]{1,0:T(8,128)(2,1)}, bf16[1024,768]{1,0:...) custom-call(s32[16]{0:T(128)} %slice_reduce_fusion.sid, ...), custom_call_target="tpu_custom_call" | custom-call | tf_op jit(solution)/shard_map/part_b/pallas_call | solution.py:583
  146.9 85.1 %part_c.1 = (f32[1024,768]{1,0:T(8,128)}, f32[16,768]{1,0:T(8,128)}, bf16[3,4,4,48,768]{4,3,2,1,0:T(8,128)(2,1)}, bf16[4,4,48,768]{3,2,1,0:T(8,128)(2,1)}, f32[4...) custom-call(s32[16]{0:T(128)} %slice_reduce_fusion.sid, ...), custom_call_target="tpu_custom_call" | custom-call | tf_op jit(solution)/shard_map/part_c/pallas_call | solution.py:775
  232.0 1.2 slice_bitcast_fusion.5
  233.2 1.2 slice_bitcast_fusion.1
  234.4 1.4 slice_bitcast_fusion
  235.9 3.9 %copy.38 = f32[1024,768]{1,0:T(8,128)} copy(f32[1024,768]{1,0:T(8,128)} %get-tuple-element.116) | data formatting | bytes 6291456
  239.8 0.0 copy-done
  239.8 0.0 copy-start.2
  239.8 0.0 copy-start.1
  239.8 1.7 copy.39
  241.5 0.0 copy-done.5
  241.5 0.6 copy.40
  242.1 0.0 copy-done.3
  242.1 0.7 copy.41
  242.8 0.6 copy.42
  243.4 0.0 copy-done.2
  243.4 0.7 copy.43
  244.1 0.7 copy.44
  (7 shorter events, 0.0 us)
Async XLA Ops:
  235.9 3.9 %copy-start = (f32[1024,768]{1,0:T(8,128)S(1)}, f32[1024,768]{1,0:T(8,128)}, u32[]{:S(2)}) copy-start(f32[1024,768]{1,0:T(8,128)} %get-tuple-element.117) | copy-start | bytes 9437188
  239.8 1.7 copy-start.5
  239.8 2.3 copy-start.3
  239.8 3.0 %copy-start.4 = (f32[24,768]{1,0:T(8,128)S(1)}, f32[24,768]{1,0:T(8,128)}, u32[]{:S(2)}) copy-start(f32[24,768]{1,0:T(8,128)} %get-tuple-element.123) | copy-start | bytes 221188
  239.8 3.6 %copy-start.2 = (f32[24,3072]{1,0:T(8,128)S(1)}, f32[24,3072]{1,0:T(8,128)}, u32[]{:S(2)}) copy-start(f32[24,3072]{1,0:T(8,128)} %get-tuple-element.127) | copy-start | bytes 884740
  239.8 4.3 %copy-start.1 = (f32[96,768]{1,0:T(8,128)S(1)}, f32[96,768]{1,0:T(8,128)}, u32[]{:S(2)}) copy-start(f32[96,768]{1,0:T(8,128)} %get-tuple-element.129) | copy-start | bytes 884740

commit v6 on v5

--- a/solution.py
+++ b/solution.py
@@ -657,8 +657,6 @@
         gdown_o[:, : 2 * DT] = down_part[...]
     mv = Mover(sems)
     early = [mv.start(s, d) for s, d in ((ot_h, ot), (gb_h, gb), (q0_h, q0), (q1_h, q1), (k0_h, k0), (k1_h, k1), (v_h, v), (kt_h, kt), (go0_h, go0), (go1_h, go1))]
-    late = [mv.start(a1t_h, a1t), mv.start(x_h, x), mv.start(gx1_h, gx1)]
-    late += [mv.start(part.at[:, pl.ds(256 * j, 256)], w.at[j, :, pl.ds(256 * n, 256)]) for n, part in enumerate((w0_h, w1_h, w2_h)) for j in range(3)]
     for c in early[:2]:
         c.wait()
     sums[...] = jnp.zeros_like(sums)
@@ -670,6 +668,8 @@
     gwo_copy = mv.start(gwo, gwo_h)
     for c in early[2:]:
         c.wait()
+    late = [mv.start(a1t_h, a1t), mv.start(x_h, x), mv.start(gx1_h, gx1)]
+    late += [mv.start(part.at[:, pl.ds(256 * j, 256)], w.at[j, :, pl.ds(256 * n, 256)]) for n, part in enumerate((w0_h, w1_h, w2_h)) for j in range(3)]
     gwo_copy.wait()
     plan.run("gwo", 0)
     steps = 2 * (BLOCK // QB)
@@ -682,12 +682,12 @@
         attention_back_apply(step, *slot, q0, q1, kt, go0, go1, gk_acc, gv_acc, gqkv)
 
     ahead(0, slots[0])
-    late[0].wait()
     step_hooks, chunk_hooks = plan.hooks("att"), plan.hooks("gw", 0, 3)
 
     @pl.loop(0, 3)
     def _(chunk):
         paired_steps(steps * chunk, steps, STEPS, slots, ahead, apply, step_hooks)
+        pl.when(chunk == 0)(late[0].wait)
         for j in range(3):
             for r in range(2):
                 part = mm(a1t[384 * r : 384 * r + 384, :], gqkv[j, :, rows_at(chunk, 256)]).astype(BF16)

time: 245 us -> 246 us (level)
  no operation moved by 1% of the time
where the time goes in v6:
time: 246 us; the launch traced here: 245 us
  Pallas kernels  229 us (93%)
  local copies, waits for them, and re-layouts  15.6 us (6%)
    pallas_call x1, Pallas kernels, call_c(): pl.pallas_call(functools.partial(kernel_c, linked), name='part_c', out_sh...  85.3 us
    pallas_call x1, Pallas kernels, call_b(): pl.pallas_call(functools.partial(kernel_b, linked), name='part_b', out_sh...  78.7 us
    pallas_call x1, Pallas kernels, call_a_links(): pl.pallas_call(functools.partial(kernel_a, True), name='part_a', out_shap...  62.8 us
    unnamed x19, local copies, waits for them, and re-layouts  8.96 us

profile of v6, /device:TPU:0, one launch (start us, length us, event | category | flops | bytes accessed | tf_op | source)
XLA Modules:
  0.0 245.0 jit_solution(16167691397208793700)
XLA Ops:
  0.7 0.9 concatenate.3
  1.5 0.6 reshape.61.small
  2.1 0.8 reshape.60
  2.8 0.6 slice_reduce_fusion.sid
  3.5 2.0 prep.1
  5.5 62.8 %part_a.1 = (f32[16,768]{1,0:T(8,128)}, f32[1024,768]{1,0:T(8,128)}, bf16[768,1024]{1,0:T(8,128)(2,1)}, bf16[1024,768]{1,0:T(8,128)(2,1)}, bf16[1024,768]{1,0:T(...) custom-call(s32[16]{0:T(128)} %slice_reduce_fusion.sid, ...), custom_call_target="tpu_custom_call" | custom-call | tf_op jit(solution)/shard_map/part_a/pallas_call | solution.py:401
  68.3 78.7 %part_b.1 = (f32[1024,768]{1,0:T(8,128)}, f32[1024,768]{1,0:T(8,128)}, bf16[1024,768]{1,0:T(8,128)(2,1)}, bf16[1024,768]{1,0:T(8,128)(2,1)}, bf16[1024,768]{1,0:...) custom-call(s32[16]{0:T(128)} %slice_reduce_fusion.sid, ...), custom_call_target="tpu_custom_call" | custom-call | tf_op jit(solution)/shard_map/part_b/pallas_call | solution.py:583
  146.9 85.3 %part_c.1 = (f32[1024,768]{1,0:T(8,128)}, f32[16,768]{1,0:T(8,128)}, bf16[3,4,4,48,768]{4,3,2,1,0:T(8,128)(2,1)}, bf16[4,4,48,768]{3,2,1,0:T(8,128)(2,1)}, f32[4...) custom-call(s32[16]{0:T(128)} %slice_reduce_fusion.sid, ...), custom_call_target="tpu_custom_call" | custom-call | tf_op jit(solution)/shard_map/part_c/pallas_call | solution.py:775
  232.2 1.2 slice_bitcast_fusion.5
  233.4 1.2 slice_bitcast_fusion.1
  234.6 1.4 slice_bitcast_fusion
  236.0 3.9 %copy.38 = f32[1024,768]{1,0:T(8,128)} copy(f32[1024,768]{1,0:T(8,128)} %get-tuple-element.116) | data formatting | bytes 6291456
  240.0 0.0 copy-done
  240.0 0.0 copy-start.2
  240.0 0.0 copy-start.1
  240.0 1.7 copy.39
  241.7 0.0 copy-done.5
  241.7 0.6 copy.40
  242.3 0.0 copy-done.3
  242.3 0.7 copy.41
  243.0 0.0 copy-done.4
  243.0 0.6 copy.42
  243.6 0.7 copy.43
  244.3 0.7 copy.44
  (7 shorter events, 0.0 us)
Async XLA Ops:
  236.0 3.9 %copy-start = (f32[1024,768]{1,0:T(8,128)S(1)}, f32[1024,768]{1,0:T(8,128)}, u32[]{:S(2)}) copy-start(f32[1024,768]{1,0:T(8,128)} %get-tuple-element.117) | copy-start | bytes 9437188
  240.0 1.7 copy-start.5
  240.0 2.3 copy-start.3
  240.0 3.0 %copy-start.4 = (f32[24,768]{1,0:T(8,128)S(1)}, f32[24,768]{1,0:T(8,128)}, u32[]{:S(2)}) copy-start(f32[24,768]{1,0:T(8,128)} %get-tuple-element.123) | copy-start | bytes 221188
  240.0 3.6 %copy-start.2 = (f32[24,3072]{1,0:T(8,128)S(1)}, f32[24,3072]{1,0:T(8,128)}, u32[]{:S(2)}) copy-start(f32[24,3072]{1,0:T(8,128)} %get-tuple-element.127) | copy-start | bytes 884740
  240.0 4.3 %copy-start.1 = (f32[96,768]{1,0:T(8,128)S(1)}, f32[96,768]{1,0:T(8,128)}, u32[]{:S(2)}) copy-start(f32[96,768]{1,0:T(8,128)} %get-tuple-element.129) | copy-start | bytes 884740
